TPU v7x, 32 devices: a whole 2x2x4 slice. The times are simulated.
32 devices in a mesh: groups: 2 (over y), space: 4 (over z), tm: 4 (over x, core).
Axes of the slice: x: 2, y: 2, z: 4, core: 2. Of those that a mesh axis runs over, the one named last changes fastest.
Arguments:
- state: float32 [8, 4, 256, 256], P(('groups', 'tm'), 'space'), parts along dimension 0, may hold values from 0 to 1
- classes: int32 [8, 256, 256], P(('groups', 'space')), parts along dimension 0, may hold values from 0 to 3
- perm_table: float32 [4], replicated, may hold values from 0.2 to 2
- rate_table: float32 [4], replicated, may hold values from 0.02 to 1
Outputs:
- new_state: float32 [8, 4, 256, 256], P(('groups', 'tm'), 'space'), parts along dimension 0
There are 2 independent parts, one for each index of `groups`. A program takes and returns all parts, laid end to end along the dimension named above; an argument that names none is the same for every part. Nothing has to cross between parts.
All inputs are finite; a program needn't handle non-finite values.
Results may differ from a plain program's by a relative error of at most 0.0001.
Values sent between devices are 32-bit elements; how exact they have to be, the bound alone decides.
No kernel may reach another device: no remote copies, remote signals or barrier semaphores. Data moves between devices by JAX's collectives and lax.ppermute only.
A program may use at most 64 MiB of HBM per device.

v0:
```python
import jax
import jax.numpy as jnp
from jax import lax
from jax.sharding import PartitionSpec as P

ITERS = 3
FINE = 2


DIFF = 2.0
ADV = 0.25


def with_halo(array, sides, width):
    for axis, dim in sides:
        devices, length = (lax.axis_size(axis), array.shape[dim])
        up = [(i, (i + 1) % devices) for i in range(devices)]
        down = [(j, i) for i, j in up]
        last = lax.slice_in_dim(array, length - width, length, axis=dim)
        first = lax.slice_in_dim(array, 0, width, axis=dim)
        before = lax.ppermute(last, axis, up)
        after = lax.ppermute(first, axis, down)
        array = jnp.concatenate([before, array, after], axis=dim)
    return array


def passed_along(array, axis, by):
    devices = lax.axis_size(axis)
    pairs = [(i, i + by) for i in range(devices) if 0 <= i + by < devices]
    return lax.ppermute(array, axis, pairs)


def lookup(table, classes):
    values = jnp.zeros(classes.shape, jnp.float32)
    for entry in range(table.shape[0]):
        values = jnp.where(classes == entry, table[entry], values)
    return values


def restrict(field):
    cx, ny, nz = field.shape
    return field.reshape(cx, ny // 2, 2, nz // 2, 2).mean(axis=(2, 4))


def prolong(coarse):
    return jnp.repeat(jnp.repeat(coarse, 2, axis=1), 2, axis=2)


def vertical(field):
    zero_plane = jnp.zeros(field.shape[:2] + (1,), jnp.float32)
    upper = jnp.concatenate([field[:, :, 1:], zero_plane], axis=2)
    lower = jnp.concatenate([zero_plane, field[:, :, :-1]], axis=2)
    return (upper, lower)


def operate(field):
    padded = with_halo(field, (("space", 0),), 1)
    upper, lower = vertical(field)
    beside = padded[2:] + padded[:-2]
    beside = beside + jnp.roll(field, -1, 1) + jnp.roll(field, 1, 1)
    beside = beside + upper + lower
    return (1.0 + 6.0 * DIFF) * field - DIFF * beside


def squares(residual):
    return lax.psum(jnp.sum(residual * residual), "space")


def fine_step(field, perm):
    upper, lower = vertical(field)
    rhs = field - ADV * perm * field * (upper - lower)
    solution = field
    residual = rhs - operate(solution)
    direction = residual
    norm_now = squares(residual)
    for step in range(ITERS):
        image = operate(direction)
        alpha = norm_now / lax.psum(jnp.sum(direction * image), "space")
        solution = solution + alpha * direction
        residual = residual - alpha * image
        norm_next = squares(residual)
        direction = residual + norm_next / norm_now * direction
        norm_now = norm_next
    return solution


def body(state, classes, perm_table, rate_table):
    start = state[0]
    perm = lookup(perm_table, classes)
    coarse_ratio = 1.0 / (1.0 + restrict(lookup(rate_table, classes)))
    field = start
    for step in range(FINE):
        field = fine_step(field, perm)
    coarse_start = restrict(start)
    jump = field - prolong(coarse_ratio * coarse_start)
    jump_coarse = restrict(jump)
    first = lax.axis_index("tm") == 0
    factor = jnp.where(first, 0.0, coarse_ratio)
    offset = jnp.where(first, coarse_ratio * coarse_start + jump_coarse, jump_coarse)
    before = passed_along(jump, "tm", 1)
    before_coarse = restrict(before)

    def relay_turn(turn, carry):
        outgoing, received = carry
        received = passed_along(outgoing, "tm", 1)
        return (factor * received + offset, received)

    outgoing, received = lax.fori_loop(
        0, lax.axis_size("tm") - 1, relay_turn, (offset, jnp.zeros_like(offset))
    )
    updated = jnp.where(first, start, before + prolong(received - before_coarse))
    return updated[None]


def solution(mesh):
    placed = (
        P(("groups", "tm"), "space", None, None),
        P(("groups", "space"), None, None),
        P(),
        P(),
    )
    return jax.shard_map(
        body,
        mesh=mesh,
        in_specs=placed,
        out_specs=P(("groups", "tm"), "space", None, None),
        check_vma=False,
    )
```

profile of v0, /device:TPU:11, one launch (start us, length us, event | category | flops | bytes accessed | tf_op | source)
XLA Modules:
  0.0 334.3 jit_solution(15333414936486038622)
XLA Ops:
  0.0 1.1 copy.16
  1.4 1.3 collective-permute-start.2
  2.9 1.5 fusion.76
  4.4 1.5 fusion.75
  5.8 18.9 %reshape_squeeze.3 = f32[128,2,128,2]{3,2,1,0:T(8,128)} reshape(f32[1,1,256,256]{3,2,1,0:T(8,128)} %param.6) | data formatting | bytes 524288 | tf_op jit(solution)/shard_map/reshape;squeeze | solution.py:42
  24.8 8.0 %reduce_sum.157 = f32[128,128]{1,0:T(8,128)S(1)} reduce(f32[128,2,128,2]{3,2,1,0:T(8,128)} %reshape_squeeze.3, f32[]{:T(128)} %constant.6.clone.1), dimensions={1,3}, to_apply=%region_25.26 | reduce | flops 49152 | bytes 327684 | tf_op jit(solution)/shard_map/reduce_sum | solution.py:42
  32.9 2.9 fusion.5
  35.9 2.1 collective-permute-start.3
  38.0 2.6 select_select_fusion
  40.8 18.1 %reshape.122 = f32[128,2,128,2]{3,2,1,0:T(8,128)} reshape(f32[1,256,256]{2,1,0:T(8,128)S(1)} %copy.21) | data formatting | bytes 524288 | tf_op jit(solution)/shard_map/reshape | solution.py:42
  59.1 0.9 multiply_reduce_fusion.8
  59.9 10.5 %all-reduce.17 = (f32[]{:T(128)}, f32[]{:T(128)}) all-reduce(f32[]{:T(128)} %get-tuple-element.35, f32[]{:T(128)} %get-tuple-element.34), channel_id=1, replica_groups=mesh['groups'=2,'space'=4,'tm'=4] {'space'}, use_global_device_ids=true, to_apply=%region_1.2 | all-reduce | flops 2 | bytes 16 | tf_op jit(solution)/shard_map/psum | solution.py:66
  71.6 0.7 multiply_reduce_fusion.7
  72.4 10.5 %psum.86 = f32[]{:T(128)} all-reduce(f32[]{:T(128)} %get-tuple-element.57), channel_id=1, replica_groups=mesh['groups'=2,'space'=4,'tm'=4] {'space'}, use_global_device_ids=true, to_apply=%region_5.6 | all-reduce | flops 1 | bytes 8 | tf_op jit(solution)/shard_map/psum | solution.py:66
  84.3 1.5 collective-permute-start.6
  86.0 6.3 %collective-permute-done.5 = f32[1,256,256]{1,2,0:T(8,128)S(1)} collective-permute-done((f32[1,256,256]{1,2,0:T(8,128)S(1)}, f32[1,256,256]{1,2,0:T(8,128)S(1)}, u32[]{:S(2)}, u32[]{:S(2)}) %collective-permute-start.5) | collective-permute-done | bytes 262176 | tf_op jit(solution)/shard_map/ppermute | solution.py:22
  92.4 0.8 multiply_reduce_fusion.6
  93.2 8.1 %psum.87 = f32[]{:T(128)} all-reduce(f32[]{:T(128)} %get-tuple-element.55), channel_id=1, replica_groups=mesh['groups'=2,'space'=4,'tm'=4] {'space'}, use_global_device_ids=true, to_apply=%region_7.8 | all-reduce | flops 1 | bytes 8 | tf_op jit(solution)/shard_map/psum | solution.py:78
  102.7 0.7 multiply_reduce_fusion.5
  103.4 8.0 %reduce_sum.156 = f32[128,128]{1,0:T(8,128)S(1)} reduce(f32[128,2,128,2]{3,2,1,0:T(8,128)} %reshape.122, f32[]{:T(128)} %constant.6.clone.1), dimensions={1,3}, to_apply=%region_24.25 | reduce | flops 49152 | bytes 327684 | tf_op jit(solution)/shard_map/reduce_sum | solution.py:42
  111.4 8.8 %psum.88 = f32[]{:T(128)} all-reduce(f32[]{:T(128)} %multiply_reduce_fusion.5), channel_id=1, replica_groups=mesh['groups'=2,'space'=4,'tm'=4] {'space'}, use_global_device_ids=true, to_apply=%region_9.10 | all-reduce | flops 1 | bytes 8 | tf_op jit(solution)/shard_map/psum | solution.py:66
  121.7 1.4 collective-permute-start.8
  123.3 6.6 %collective-permute-done.7 = f32[1,256,256]{1,2,0:T(8,128)S(1)} collective-permute-done((f32[1,256,256]{1,2,0:T(8,128)S(1)}, f32[1,256,256]{1,2,0:T(8,128)S(1)}, u32[]{:S(2)}, u32[]{:S(2)}) %collective-permute-start.7) | collective-permute-done | bytes 262176 | tf_op jit(solution)/shard_map/ppermute | solution.py:22
  129.8 0.8 fusion.22
  130.7 8.0 %psum.89 = f32[]{:T(128)} all-reduce(f32[]{:T(128)} %fusion.22), channel_id=1, replica_groups=mesh['groups'=2,'space'=4,'tm'=4] {'space'}, use_global_device_ids=true, to_apply=%region_11.12 | all-reduce | flops 1 | bytes 8 | tf_op jit(solution)/shard_map/psum | solution.py:78
  140.2 1.6 collective-permute-start.9
  141.9 6.7 %collective-permute-done.9 = f32[1,256,256]{1,2,0:T(8,128)S(1)} collective-permute-done((f32[1,256,256]{1,2,0:T(8,128)S(1)}, f32[1,256,256]{1,2,0:T(8,128)S(1)}, u32[]{:S(2)}, u32[]{:S(2)}) %collective-permute-start.9) | collective-permute-done | bytes 262176 | tf_op jit(solution)/shard_map/ppermute | solution.py:22
  148.8 2.9 fusion.28
  151.8 1.4 collective-permute-start.11
  153.5 3.5 %collective-permute-done.11 = f32[1,256,256]{1,2,0:T(8,128)S(1)} collective-permute-done((f32[1,256,256]{1,2,0:T(8,128)S(1)}, f32[1,256,256]{1,2,0:T(8,128)S(1)}, u32[]{:S(2)}, u32[]{:S(2)}) %collective-permute-start.11) | collective-permute-done | bytes 262176 | tf_op jit(solution)/shard_map/ppermute | solution.py:22
  157.0 6.8 %collective-permute-done.12 = f32[1,256,256]{1,2,0:T(8,128)S(1)} collective-permute-done((f32[1,256,256]{1,2,0:T(8,128)S(1)}, f32[1,256,256]{1,2,0:T(8,128)S(1)}, u32[]{:S(2)}, u32[]{:S(2)}) %collective-permute-start.12) | collective-permute-done | bytes 262176 | tf_op jit(solution)/shard_map/ppermute | solution.py:21
  163.8 0.9 multiply_reduce_fusion.3
  164.7 9.6 %all-reduce.16 = (f32[]{:T(128)}, f32[]{:T(128)}) all-reduce(f32[]{:T(128)} %get-tuple-element.33, f32[]{:T(128)} %get-tuple-element.32), channel_id=1, replica_groups=mesh['groups'=2,'space'=4,'tm'=4] {'space'}, use_global_device_ids=true, to_apply=%region_13.14 | all-reduce | flops 2 | bytes 16 | tf_op jit(solution)/shard_map/psum | solution.py:66
  175.6 0.7 multiply_reduce_fusion.2
  176.3 9.9 %psum.92 = f32[]{:T(128)} all-reduce(f32[]{:T(128)} %get-tuple-element.52), channel_id=1, replica_groups=mesh['groups'=2,'space'=4,'tm'=4] {'space'}, use_global_device_ids=true, to_apply=%region_17.18 | all-reduce | flops 1 | bytes 8 | tf_op jit(solution)/shard_map/psum | solution.py:66
  187.6 1.4 collective-permute-start.14
  189.2 6.4 %collective-permute-done.13 = f32[1,256,256]{1,2,0:T(8,128)S(1)} collective-permute-done((f32[1,256,256]{1,2,0:T(8,128)S(1)}, f32[1,256,256]{1,2,0:T(8,128)S(1)}, u32[]{:S(2)}, u32[]{:S(2)}) %collective-permute-start.13) | collective-permute-done | bytes 262176 | tf_op jit(solution)/shard_map/ppermute | solution.py:22
  195.7 0.9 multiply_reduce_fusion.1
  196.6 8.0 %psum.93 = f32[]{:T(128)} all-reduce(f32[]{:T(128)} %get-tuple-element.50), channel_id=1, replica_groups=mesh['groups'=2,'space'=4,'tm'=4] {'space'}, use_global_device_ids=true, to_apply=%region_19.20 | all-reduce | flops 1 | bytes 8 | tf_op jit(solution)/shard_map/psum | solution.py:78
  205.8 0.7 multiply_reduce_fusion
  206.7 9.1 %psum.94 = f32[]{:T(128)} all-reduce(f32[]{:T(128)} %multiply_reduce_fusion), channel_id=1, replica_groups=mesh['groups'=2,'space'=4,'tm'=4] {'space'}, use_global_device_ids=true, to_apply=%region_21.22 | all-reduce | flops 1 | bytes 8 | tf_op jit(solution)/shard_map/psum | solution.py:66
  217.3 0.7 collective-permute-start.15
  218.0 0.8 collective-permute-start.16
  219.0 3.7 %collective-permute-done.15 = f32[1,256,256]{1,2,0:T(8,128)S(1)} collective-permute-done((f32[1,256,256]{1,2,0:T(8,128)S(1)}, f32[1,256,256]{1,2,0:T(8,128)S(1)}, u32[]{:S(2)}, u32[]{:S(2)}) %collective-permute-start.15) | collective-permute-done | bytes 262176 | tf_op jit(solution)/shard_map/ppermute | solution.py:22
  222.6 3.0 collective-permute-done.16
  225.6 0.8 fusion.45
  226.7 8.5 %psum.95 = f32[]{:T(128)} all-reduce(f32[]{:T(128)} %fusion.45), channel_id=1, replica_groups=mesh['groups'=2,'space'=4,'tm'=4] {'space'}, use_global_device_ids=true, to_apply=%region_23.24 | all-reduce | flops 1 | bytes 8 | tf_op jit(solution)/shard_map/psum | solution.py:78
  236.7 1.3 collective-permute-start.17
  238.1 18.1 %reshape.123 = f32[128,2,128,2]{3,2,1,0:T(8,128)} reshape(f32[1,256,256]{2,1,0:T(8,128)S(1)} %copy.23) | data formatting | bytes 524288 | tf_op jit(solution)/shard_map/reshape | solution.py:42
  256.2 8.0 %reduce_sum.158 = f32[128,128]{1,0:T(8,128)S(1)} reduce(f32[128,2,128,2]{3,2,1,0:T(8,128)} %reshape.123, f32[]{:T(128)} %constant.6.clone.1), dimensions={1,3}, to_apply=%region_26.27 | reduce | flops 49152 | bytes 327684 | tf_op jit(solution)/shard_map/reduce_sum | solution.py:42
  264.3 0.6 collective-permute-done.17
  265.0 18.1 %reshape.124 = f32[128,2,128,2]{3,2,1,0:T(8,128)} reshape(f32[1,256,256]{2,1,0:T(8,128)S(1)} %copy.24) | data formatting | bytes 524288 | tf_op jit(solution)/shard_map/reshape | solution.py:42
  283.1 8.0 %reduce_sum.159 = f32[128,128]{1,0:T(8,128)S(1)} reduce(f32[128,2,128,2]{3,2,1,0:T(8,128)} %reshape.124, f32[]{:T(128)} %constant.6.clone.1), dimensions={1,3}, to_apply=%region_29.30 | reduce | flops 49152 | bytes 327684 | tf_op jit(solution)/shard_map/reduce_sum | solution.py:42
  291.1 41.0 %while.12 = (s32[]{:T(128)}, f32[1,128,128]{2,1,0:T(8,128)S(1)}, f32[1,128,128]{2,1,0:T(8,128)}, f32[1,128,128]{2,1,0:T(8,128)S(1)}, f32[1,128,128]{2,1,0:T(8,128)S(1)}, /*index=5*/s32[]{:T(128)}) while((s32[]{:T(128)}, f32[1,128,128]{2,1,0:T(8,128)S(1)}, f32[1,128,128]{2,1,0:T(8,128)}, f32[1,128,128]{2,1,0:T(8,128)S(1)}, ...), condition=%wide.region_28.29_spmd, body=%wide.region_27.28_spmd.sunk | while | flops 32770 | bytes 786569 | solution.py:108
  291.1 1.3 collective-permute-start
  292.4 26.7 %collective-permute-done = f32[1,128,128]{2,1,0:T(8,128)S(1)} collective-permute-done((f32[1,128,128]{2,1,0:T(8,128)S(1)}, f32[1,128,128]{2,1,0:T(8,128)S(1)}, u32[]{:S(2)}, u32[]{:S(2)}) %collective-permute-start) | collective-permute-done | bytes 65568 | tf_op jit(solution)/shard_map/while/body/eval_jaxpr/ppermute | solution.py:30
  319.1 0.6 copy-done
  319.7 1.3 collective-permute-start
  321.0 4.3 %collective-permute-done = f32[1,128,128]{2,1,0:T(8,128)S(1)} collective-permute-done((f32[1,128,128]{2,1,0:T(8,128)S(1)}, f32[1,128,128]{2,1,0:T(8,128)S(1)}, u32[]{:S(2)}, u32[]{:S(2)}) %collective-permute-start) | collective-permute-done | bytes 65568 | tf_op jit(solution)/shard_map/while/body/eval_jaxpr/ppermute | solution.py:30
  325.3 0.6 copy-done
  325.9 1.3 collective-permute-start
  327.2 4.3 %collective-permute-done = f32[1,128,128]{2,1,0:T(8,128)S(1)} collective-permute-done((f32[1,128,128]{2,1,0:T(8,128)S(1)}, f32[1,128,128]{2,1,0:T(8,128)S(1)}, u32[]{:S(2)}, u32[]{:S(2)}) %collective-permute-start) | collective-permute-done | bytes 65568 | tf_op jit(solution)/shard_map/while/body/eval_jaxpr/ppermute | solution.py:30
  332.1 0.8 fusion.46
  333.5 0.8 copy.26
  (71 shorter events, 5.5 us)
Async XLA Ops:
  0.0 24.7 %copy-start.1 = (s32[1,256,256]{2,1,0:T(8,128)S(1)}, s32[1,256,256]{2,1,0:T(8,128)}, u32[]{:S(2)}) copy-start(s32[1,256,256]{2,1,0:T(8,128)} %param.7) | copy-start | bytes 786436
  1.1 31.7 %collective-permute-start.1 = (f32[1,256,256]{1,2,0:T(8,128)S(1)}, f32[1,256,256]{1,2,0:T(8,128)S(1)}, u32[]{:S(2)}, u32[]{:S(2)}) collective-permute-start(f32[1,256,256]{1,2,0:T(8,128)S(1)} %bitcast.34), channel_id=1, source_target_pairs={{4,0},{8,4},{12,8},{0,12},{5,1},{9,5},{13,9},{1,13},{6,2},{10,6},{... | collective-permute-start | bytes 786440 | tf_op jit(solution)/shard_map/ppermute | solution.py:22
  1.4 31.5 %collective-permute-start.2 = (f32[1,256,256]{1,2,0:T(8,128)S(1)}, f32[1,256,256]{1,2,0:T(8,128)S(1)}, u32[]{:S(2)}, u32[]{:S(2)}) collective-permute-start(f32[1,256,256]{1,2,0:T(8,128)S(1)} %bitcast.35), channel_id=1, source_target_pairs={{0,4},{4,8},{8,12},{12,0},{1,5},{5,9},{9,13},{13,1},{2,6},{6,10},{... | collective-permute-start | bytes 786440 | tf_op jit(solution)/shard_map/ppermute | solution.py:21
  35.9 23.2 %collective-permute-start.3 = (f32[1,256,256]{1,2,0:T(8,128)S(1)}, f32[1,256,256]{1,2,0:T(8,128)S(1)}, u32[]{:S(2)}, u32[]{:S(2)}) collective-permute-start(f32[1,256,256]{1,2,0:T(8,128)S(1)} %get-tuple-element.60), channel_id=1, source_target_pairs={{4,0},{8,4},{12,8},{0,12},{5,1},{9,5},{13,9},{1,13},{6,2},{10,6},{... | collective-permute-start | bytes 786440 | tf_op jit(solution)/shard_map/ppermute | solution.py:22
  38.0 21.1 %collective-permute-start.4 = (f32[1,256,256]{1,2,0:T(8,128)S(1)}, f32[1,256,256]{1,2,0:T(8,128)S(1)}, u32[]{:S(2)}, u32[]{:S(2)}) collective-permute-start(f32[1,256,256]{1,2,0:T(8,128)S(1)} %get-tuple-element.60), channel_id=1, source_target_pairs={{0,4},{4,8},{8,12},{12,0},{1,5},{5,9},{9,13},{13,1},{2,6},{6,10},{... | collective-permute-start | bytes 786440 | tf_op jit(solution)/shard_map/ppermute | solution.py:21
  84.3 8.1 %collective-permute-start.5 = (f32[1,256,256]{1,2,0:T(8,128)S(1)}, f32[1,256,256]{1,2,0:T(8,128)S(1)}, u32[]{:S(2)}, u32[]{:S(2)}) collective-permute-start(f32[1,256,256]{1,2,0:T(8,128)S(1)} %multiply_add_fusion.5), channel_id=1, source_target_pairs={{4,0},{8,4},{12,8},{0,12},{5,1},{9,5},{13,9},{1,13},{6,2},{10,6},{... | collective-permute-start | bytes 786440 | tf_op jit(solution)/shard_map/ppermute | solution.py:22
  84.3 8.1 %collective-permute-start.6 = (f32[1,256,256]{1,2,0:T(8,128)S(1)}, f32[1,256,256]{1,2,0:T(8,128)S(1)}, u32[]{:S(2)}, u32[]{:S(2)}) collective-permute-start(f32[1,256,256]{1,2,0:T(8,128)S(1)} %multiply_add_fusion.5), channel_id=1, source_target_pairs={{0,4},{4,8},{8,12},{12,0},{1,5},{5,9},{9,13},{13,1},{2,6},{6,10},{... | collective-permute-start | bytes 786440 | tf_op jit(solution)/shard_map/ppermute | solution.py:21
  121.6 8.2 %collective-permute-start.7 = (f32[1,256,256]{1,2,0:T(8,128)S(1)}, f32[1,256,256]{1,2,0:T(8,128)S(1)}, u32[]{:S(2)}, u32[]{:S(2)}) collective-permute-start(f32[1,256,256]{1,2,0:T(8,128)S(1)} %multiply_add_fusion.4), channel_id=1, source_target_pairs={{4,0},{8,4},{12,8},{0,12},{5,1},{9,5},{13,9},{1,13},{6,2},{10,6},{... | collective-permute-start | bytes 786440 | tf_op jit(solution)/shard_map/ppermute | solution.py:22
  121.7 8.1 %collective-permute-start.8 = (f32[1,256,256]{1,2,0:T(8,128)S(1)}, f32[1,256,256]{1,2,0:T(8,128)S(1)}, u32[]{:S(2)}, u32[]{:S(2)}) collective-permute-start(f32[1,256,256]{1,2,0:T(8,128)S(1)} %multiply_add_fusion.4), channel_id=1, source_target_pairs={{0,4},{4,8},{8,12},{12,0},{1,5},{5,9},{9,13},{13,1},{2,6},{6,10},{... | collective-permute-start | bytes 786440 | tf_op jit(solution)/shard_map/ppermute | solution.py:21
  140.2 8.4 %collective-permute-start.9 = (f32[1,256,256]{1,2,0:T(8,128)S(1)}, f32[1,256,256]{1,2,0:T(8,128)S(1)}, u32[]{:S(2)}, u32[]{:S(2)}) collective-permute-start(f32[1,256,256]{1,2,0:T(8,128)S(1)} %multiply_add_fusion.3), channel_id=1, source_target_pairs={{4,0},{8,4},{12,8},{0,12},{5,1},{9,5},{13,9},{1,13},{6,2},{10,6},{... | collective-permute-start | bytes 786440 | tf_op jit(solution)/shard_map/ppermute | solution.py:22
  141.8 7.1 %collective-permute-start.10 = (f32[1,256,256]{1,2,0:T(8,128)S(1)}, f32[1,256,256]{1,2,0:T(8,128)S(1)}, u32[]{:S(2)}, u32[]{:S(2)}) collective-permute-start(f32[1,256,256]{1,2,0:T(8,128)S(1)} %multiply_add_fusion.3), channel_id=1, source_target_pairs={{0,4},{4,8},{8,12},{12,0},{1,5},{5,9},{9,13},{13,1},{2,6},{6,10},{... | collective-permute-start | bytes 786440 | tf_op jit(solution)/shard_map/ppermute | solution.py:21
  151.8 5.3 %collective-permute-start.11 = (f32[1,256,256]{1,2,0:T(8,128)S(1)}, f32[1,256,256]{1,2,0:T(8,128)S(1)}, u32[]{:S(2)}, u32[]{:S(2)}) collective-permute-start(f32[1,256,256]{1,2,0:T(8,128)S(1)} %fusion.28), channel_id=1, source_target_pairs={{4,0},{8,4},{12,8},{0,12},{5,1},{9,5},{13,9},{1,13},{6,2},{10,6},{... | collective-permute-start | bytes 786440 | tf_op jit(solution)/shard_map/ppermute | solution.py:22
  153.1 10.7 %collective-permute-start.12 = (f32[1,256,256]{1,2,0:T(8,128)S(1)}, f32[1,256,256]{1,2,0:T(8,128)S(1)}, u32[]{:S(2)}, u32[]{:S(2)}) collective-permute-start(f32[1,256,256]{1,2,0:T(8,128)S(1)} %fusion.28), channel_id=1, source_target_pairs={{0,4},{4,8},{8,12},{12,0},{1,5},{5,9},{9,13},{13,1},{2,6},{6,10},{... | collective-permute-start | bytes 786440 | tf_op jit(solution)/shard_map/ppermute | solution.py:21
  187.5 8.1 %collective-permute-start.13 = (f32[1,256,256]{1,2,0:T(8,128)S(1)}, f32[1,256,256]{1,2,0:T(8,128)S(1)}, u32[]{:S(2)}, u32[]{:S(2)}) collective-permute-start(f32[1,256,256]{1,2,0:T(8,128)S(1)} %multiply_add_fusion.2), channel_id=1, source_target_pairs={{4,0},{8,4},{12,8},{0,12},{5,1},{9,5},{13,9},{1,13},{6,2},{10,6},{... | collective-permute-start | bytes 786440 | tf_op jit(solution)/shard_map/ppermute | solution.py:22
  187.6 8.1 %collective-permute-start.14 = (f32[1,256,256]{1,2,0:T(8,128)S(1)}, f32[1,256,256]{1,2,0:T(8,128)S(1)}, u32[]{:S(2)}, u32[]{:S(2)}) collective-permute-start(f32[1,256,256]{1,2,0:T(8,128)S(1)} %multiply_add_fusion.2), channel_id=1, source_target_pairs={{0,4},{4,8},{8,12},{12,0},{1,5},{5,9},{9,13},{13,1},{2,6},{6,10},{... | collective-permute-start | bytes 786440 | tf_op jit(solution)/shard_map/ppermute | solution.py:21
  217.3 5.3 %collective-permute-start.15 = (f32[1,256,256]{1,2,0:T(8,128)S(1)}, f32[1,256,256]{1,2,0:T(8,128)S(1)}, u32[]{:S(2)}, u32[]{:S(2)}) collective-permute-start(f32[1,256,256]{1,2,0:T(8,128)S(1)} %multiply_add_fusion.1), channel_id=1, source_target_pairs={{4,0},{8,4},{12,8},{0,12},{5,1},{9,5},{13,9},{1,13},{6,2},{10,6},{... | collective-permute-start | bytes 786440 | tf_op jit(solution)/shard_map/ppermute | solution.py:22
  218.0 7.6 %collective-permute-start.16 = (f32[1,256,256]{1,2,0:T(8,128)S(1)}, f32[1,256,256]{1,2,0:T(8,128)S(1)}, u32[]{:S(2)}, u32[]{:S(2)}) collective-permute-start(f32[1,256,256]{1,2,0:T(8,128)S(1)} %multiply_add_fusion.1), channel_id=1, source_target_pairs={{0,4},{4,8},{8,12},{12,0},{1,5},{5,9},{9,13},{13,1},{2,6},{6,10},{... | collective-permute-start | bytes 786440 | tf_op jit(solution)/shard_map/ppermute | solution.py:21
  236.7 28.2 %collective-permute-start.17 = (f32[1,256,256]{1,2,0:T(8,128)S(1)}, f32[1,256,256]{1,2,0:T(8,128)S(1)}, u32[]{:S(2)}, u32[]{:S(2)}) collective-permute-start(f32[1,256,256]{1,2,0:T(8,128)S(1)} %add_subtract_fusion), channel_id=1, source_target_pairs={{0,1},{1,2},{2,3},{4,5},{5,6},{6,7},{8,9},{9,10},{10,11},{12,13},{... | collective-permute-start | bytes 786440 | tf_op jit(solution)/shard_map/ppermute | solution.py:30
  291.1 28.0 %collective-permute-start = (f32[1,128,128]{2,1,0:T(8,128)S(1)}, f32[1,128,128]{2,1,0:T(8,128)S(1)}, u32[]{:S(2)}, u32[]{:S(2)}) collective-permute-start(f32[1,128,128]{2,1,0:T(8,128)S(1)} %get-tuple-element.159), channel_id=1, source_target_pairs={{0,1},{1,2},{2,3},{4,5},{5,6},{6,7},{8,9},{9,10},{10,11},{12,13},{... | collective-permute-start | bytes 196616 | tf_op jit(solution)/shard_map/while/body/eval_jaxpr/ppermute | solution.py:30
  319.1 0.6 copy-start
  319.7 5.6 %collective-permute-start = (f32[1,128,128]{2,1,0:T(8,128)S(1)}, f32[1,128,128]{2,1,0:T(8,128)S(1)}, u32[]{:S(2)}, u32[]{:S(2)}) collective-permute-start(f32[1,128,128]{2,1,0:T(8,128)S(1)} %get-tuple-element.159), channel_id=1, source_target_pairs={{0,1},{1,2},{2,3},{4,5},{5,6},{6,7},{8,9},{9,10},{10,11},{12,13},{... | collective-permute-start | bytes 196616 | tf_op jit(solution)/shard_map/while/body/eval_jaxpr/ppermute | solution.py:30
  325.3 0.6 copy-start
  325.9 5.6 %collective-permute-start = (f32[1,128,128]{2,1,0:T(8,128)S(1)}, f32[1,128,128]{2,1,0:T(8,128)S(1)}, u32[]{:S(2)}, u32[]{:S(2)}) collective-permute-start(f32[1,128,128]{2,1,0:T(8,128)S(1)} %get-tuple-element.159), channel_id=1, source_target_pairs={{0,1},{1,2},{2,3},{4,5},{5,6},{6,7},{8,9},{9,10},{10,11},{12,13},{... | collective-permute-start | bytes 196616 | tf_op jit(solution)/shard_map/while/body/eval_jaxpr/ppermute | solution.py:30
  331.5 0.6 copy-start
where the time goes:
time: 339 us; the launch traced here: 334 us
  blocking collectives  90.9 us (27%)
  local copies, waits for them, and re-layouts  83.3 us (25%)
  waiting for transfers between devices  79.1 us (23%)
  other arithmetic  49.6 us (15%)
  starting transfers between devices  17.9 us (5%)
  between operations  13.3 us (4%)
    psum x6, blocking collectives, squares(): return lax.psum(jnp.sum(residual * residual), 'space')  58.3 us
    reshape x3, local copies, waits for them, and re-layouts, restrict(): return field.reshape(cx, ny // 2, 2, nz // 2, 2).mean(axis=(2, 4))  54.3 us
    ppermute x4, waiting for transfers between devices, passed_along(): return lax.ppermute(array, axis, pairs)  35.8 us
    ppermute x8, waiting for transfers between devices, with_halo(): after = lax.ppermute(first, axis, down)  33.1 us
    psum x4, blocking collectives, fine_step(): alpha = norm_now / lax.psum(jnp.sum(direction * image), 'space')  32.6 us
    reduce_sum x4, other arithmetic, restrict(): return field.reshape(cx, ny // 2, 2, nz // 2, 2).mean(axis=(2, 4))  32 us
    another operation x1, local copies, waits for them, and re-layouts, restrict(): return field.reshape(cx, ny // 2, 2, nz // 2, 2).mean(axis=(2, 4))  18.9 us
    ppermute x8, waiting for transfers between devices, with_halo(): before = lax.ppermute(last, axis, up)  10.1 us
  transfers between devices with their start and end apart: 20, of which 14 were waited for; matrix products, arithmetic and copies ran while one was open for 23% of the time, Pallas kernels for 0%

commit v1 on v0

--- a/solution.py
+++ b/solution.py
@@ -1,6 +1,8 @@
 import jax
 import jax.numpy as jnp
 from jax import lax
+from jax.experimental import pallas as pl
+from jax.experimental.pallas import tpu as pltpu
 from jax.sharding import PartitionSpec as P
 
 ITERS = 3
@@ -9,6 +11,10 @@
 
 DIFF = 2.0
 ADV = 0.25
+
+PAD = 8
+ROWS = 16
+MOST_PLANES = 8
 
 
 def with_halo(array, sides, width):
@@ -84,7 +90,7 @@
     return solution
 
 
-def body(state, classes, perm_table, rate_table):
+def spread_body(state, classes, perm_table, rate_table):
     start = state[0]
     perm = lookup(perm_table, classes)
     coarse_ratio = 1.0 / (1.0 + restrict(lookup(rate_table, classes)))
@@ -112,6 +118,331 @@
     return updated[None]
 
 
+def beside_in_plane(block, lane, cells):
+    rows = block.shape[0]
+    inner = block[PAD:rows - PAD]
+    after = pltpu.roll(block, rows - 1, 0)[PAD:rows - PAD]
+    before = pltpu.roll(block, 1, 0)[PAD:rows - PAD]
+    upper = jnp.where(lane == cells - 1, 0.0, pltpu.roll(inner, cells - 1, 1))
+    lower = jnp.where(lane == 0, 0.0, pltpu.roll(inner, 1, 1))
+    return inner, after + before, upper, lower
+
+
+def gram_steps(g00, g01, g11, g12, g22, h22):
+    a = 1.0 + 6.0 * DIFF
+    b = 6.0 * DIFF
+    g02 = 2.0 * g11 - g00
+    h00, h01, h02 = g01, g11, g12
+    h11, h12 = 0.5 * (g12 + g01), 0.5 * (g22 + g02)
+    rr = g00
+    alpha0 = rr / (a * g00 - b * h00)
+    p, q = 1.0 - a * alpha0, b * alpha0
+    new = p * p * g00 + 2.0 * p * q * g01 + q * q * g11
+    beta = new / rr
+    rr = new
+    e, f = p + beta, q
+    dd = e * e * g00 + 2.0 * e * f * g01 + f * f * g11
+    dmd = e * e * h00 + 2.0 * e * f * h01 + f * f * h11
+    alpha1 = rr / (a * dd - b * dmd)
+    u = p - alpha1 * (a * e - 0.5 * b * f)
+    v = q - alpha1 * (a * f - b * e)
+    w = alpha1 * (0.5 * b) * f
+    new = (u * u * g00 + v * v * g11 + w * w * g22
+           + 2.0 * (u * v * g01 + u * w * g02 + v * w * g12))
+    beta = new / rr
+    rr = new
+    u, v = u + beta * e, v + beta * f
+    dd = (u * u * g00 + v * v * g11 + w * w * g22
+          + 2.0 * (u * v * g01 + u * w * g02 + v * w * g12))
+    dmd = (u * u * h00 + v * v * h11 + w * w * h22
+           + 2.0 * (u * v * h01 + u * w * h02 + v * w * h12))
+    alpha2 = rr / (a * dd - b * dmd)
+    return (alpha0 + alpha1 * e + alpha2 * u, alpha1 * f + alpha2 * v, alpha2 * w)
+
+
+def fine_kernel(planes, ny, nz, table_len):
+    chunks = ny // ROWS
+
+    def kernel(table, *refs):
+        state_in = refs[:planes]
+        classes_in = refs[planes:2 * planes]
+        outs = refs[2 * planes:3 * planes]
+        x, r, p1, p2, perm, sems = refs[3 * planes:]
+        copies = []
+        for i in range(planes):
+            src = state_in[i]
+            parts = (
+                (src, x.at[i, pl.ds(PAD, ny)]),
+                (src.at[pl.ds(ny - PAD, PAD)], x.at[i, pl.ds(0, PAD)]),
+                (src.at[pl.ds(0, PAD)], x.at[i, pl.ds(PAD + ny, PAD)]),
+                (classes_in[i], perm.at[i]),
+            )
+            for k, (a, b) in enumerate(parts):
+                copies.append(pltpu.make_async_copy(a, b, sems.at[i, k]))
+        for copy in copies:
+            copy.start()
+        for copy in copies:
+            copy.wait()
+        lane = lax.broadcasted_iota(jnp.int32, (ROWS, nz), 1)
+        zero = jnp.zeros((8, nz), jnp.float32)
+
+        def folded(value):
+            total = value[:8]
+            for k in range(8, ROWS, 8):
+                total = total + value[k:k + 8]
+            return total
+
+        def total(acc):
+            return jnp.sum(jnp.sum(acc, axis=1, keepdims=True), axis=0, keepdims=True)
+
+        def wrap(field):
+            for i in range(planes):
+                field[i, pl.ds(0, PAD)] = field[i, pl.ds(ny, PAD)]
+                field[i, pl.ds(PAD + ny, PAD)] = field[i, pl.ds(PAD, PAD)]
+
+        def stencil(field, row):
+            parts = []
+            for i in range(planes):
+                block = field[i, pl.ds(row, ROWS + 2 * PAD)]
+                parts.append(beside_in_plane(block, lane, nz))
+            result = []
+            for i in range(planes):
+                inner, along_y, upper, lower = parts[i]
+                along_x = parts[i - 1][0] + parts[(i + 1) % planes][0]
+                result.append((inner, along_x + along_y + (upper + lower), upper, lower))
+            return result
+
+        for step in range(FINE):
+            last = step == FINE - 1
+
+            def first_pass(c, g00):
+                row = pl.multiple_of(c * ROWS, ROWS)
+                for i, (v, six, upper, lower) in enumerate(stencil(x, row)):
+                    kind = perm[i, pl.ds(row, ROWS)]
+                    k = jnp.zeros((ROWS, nz), jnp.float32)
+                    for entry in range(table_len):
+                        k = jnp.where(kind == entry, table[entry], k)
+                    value = DIFF * six - (6.0 * DIFF) * v - ADV * k * v * (upper - lower)
+                    r[i, pl.ds(row + PAD, ROWS)] = value
+                    g00 = g00 + folded(value * value)
+                return g00
+
+            g00 = lax.fori_loop(0, chunks, first_pass, zero)
+            wrap(r)
+
+            def second_pass(c, carry):
+                g01, g11 = carry
+                row = pl.multiple_of(c * ROWS, ROWS)
+                for i, (v, six, _, _) in enumerate(stencil(r, row)):
+                    value = six * (1.0 / 6.0)
+                    p1[i, pl.ds(row + PAD, ROWS)] = value
+                    g01 = g01 + folded(value * v)
+                    g11 = g11 + folded(value * value)
+                return g01, g11
+
+            g01, g11 = lax.fori_loop(0, chunks, second_pass, (zero, zero))
+            wrap(p1)
+
+            def third_pass(c, carry):
+                g12, g22 = carry
+                row = pl.multiple_of(c * ROWS, ROWS)
+                for i, (v, six, _, _) in enumerate(stencil(p1, row)):
+                    value = six * (1.0 / 3.0) - r[i, pl.ds(row + PAD, ROWS)]
+                    p2[i, pl.ds(row + PAD, ROWS)] = value
+                    g12 = g12 + folded(value * v)
+                    g22 = g22 + folded(value * value)
+                return g12, g22
+
+            g12, g22 = lax.fori_loop(0, chunks, third_pass, (zero, zero))
+            wrap(p2)
+
+            def fourth_pass(c, h22):
+                row = pl.multiple_of(c * ROWS, ROWS)
+                inner = []
+                for i in range(planes):
+                    block = p2[i, pl.ds(row, ROWS + 2 * PAD)]
+                    rows = ROWS + 2 * PAD
+                    v = block[PAD:rows - PAD]
+                    after = pltpu.roll(block, rows - 1, 0)[PAD:rows - PAD]
+                    upper = jnp.where(lane == nz - 1, 0.0, pltpu.roll(v, nz - 1, 1))
+                    inner.append((v, after + upper))
+                for i in range(planes):
+                    v, some = inner[i]
+                    h22 = h22 + folded(v * (some + inner[(i + 1) % planes][0]))
+                return h22
+
+            h22 = lax.fori_loop(0, chunks, fourth_pass, zero)
+            c0, c1, c2 = gram_steps(
+                total(g00), total(g01), total(g11), total(g12), total(g22),
+                total(h22) * (1.0 / 3.0))
+
+            def last_pass(c, carry):
+                row = pl.multiple_of(c * ROWS, ROWS)
+                rows = pl.ds(row + PAD, ROWS)
+                for i in range(planes):
+                    value = (x[i, rows] + c0 * r[i, rows]) + (c1 * p1[i, rows] + c2 * p2[i, rows])
+                    if last:
+                        outs[i][pl.ds(row, ROWS)] = value
+                    else:
+                        x[i, rows] = value
+                return carry
+
+            lax.fori_loop(0, chunks, last_pass, 0)
+            if not last:
+                wrap(x)
+
+    return kernel
+
+
+def fine_steps(state_planes, classes_planes, table):
+    planes = len(state_planes)
+    ny, nz = state_planes[0].shape
+    any_space = pl.BlockSpec(memory_space=pl.ANY)
+    field = pltpu.VMEM((planes, ny + 2 * PAD, nz), jnp.float32)
+    return pl.pallas_call(
+        fine_kernel(planes, ny, nz, table.shape[0]),
+        out_shape=[jax.ShapeDtypeStruct((ny, nz), jnp.float32)] * planes,
+        in_specs=[pl.BlockSpec(memory_space=pltpu.SMEM)] + [any_space] * (2 * planes),
+        out_specs=[pl.BlockSpec(memory_space=pltpu.VMEM)] * planes,
+        scratch_shapes=[field, field, field, field,
+                        pltpu.VMEM((planes, ny, nz), jnp.int32),
+                        pltpu.SemaphoreType.DMA((planes, 4))],
+        compiler_params=pltpu.CompilerParams(vmem_limit_bytes=48 * 1024 * 1024),
+        name="fine_steps",
+    )(table, *state_planes, *classes_planes)
+
+
+def pairs_matrix(coarse, fine, transposed):
+    shape = (fine, coarse) if transposed else (coarse, fine)
+    along_coarse = lax.broadcasted_iota(jnp.int32, shape, 1 if transposed else 0)
+    along_fine = lax.broadcasted_iota(jnp.int32, shape, 0 if transposed else 1)
+    return jnp.where(along_fine // 2 == along_coarse, 1.0, 0.0).astype(jnp.float32)
+
+
+def exact_dot(a, b):
+    return jnp.dot(a, b, precision=lax.Precision.HIGHEST, preferred_element_type=jnp.float32)
+
+
+def restrict_plane(field):
+    ny, nz = field.shape
+    rows = exact_dot(pairs_matrix(ny // 2, ny, False), field)
+    return 0.25 * exact_dot(rows, pairs_matrix(nz // 2, nz, True))
+
+
+def prolong_plane(coarse):
+    cy, cz = coarse.shape
+    rows = exact_dot(pairs_matrix(cy, 2 * cy, True), coarse)
+    return exact_dot(rows, pairs_matrix(cz, 2 * cz, False))
+
+
+def ratio_plane(classes, rate_table):
+    ny, nz = classes.shape
+
+    def kernel(table, kind, out):
+        rate = jnp.zeros((ny, nz), jnp.float32)
+        for entry in range(rate_table.shape[0]):
+            rate = jnp.where(kind[...] == entry, table[entry], rate)
+        out[...] = 1.0 / (1.0 + restrict_plane(rate))
+
+    return pl.pallas_call(
+        kernel,
+        out_shape=jax.ShapeDtypeStruct((ny // 2, nz // 2), jnp.float32),
+        in_specs=[pl.BlockSpec(memory_space=pltpu.SMEM), pl.BlockSpec(memory_space=pltpu.VMEM)],
+        out_specs=pl.BlockSpec(memory_space=pltpu.VMEM),
+        name="ratio",
+    )(rate_table, classes)
+
+
+def settle(which, candidates, start):
+    ny, nz = start.shape
+    count = len(candidates)
+
+    def kernel(choice, *refs):
+        own, end, diff, sem = refs[count], refs[count + 1], refs[count + 2], refs[count + 3]
+        for k in range(count):
+            @pl.when(choice[0] == k)
+            def _():
+                copy = pltpu.make_async_copy(refs[k], end, sem)
+                copy.start()
+                copy.wait()
+        diff[...] = restrict_plane(end[...] - own[...])
+
+    return pl.pallas_call(
+        kernel,
+        out_shape=[jax.ShapeDtypeStruct((ny, nz), jnp.float32),
+                   jax.ShapeDtypeStruct((ny // 2, nz // 2), jnp.float32)],
+        in_specs=[pl.BlockSpec(memory_space=pltpu.SMEM)]
+        + [pl.BlockSpec(memory_space=pl.ANY)] * count
+        + [pl.BlockSpec(memory_space=pltpu.VMEM)],
+        out_specs=[pl.BlockSpec(memory_space=pltpu.VMEM)] * 2,
+        scratch_shapes=[pltpu.SemaphoreType.DMA(())],
+        name="settle",
+    )(which, *candidates, start)
+
+
+def correct(first, ratio, diffs, end, start):
+    ny, nz = start.shape
+    count = len(diffs)
+
+    def kernel(is_first, share, *refs):
+        end_ref, start_ref, out = refs[count:]
+        drift = jnp.zeros((ny // 2, nz // 2), jnp.float32)
+        for k in reversed(range(count)):
+            drift = share[...] * (drift + refs[k][...])
+        moved = end_ref[...] + prolong_plane(drift)
+        out[...] = jnp.where(is_first[0] == 1, start_ref[...], moved)
+
+    vmem = pl.BlockSpec(memory_space=pltpu.VMEM)
+    return pl.pallas_call(
+        kernel,
+        out_shape=jax.ShapeDtypeStruct((ny, nz), jnp.float32),
+        in_specs=[pl.BlockSpec(memory_space=pltpu.SMEM)] + [vmem] * (count + 3),
+        out_specs=vmem,
+        name="correct",
+    )(first, ratio, *diffs, end, start)
+
+
+def gathered_body(state, classes, perm_table, rate_table):
+    start = state[0, 0]
+    kinds = classes[0]
+    width, slices = lax.axis_size("space"), lax.axis_size("tm")
+    axes = ("space", "tm")
+    place = lambda s, t: (s % width) * slices + t
+    site = lambda j: (width // 2 - 1 + j % 2) % width
+    used = range(slices - 1)
+    state_planes = [
+        lax.ppermute(start, axes, [(place(site(j) + k, j), place(site(j), j + 1)) for j in used])
+        for k in range(width)
+    ]
+    classes_planes = [kinds] + [
+        lax.ppermute(kinds, axes, [(place(site(j) + k, j + 1), place(site(j), j + 1)) for j in used])
+        for k in range(1, width)
+    ]
+    ratio = ratio_plane(kinds, rate_table)
+    ends = fine_steps(state_planes, classes_planes, perm_table)
+    candidates = [ends[0]] + [
+        lax.ppermute(ends[k], axes, [(place(site(j), j + 1), place(site(j) + k, j + 1)) for j in used])
+        for k in range(1, width)
+    ]
+    turn = lax.axis_index("tm")
+    which = (lax.axis_index("space") - site(turn - 1)) % width
+    end, diff = settle(which.astype(jnp.int32)[None], candidates, start)
+    diffs = [
+        lax.ppermute(diff, "tm", [(i, i + k) for i in range(1, slices - k)])
+        for k in range(1, slices - 1)
+    ]
+    new = correct((turn == 0).astype(jnp.int32)[None], ratio, diffs, end, start)
+    return new[None, None]
+
+
+def body(state, classes, perm_table, rate_table):
+    width = lax.axis_size("space")
+    one_plane = state.shape[:2] == (1, 1) and classes.shape[0] == 1
+    if one_plane and 2 < width <= MOST_PLANES and lax.axis_size("tm") > 2:
+        return gathered_body(state, classes, perm_table, rate_table)
+    return spread_body(state, classes, perm_table, rate_table)
+
+
 def solution(mesh):
     placed = (
         P(("groups", "tm"), "space", None, None),

time: 339 us -> 65.3 us (0.19); the launches traced: 334 us -> 64.5 us
  blocking collectives: 90.9 us -> 0 us
  local copies, waits for them, and re-layouts: 83.3 us -> 2.96 us
  waiting for transfers between devices: 79.1 us -> 22.2 us
  other arithmetic: 49.6 us -> 0 us
  Pallas kernels: 0 us -> 23.5 us
  between operations: 13.3 us -> 0.21 us
    psum x10 -> x0, blocking collectives: 90.9 us -> none  [the longest x6 58.3 us: squares(): return lax.psum(jnp.sum(residual * residual), 'space')]
    ppermute x20 -> x12, waiting for transfers between devices: 79.1 us -> 22.2 us  [the longest x4 6.17 us: gathered_body(): lax.ppermute(start, axes, [(place(site(j) + k, j), place(site(j), j + 1))...]
    reshape x3 -> x0, local copies, waits for them, and re-layouts: 54.3 us -> none  [restrict(): return field.reshape(cx, ny // 2, 2, nz // 2, 2).mean(axis=(2, 4))]
    reduce_sum x14 -> x0, other arithmetic: 39.9 us -> none  [the longest x4 32 us: restrict(): return field.reshape(cx, ny // 2, 2, nz // 2, 2).mean(axis=(2, 4))]
    pallas_call x0 -> x4, Pallas kernels: none -> 23.5 us  [the longest x1 15.4 us: fine_steps(): pl.pallas_call(fine_kernel(planes, ny, nz, table.shape[0]), out_shape=[ja...]
    another operation x1 -> x0, local copies, waits for them, and re-layouts: 18.9 us -> none  [restrict(): return field.reshape(cx, ny // 2, 2, nz // 2, 2).mean(axis=(2, 4))]
    sub x4 -> x0, other arithmetic: 6.74 us -> none  [the longest x2 5.81 us: fine_step(): residual = rhs - operate(solution)]
    slice x26 -> x0, local copies, waits for them, and re-layouts: 5.01 us -> none  [the longest x2 2.94 us: lookup(): values = jnp.where(classes == entry, table[entry], values)]
  transfers between devices with their start and end apart: 20 -> 12, of which waited for: 14 -> 8; matrix products, arithmetic and copies ran while one was open for 23% -> 0% of each run, Pallas kernels for 0% -> 4%
where the time goes in v1:
time: 65.3 us; the launch traced here: 64.5 us
  Pallas kernels  23.5 us (36%)
  waiting for transfers between devices  22.2 us (34%)
  starting transfers between devices  15.6 us (24%)
  local copies, waits for them, and re-layouts  2.96 us (5%)
    pallas_call x1, Pallas kernels, fine_steps(): pl.pallas_call(fine_kernel(planes, ny, nz, table.shape[0]), out_shape=[ja...  15.4 us
    ppermute x4, waiting for transfers between devices, gathered_body(): lax.ppermute(start, axes, [(place(site(j) + k, j), place(site(j), j + 1))...  6.17 us
    ppermute x3, waiting for transfers between devices, gathered_body(): lax.ppermute(ends[k], axes, [(place(site(j), j + 1), place(site(j) + k, j...  6.04 us
    ppermute x3, waiting for transfers between devices, gathered_body(): lax.ppermute(kinds, axes, [(place(site(j) + k, j + 1), place(site(j), j +...  6.01 us
    ppermute x4, starting transfers between devices, gathered_body(): lax.ppermute(start, axes, [(place(site(j) + k, j), place(site(j), j + 1))...  5.29 us
    ppermute x2, waiting for transfers between devices, gathered_body(): lax.ppermute(diff, 'tm', [(i, i + k) for i in range(1, slices - k)])  4.02 us
    ppermute x3, starting transfers between devices, gathered_body(): lax.ppermute(ends[k], axes, [(place(site(j), j + 1), place(site(j) + k, j...  3.91 us
    ppermute x3, starting transfers between devices, gathered_body(): lax.ppermute(kinds, axes, [(place(site(j) + k, j + 1), place(site(j), j +...  3.86 us
  transfers between devices with their start and end apart: 12, of which 8 were waited for; matrix products, arithmetic and copies ran while one was open for 0% of the time, Pallas kernels for 4%

profile of v1, /device:TPU:11, one launch (start us, length us, event | category | flops | bytes accessed | tf_op | source)
XLA Modules:
  0.0 64.5 jit_solution(13645364144751503036)
XLA Ops:
  0.0 0.0 copy-start.2
  0.0 1.4 %collective-permute-start = (f32[256,256]{1,0:T(8,128)}, f32[256,256]{1,0:T(8,128)S(1)}, u32[]{:S(2)}, u32[]{:S(2)}) collective-permute-start(f32[256,256]{1,0:T(8,128)} %bitcast.10), channel_id=1, source_target_pairs={{4,5},{9,10},{6,7},{20,21},{25,26},{22,23}} | collective-permute-start | bytes 786440 | tf_op jit(solution)/shard_map/ppermute | solution.py:414
  1.4 1.3 %collective-permute-start.1 = (f32[256,256]{1,0:T(8,128)}, f32[256,256]{1,0:T(8,128)S(1)}, u32[]{:S(2)}, u32[]{:S(2)}) collective-permute-start(f32[256,256]{1,0:T(8,128)} %bitcast.11), channel_id=1, source_target_pairs={{8,5},{13,10},{10,7},{24,21},{29,26},{26,23}} | collective-permute-start | bytes 786440 | tf_op jit(solution)/shard_map/ppermute | solution.py:414
  2.7 1.3 %collective-permute-start.2 = (f32[256,256]{1,0:T(8,128)}, f32[256,256]{1,0:T(8,128)S(1)}, u32[]{:S(2)}, u32[]{:S(2)}) collective-permute-start(f32[256,256]{1,0:T(8,128)} %bitcast.12), channel_id=1, source_target_pairs={{12,5},{1,10},{14,7},{28,21},{17,26},{30,23}} | collective-permute-start | bytes 786440 | tf_op jit(solution)/shard_map/ppermute | solution.py:414
  4.0 1.3 %collective-permute-start.3 = (f32[256,256]{1,0:T(8,128)}, f32[256,256]{1,0:T(8,128)S(1)}, u32[]{:S(2)}, u32[]{:S(2)}) collective-permute-start(f32[256,256]{1,0:T(8,128)} %bitcast.13), channel_id=1, source_target_pairs={{0,5},{5,10},{2,7},{16,21},{21,26},{18,23}} | collective-permute-start | bytes 786440 | tf_op jit(solution)/shard_map/ppermute | solution.py:414
  5.3 1.3 %collective-permute-start.4 = (s32[256,256]{1,0:T(8,128)}, s32[256,256]{1,0:T(8,128)S(1)}, u32[]{:S(2)}, u32[]{:S(2)}) collective-permute-start(s32[256,256]{1,0:T(8,128)} %bitcast.5), channel_id=1, source_target_pairs={{9,5},{14,10},{11,7},{25,21},{30,26},{27,23}} | collective-permute-start | bytes 786440 | tf_op jit(solution)/shard_map/ppermute | solution.py:418
  6.6 0.0 collective-permute-done.refs_0_
  6.6 1.3 %collective-permute-start.5 = (s32[256,256]{1,0:T(8,128)}, s32[256,256]{1,0:T(8,128)S(1)}, u32[]{:S(2)}, u32[]{:S(2)}) collective-permute-start(s32[256,256]{1,0:T(8,128)} %bitcast.6), channel_id=1, source_target_pairs={{13,5},{2,10},{15,7},{29,21},{18,26},{31,23}} | collective-permute-start | bytes 786440 | tf_op jit(solution)/shard_map/ppermute | solution.py:418
  7.9 6.2 %collective-permute-done.1.refs_1_ = f32[256,256]{1,0:T(8,128)S(1)} collective-permute-done((f32[256,256]{1,0:T(8,128)}, f32[256,256]{1,0:T(8,128)S(1)}, u32[]{:S(2)}, u32[]{:S(2)}) %collective-permute-start.1) | collective-permute-done | bytes 262176 | tf_op jit(solution)/shard_map/ppermute | solution.py:414
  14.1 1.3 %collective-permute-start.6 = (s32[256,256]{1,0:T(8,128)}, s32[256,256]{1,0:T(8,128)S(1)}, u32[]{:S(2)}, u32[]{:S(2)}) collective-permute-start(s32[256,256]{1,0:T(8,128)} %bitcast.7), channel_id=1, source_target_pairs={{1,5},{6,10},{3,7},{17,21},{22,26},{19,23}} | collective-permute-start | bytes 786440 | tf_op jit(solution)/shard_map/ppermute | solution.py:418
  15.4 0.0 collective-permute-done.2.refs_2_
  15.4 0.0 collective-permute-done.3.refs_3_
  15.4 2.5 %collective-permute-done.4.refs_5_ = s32[256,256]{1,0:T(8,128)S(1)} collective-permute-done((s32[256,256]{1,0:T(8,128)}, s32[256,256]{1,0:T(8,128)S(1)}, u32[]{:S(2)}, u32[]{:S(2)}) %collective-permute-start.4) | collective-permute-done | bytes 262176 | tf_op jit(solution)/shard_map/ppermute | solution.py:418
  17.9 0.0 collective-permute-done.5.refs_6_
  17.9 3.5 %collective-permute-done.6.refs_7_ = s32[256,256]{1,0:T(8,128)S(1)} collective-permute-done((s32[256,256]{1,0:T(8,128)}, s32[256,256]{1,0:T(8,128)S(1)}, u32[]{:S(2)}, u32[]{:S(2)}) %collective-permute-start.6) | collective-permute-done | bytes 262176 | tf_op jit(solution)/shard_map/ppermute | solution.py:418
  21.4 0.0 copy-done.2
  21.4 0.0 copy-start
  21.4 0.9 %copy-done = s32[1,256,256]{2,1,0:T(8,128)S(1)} copy-done((s32[1,256,256]{2,1,0:T(8,128)S(1)}, s32[1,256,256]{2,1,0:T(8,128)}, u32[]{:S(2)}) %copy-start) | copy-done | bytes 262168
  22.4 15.4 %fine_steps.1 = (f32[256,256]{1,0:T(8,128)S(1)}, f32[256,256]{1,0:T(8,128)S(1)}, f32[256,256]{1,0:T(8,128)S(1)}, f32[256,256]{1,0:T(8,128)S(1)}) custom-call(f32[4]{0:T(128)S(1)} %copy-done.2, f32[256,256]{1,0:T(8,128)S(1)} %collective-permute-done.refs_0_, f32[256,256]{1,0:T(8,128)S(1)} %collective-permute-done.1.refs_1_, ...), custom_call_target="tpu_custom_call" | custom-call | tf_op jit(solution)/shard_map/fine_steps/pallas_call | solution.py:302
  37.7 0.0 copy-start.1
  37.7 0.7 %copy-done.1 = f32[256,256]{1,0:T(8,128)} copy-done((f32[256,256]{1,0:T(8,128)}, f32[256,256]{1,0:T(8,128)S(1)}, u32[]{:S(2)}) %copy-start.1) | copy-done | bytes 262168
  38.4 1.3 %collective-permute-start.7 = (f32[256,256]{1,0:T(8,128)S(1)}, f32[256,256]{1,0:T(8,128)S(1)}, u32[]{:S(2)}, u32[]{:S(2)}) collective-permute-start(f32[256,256]{1,0:T(8,128)S(1)} %get-tuple-element.12), channel_id=1, source_target_pairs={{5,9},{10,14},{7,11},{21,25},{26,30},{23,27}} | collective-permute-start | bytes 786440 | tf_op jit(solution)/shard_map/ppermute | solution.py:424
  39.7 1.3 %collective-permute-start.8 = (f32[256,256]{1,0:T(8,128)S(1)}, f32[256,256]{1,0:T(8,128)S(1)}, u32[]{:S(2)}, u32[]{:S(2)}) collective-permute-start(f32[256,256]{1,0:T(8,128)S(1)} %get-tuple-element.13), channel_id=1, source_target_pairs={{5,13},{10,2},{7,15},{21,29},{26,18},{23,31}} | collective-permute-start | bytes 786440 | tf_op jit(solution)/shard_map/ppermute | solution.py:424
  41.1 1.3 %collective-permute-start.9 = (f32[256,256]{1,0:T(8,128)S(1)}, f32[256,256]{1,0:T(8,128)S(1)}, u32[]{:S(2)}, u32[]{:S(2)}) collective-permute-start(f32[256,256]{1,0:T(8,128)S(1)} %get-tuple-element.14), channel_id=1, source_target_pairs={{5,1},{10,6},{7,3},{21,17},{26,22},{23,19}} | collective-permute-start | bytes 786440 | tf_op jit(solution)/shard_map/ppermute | solution.py:424
  42.4 0.6 collective-permute-done.7.refs_1_
  43.0 0.0 copy-start.3
  43.0 2.9 %collective-permute-done.8.refs_2_ = f32[256,256]{1,0:T(8,128)S(1)} collective-permute-done((f32[256,256]{1,0:T(8,128)S(1)}, f32[256,256]{1,0:T(8,128)S(1)}, u32[]{:S(2)}, u32[]{:S(2)}) %collective-permute-start.8) | collective-permute-done | bytes 262176 | tf_op jit(solution)/shard_map/ppermute | solution.py:424
  45.9 0.0 copy-start.4
  45.9 2.6 %collective-permute-done.9.refs_3_ = f32[256,256]{1,0:T(8,128)S(1)} collective-permute-done((f32[256,256]{1,0:T(8,128)S(1)}, f32[256,256]{1,0:T(8,128)S(1)}, u32[]{:S(2)}, u32[]{:S(2)}) %collective-permute-start.9) | collective-permute-done | bytes 262176 | tf_op jit(solution)/shard_map/ppermute | solution.py:424
  48.5 0.0 copy-start.5
  48.5 0.0 copy-done.3
  48.5 0.0 copy-done.4
  48.5 0.7 %copy-done.5 = f32[256,256]{1,0:T(8,128)} copy-done((f32[256,256]{1,0:T(8,128)}, f32[256,256]{1,0:T(8,128)S(1)}, u32[]{:S(2)}) %copy-start.5) | copy-done | bytes 262168
  49.2 3.2 %settle.1 = (f32[256,256]{1,0:T(8,128)}, f32[128,128]{1,0:T(8,128)}) custom-call(s32[1]{0:T(128)} %bitcast.2.choice, f32[256,256]{1,0:T(8,128)} %copy-done.1, f32[256,256]{1,0:T(8,128)} %copy-done.3, f32[256,256]{1,0:T(8,128)} %copy-done.4, f32[256,256]{1,0:T(8,128)} %copy-done.5, f32[256,256]{1,0:T(8,128)} %bitcast.14), custom_call_target="tpu_custom_call" | custom-call | tf_op jit(solution)/shard_map/settle/pallas_call | solution.py:370
  52.4 1.3 %collective-permute-start.10 = (f32[128,128]{1,0:T(8,128)}, f32[128,128]{1,0:T(8,128)S(1)}, u32[]{:S(2)}, u32[]{:S(2)}) collective-permute-start(f32[128,128]{1,0:T(8,128)} %get-tuple-element.15), channel_id=1, source_target_pairs={{1,2},{2,3},{5,6},{6,7},{9,10},{10,11},{13,14},{14,15},{17,18},{18... | collective-permute-start | bytes 196616 | tf_op jit(solution)/shard_map/ppermute | solution.py:431
  53.7 1.3 %collective-permute-start.11 = (f32[128,128]{1,0:T(8,128)}, f32[128,128]{1,0:T(8,128)S(1)}, u32[]{:S(2)}, u32[]{:S(2)}) collective-permute-start(f32[128,128]{1,0:T(8,128)} %get-tuple-element.15), channel_id=1, source_target_pairs={{1,3},{5,7},{9,11},{13,15},{17,19},{21,23},{25,27},{29,31}} | collective-permute-start | bytes 196616 | tf_op jit(solution)/shard_map/ppermute | solution.py:431
  55.0 2.3 %ratio.1.share = f32[128,128]{1,0:T(8,128)} custom-call(f32[4]{0:T(128)} %table.2, s32[256,256]{1,0:T(8,128)} %bitcast.8), custom_call_target="tpu_custom_call" | custom-call | tf_op jit(solution)/shard_map/ratio/pallas_call | solution.py:347
  57.3 0.5 collective-permute-done.10.refs_0_
  57.7 0.0 copy-start.6
  57.7 3.5 %collective-permute-done.11.refs_1_ = f32[128,128]{1,0:T(8,128)S(1)} collective-permute-done((f32[128,128]{1,0:T(8,128)}, f32[128,128]{1,0:T(8,128)S(1)}, u32[]{:S(2)}, u32[]{:S(2)}) %collective-permute-start.11) | collective-permute-done | bytes 65568 | tf_op jit(solution)/shard_map/ppermute | solution.py:431
  61.3 0.0 copy-start.7
  61.3 0.0 copy-done.6
  61.3 0.6 copy-done.7
  61.9 2.6 %correct.1 = f32[256,256]{1,0:T(8,128)} custom-call(s32[1]{0:T(128)} %bitcast.is_first, f32[128,128]{1,0:T(8,128)} %ratio.1.share, f32[128,128]{1,0:T(8,128)} %copy-done.6, f32[128,128]{1,0:T(8,128)} %copy-done.7, f32[256,256]{1,0:T(8,128)} %get-tuple-element.16.refs_2_, f32[256,256]{1,0:T(8,128)} %bitcast.15), custom_call_target="tpu_custom_call" | custom-call | tf_op jit(solution)/shard_map/correct/pallas_call | solution.py:396
Async XLA Ops:
  0.0 21.4 %copy-start.2 = (f32[4]{0:T(128)S(1)}, f32[4]{0:T(128)}, u32[]{:S(2)}) copy-start(f32[4]{0:T(128)} %table.3) | copy-start | bytes 52
  0.0 6.6 %collective-permute-start = (f32[256,256]{1,0:T(8,128)}, f32[256,256]{1,0:T(8,128)S(1)}, u32[]{:S(2)}, u32[]{:S(2)}) collective-permute-start(f32[256,256]{1,0:T(8,128)} %bitcast.10), channel_id=1, source_target_pairs={{4,5},{9,10},{6,7},{20,21},{25,26},{22,23}} | collective-permute-start | bytes 786440 | tf_op jit(solution)/shard_map/ppermute | solution.py:414
  1.4 12.7 %collective-permute-start.1 = (f32[256,256]{1,0:T(8,128)}, f32[256,256]{1,0:T(8,128)S(1)}, u32[]{:S(2)}, u32[]{:S(2)}) collective-permute-start(f32[256,256]{1,0:T(8,128)} %bitcast.11), channel_id=1, source_target_pairs={{8,5},{13,10},{10,7},{24,21},{29,26},{26,23}} | collective-permute-start | bytes 786440 | tf_op jit(solution)/shard_map/ppermute | solution.py:414
  2.7 12.7 %collective-permute-start.2 = (f32[256,256]{1,0:T(8,128)}, f32[256,256]{1,0:T(8,128)S(1)}, u32[]{:S(2)}, u32[]{:S(2)}) collective-permute-start(f32[256,256]{1,0:T(8,128)} %bitcast.12), channel_id=1, source_target_pairs={{12,5},{1,10},{14,7},{28,21},{17,26},{30,23}} | collective-permute-start | bytes 786440 | tf_op jit(solution)/shard_map/ppermute | solution.py:414
  4.0 11.4 %collective-permute-start.3 = (f32[256,256]{1,0:T(8,128)}, f32[256,256]{1,0:T(8,128)S(1)}, u32[]{:S(2)}, u32[]{:S(2)}) collective-permute-start(f32[256,256]{1,0:T(8,128)} %bitcast.13), channel_id=1, source_target_pairs={{0,5},{5,10},{2,7},{16,21},{21,26},{18,23}} | collective-permute-start | bytes 786440 | tf_op jit(solution)/shard_map/ppermute | solution.py:414
  5.3 12.6 %collective-permute-start.4 = (s32[256,256]{1,0:T(8,128)}, s32[256,256]{1,0:T(8,128)S(1)}, u32[]{:S(2)}, u32[]{:S(2)}) collective-permute-start(s32[256,256]{1,0:T(8,128)} %bitcast.5), channel_id=1, source_target_pairs={{9,5},{14,10},{11,7},{25,21},{30,26},{27,23}} | collective-permute-start | bytes 786440 | tf_op jit(solution)/shard_map/ppermute | solution.py:418
  6.6 11.2 %collective-permute-start.5 = (s32[256,256]{1,0:T(8,128)}, s32[256,256]{1,0:T(8,128)S(1)}, u32[]{:S(2)}, u32[]{:S(2)}) collective-permute-start(s32[256,256]{1,0:T(8,128)} %bitcast.6), channel_id=1, source_target_pairs={{13,5},{2,10},{15,7},{29,21},{18,26},{31,23}} | collective-permute-start | bytes 786440 | tf_op jit(solution)/shard_map/ppermute | solution.py:418
  14.1 7.3 %collective-permute-start.6 = (s32[256,256]{1,0:T(8,128)}, s32[256,256]{1,0:T(8,128)S(1)}, u32[]{:S(2)}, u32[]{:S(2)}) collective-permute-start(s32[256,256]{1,0:T(8,128)} %bitcast.7), channel_id=1, source_target_pairs={{1,5},{6,10},{3,7},{17,21},{22,26},{19,23}} | collective-permute-start | bytes 786440 | tf_op jit(solution)/shard_map/ppermute | solution.py:418
  21.4 1.0 %copy-start = (s32[1,256,256]{2,1,0:T(8,128)S(1)}, s32[1,256,256]{2,1,0:T(8,128)}, u32[]{:S(2)}) copy-start(s32[1,256,256]{2,1,0:T(8,128)} %param.5) | copy-start | bytes 786436
  37.7 0.7 %copy-start.1 = (f32[256,256]{1,0:T(8,128)}, f32[256,256]{1,0:T(8,128)S(1)}, u32[]{:S(2)}) copy-start(f32[256,256]{1,0:T(8,128)S(1)} %get-tuple-element.11.refs_0_) | copy-start | bytes 786436
  38.4 4.6 %collective-permute-start.7 = (f32[256,256]{1,0:T(8,128)S(1)}, f32[256,256]{1,0:T(8,128)S(1)}, u32[]{:S(2)}, u32[]{:S(2)}) collective-permute-start(f32[256,256]{1,0:T(8,128)S(1)} %get-tuple-element.12), channel_id=1, source_target_pairs={{5,9},{10,14},{7,11},{21,25},{26,30},{23,27}} | collective-permute-start | bytes 786440 | tf_op jit(solution)/shard_map/ppermute | solution.py:424
  39.7 6.1 %collective-permute-start.8 = (f32[256,256]{1,0:T(8,128)S(1)}, f32[256,256]{1,0:T(8,128)S(1)}, u32[]{:S(2)}, u32[]{:S(2)}) collective-permute-start(f32[256,256]{1,0:T(8,128)S(1)} %get-tuple-element.13), channel_id=1, source_target_pairs={{5,13},{10,2},{7,15},{21,29},{26,18},{23,31}} | collective-permute-start | bytes 786440 | tf_op jit(solution)/shard_map/ppermute | solution.py:424
  41.1 7.4 %collective-permute-start.9 = (f32[256,256]{1,0:T(8,128)S(1)}, f32[256,256]{1,0:T(8,128)S(1)}, u32[]{:S(2)}, u32[]{:S(2)}) collective-permute-start(f32[256,256]{1,0:T(8,128)S(1)} %get-tuple-element.14), channel_id=1, source_target_pairs={{5,1},{10,6},{7,3},{21,17},{26,22},{23,19}} | collective-permute-start | bytes 786440 | tf_op jit(solution)/shard_map/ppermute | solution.py:424
  43.0 5.4 %copy-start.3 = (f32[256,256]{1,0:T(8,128)}, f32[256,256]{1,0:T(8,128)S(1)}, u32[]{:S(2)}) copy-start(f32[256,256]{1,0:T(8,128)S(1)} %collective-permute-done.7.refs_1_) | copy-start | bytes 786436
  45.9 2.6 %copy-start.4 = (f32[256,256]{1,0:T(8,128)}, f32[256,256]{1,0:T(8,128)S(1)}, u32[]{:S(2)}) copy-start(f32[256,256]{1,0:T(8,128)S(1)} %collective-permute-done.8.refs_2_) | copy-start | bytes 786436
  48.5 0.7 %copy-start.5 = (f32[256,256]{1,0:T(8,128)}, f32[256,256]{1,0:T(8,128)S(1)}, u32[]{:S(2)}) copy-start(f32[256,256]{1,0:T(8,128)S(1)} %collective-permute-done.9.refs_3_) | copy-start | bytes 786436
  52.4 5.4 %collective-permute-start.10 = (f32[128,128]{1,0:T(8,128)}, f32[128,128]{1,0:T(8,128)S(1)}, u32[]{:S(2)}, u32[]{:S(2)}) collective-permute-start(f32[128,128]{1,0:T(8,128)} %get-tuple-element.15), channel_id=1, source_target_pairs={{1,2},{2,3},{5,6},{6,7},{9,10},{10,11},{13,14},{14,15},{17,18},{18... | collective-permute-start | bytes 196616 | tf_op jit(solution)/shard_map/ppermute | solution.py:431
  53.7 7.6 %collective-permute-start.11 = (f32[128,128]{1,0:T(8,128)}, f32[128,128]{1,0:T(8,128)S(1)}, u32[]{:S(2)}, u32[]{:S(2)}) collective-permute-start(f32[128,128]{1,0:T(8,128)} %get-tuple-element.15), channel_id=1, source_target_pairs={{1,3},{5,7},{9,11},{13,15},{17,19},{21,23},{25,27},{29,31}} | collective-permute-start | bytes 196616 | tf_op jit(solution)/shard_map/ppermute | solution.py:431
  57.7 3.5 %copy-start.6 = (f32[128,128]{1,0:T(8,128)}, f32[128,128]{1,0:T(8,128)S(1)}, u32[]{:S(2)}) copy-start(f32[128,128]{1,0:T(8,128)S(1)} %collective-permute-done.10.refs_0_) | copy-start | bytes 196612
  61.3 0.6 copy-start.7

commit v2 on v0

--- a/solution.py
+++ b/solution.py
@@ -1,6 +1,8 @@
 import jax
 import jax.numpy as jnp
 from jax import lax
+from jax.experimental import pallas as pl
+from jax.experimental.pallas import tpu as pltpu
 from jax.sharding import PartitionSpec as P
 
 ITERS = 3
@@ -9,6 +11,12 @@
 
 DIFF = 2.0
 ADV = 0.25
+
+SUB = 8
+LANES = 128
+DEPTH = 2
+MOST_PLANES = 8
+VMEM_BYTES = 16 * 1024 * 1024
 
 
 def with_halo(array, sides, width):
@@ -84,7 +92,7 @@
     return solution
 
 
-def body(state, classes, perm_table, rate_table):
+def spread_body(state, classes, perm_table, rate_table):
     start = state[0]
     perm = lookup(perm_table, classes)
     coarse_ratio = 1.0 / (1.0 + restrict(lookup(rate_table, classes)))
@@ -112,6 +120,479 @@
     return updated[None]
 
 
+def in_vmem(count):
+    return [pl.BlockSpec(memory_space=pltpu.VMEM)] * count
+
+
+def anywhere(count):
+    return [pl.BlockSpec(memory_space=pl.ANY)] * count
+
+
+def in_smem(count):
+    return [pl.BlockSpec(memory_space=pltpu.SMEM)] * count
+
+
+def small_vmem():
+    return pltpu.CompilerParams(vmem_limit_bytes=VMEM_BYTES)
+
+
+def strips_shape(ny, nz, extra=0):
+    return (nz // LANES, ny // SUB + extra, SUB, LANES)
+
+
+def halves_of(plane, halves, sems):
+    return [
+        pltpu.make_async_copy(plane.at[:, pl.ds(h * LANES, LANES)], halves.at[h], sems.at[h])
+        for h in range(halves.shape[0])
+    ]
+
+
+def strip(halves, h, o, strips):
+    return halves[h, pl.ds(o, SUB, stride=strips)]
+
+
+def pairs(coarse_lane, h, transposed):
+    shape = (LANES, LANES)
+    fine = lax.broadcasted_iota(jnp.int32, shape, 1 if transposed else 0) + h * LANES
+    coarse = lax.broadcasted_iota(jnp.int32, shape, 0 if transposed else 1) + coarse_lane * LANES
+    return jnp.where(fine // 2 == coarse, 1.0, 0.0).astype(jnp.bfloat16)
+
+
+def exact_dot(a, ones):
+    total = jnp.zeros((a.shape[0], ones.shape[1]), jnp.float32)
+    parts = []
+    for _ in range(3):
+        part = a.astype(jnp.bfloat16)
+        parts.append(part)
+        a = a - part.astype(jnp.float32)
+    for part in reversed(parts):
+        total = total + jnp.dot(part, ones, preferred_element_type=jnp.float32)
+    return total
+
+
+def restrict_strips(read, halves, strips):
+    rows = [
+        jnp.concatenate([read(h, o) + read(h, o + 1) for o in range(0, strips, 2)], axis=0)
+        for h in range(halves)
+    ]
+    result = []
+    for c in range(halves // 2):
+        tile = exact_dot(rows[2 * c], pairs(c, 2 * c, False))
+        tile = tile + exact_dot(rows[2 * c + 1], pairs(c, 2 * c + 1, False))
+        result.append(0.25 * tile)
+    return result
+
+
+def strips_of_perm(classes, table):
+    ny, nz = classes.shape
+    shape = strips_shape(ny, nz)
+
+    def kernel(values, kinds, out, halves, sems):
+        copies = halves_of(kinds, halves, sems)
+        for copy in copies:
+            copy.start()
+        for h in range(shape[0]):
+            copies[h].wait()
+            for o in range(shape[1]):
+                kind = strip(halves, h, o, shape[1])
+                value = jnp.zeros((SUB, LANES), jnp.float32)
+                for entry in range(table.shape[0]):
+                    value = jnp.where(kind == entry, -ADV * values[entry], value)
+                out[h, o] = value
+
+    return pl.pallas_call(
+        kernel,
+        out_shape=jax.ShapeDtypeStruct(shape, jnp.float32),
+        in_specs=in_smem(1) + anywhere(1),
+        out_specs=in_vmem(1)[0],
+        scratch_shapes=[pltpu.VMEM((shape[0], ny, LANES), jnp.int32),
+                        pltpu.SemaphoreType.DMA((shape[0],))],
+        compiler_params=small_vmem(),
+        name="strips_of_perm",
+    )(table, classes)
+
+
+def strips_of_state(planes):
+    count = len(planes)
+    ny, nz = planes[0].shape
+    halves_count, strips = nz // LANES, ny // SUB
+
+    def kernel(*refs):
+        outs, halves, sems = refs[count:2 * count], refs[2 * count], refs[2 * count + 1]
+        copies = [halves_of(refs[i], halves.at[i], sems.at[i]) for i in range(count)]
+        for row in copies:
+            for copy in row:
+                copy.start()
+        for i in range(count):
+            for h in range(halves_count):
+                copies[i][h].wait()
+                for o in range(strips):
+                    value = strip(halves.at[i], h, o, strips)
+                    outs[i][h, o + 1] = value
+                    if o == 0:
+                        outs[i][h, strips + 1] = pltpu.roll(value, SUB - 1, 0)
+                    if o == strips - 1:
+                        outs[i][h, 0] = pltpu.roll(value, 1, 0)
+
+    return pl.pallas_call(
+        kernel,
+        out_shape=[jax.ShapeDtypeStruct(strips_shape(ny, nz, 2), jnp.float32)] * count,
+        in_specs=anywhere(count),
+        out_specs=in_vmem(count),
+        scratch_shapes=[pltpu.VMEM((count, halves_count, ny, LANES), jnp.float32),
+                        pltpu.SemaphoreType.DMA((count, halves_count))],
+        compiler_params=small_vmem(),
+        name="strips_of_state",
+    )(*planes)
+
+
+def coarse_parts(state, classes, rate_table):
+    ny, nz = state.shape
+    halves_count, strips = nz // LANES, ny // SUB
+    coarse = (nz // (2 * LANES), ny // 2, LANES)
+
+    def kernel(rates, field, kinds, own, ratio, fields_in, kinds_in, sems):
+        copies = halves_of(field, fields_in, sems.at[0]) + halves_of(kinds, kinds_in, sems.at[1])
+        for copy in copies:
+            copy.start()
+        for copy in copies:
+            copy.wait()
+
+        def rate(h, o):
+            kind = strip(kinds_in, h, o, strips)
+            value = jnp.zeros((SUB, LANES), jnp.float32)
+            for entry in range(rate_table.shape[0]):
+                value = jnp.where(kind == entry, rates[entry], value)
+            return value
+
+        for c, tile in enumerate(restrict_strips(rate, halves_count, strips)):
+            ratio[c] = 1.0 / (1.0 + tile)
+        read = lambda h, o: strip(fields_in, h, o, strips)
+        for c, tile in enumerate(restrict_strips(read, halves_count, strips)):
+            own[c] = tile
+
+    return pl.pallas_call(
+        kernel,
+        out_shape=[jax.ShapeDtypeStruct(coarse, jnp.float32)] * 2,
+        in_specs=in_smem(1) + anywhere(2),
+        out_specs=in_vmem(2),
+        scratch_shapes=[pltpu.VMEM((halves_count, ny, LANES), jnp.float32),
+                        pltpu.VMEM((halves_count, ny, LANES), jnp.int32),
+                        pltpu.SemaphoreType.DMA((2, halves_count))],
+        compiler_params=small_vmem(),
+        name="coarse_parts",
+    )(rate_table, state, classes)
+
+
+def gram_steps(g00, g01, g11, g12, g22, h22):
+    a = 1.0 + 6.0 * DIFF
+    b = 6.0 * DIFF
+    g02 = 2.0 * g11 - g00
+    h00, h01, h02 = g01, g11, g12
+    h11, h12 = 0.5 * (g12 + g01), 0.5 * (g22 + g02)
+    rr = g00
+    alpha0 = rr / (a * g00 - b * h00)
+    p, q = 1.0 - a * alpha0, b * alpha0
+    new = p * p * g00 + 2.0 * p * q * g01 + q * q * g11
+    beta = new / rr
+    rr = new
+    e, f = p + beta, q
+    dd = e * e * g00 + 2.0 * e * f * g01 + f * f * g11
+    dmd = e * e * h00 + 2.0 * e * f * h01 + f * f * h11
+    alpha1 = rr / (a * dd - b * dmd)
+    u = p - alpha1 * (a * e - 0.5 * b * f)
+    v = q - alpha1 * (a * f - b * e)
+    w = alpha1 * (0.5 * b) * f
+    new = (u * u * g00 + v * v * g11 + w * w * g22
+           + 2.0 * (u * v * g01 + u * w * g02 + v * w * g12))
+    beta = new / rr
+    rr = new
+    u, v = u + beta * e, v + beta * f
+    dd = (u * u * g00 + v * v * g11 + w * w * g22
+          + 2.0 * (u * v * g01 + u * w * g02 + v * w * g12))
+    dmd = (u * u * h00 + v * v * h11 + w * w * h22
+           + 2.0 * (u * v * h01 + u * w * h02 + v * w * h12))
+    alpha2 = rr / (a * dd - b * dmd)
+    return (alpha0 + alpha1 * e + alpha2 * u, alpha1 * f + alpha2 * v, alpha2 * w)
+
+
+def fine_kernel(planes, halves, strips):
+    def kernel(*refs):
+        x_in = refs[:planes]
+        perm = refs[planes:2 * planes]
+        outs = refs[2 * planes:3 * planes]
+        x_next, r, p1, p2 = refs[3 * planes:]
+        lane = lax.broadcasted_iota(jnp.int32, (DEPTH, SUB, LANES), 2)
+        first_lane, last_lane = lane == 0, lane == LANES - 1
+        zero = jnp.zeros((SUB, LANES), jnp.float32)
+        cells = [(i, h) for i in range(planes) for h in range(halves)]
+
+        def wrap(field):
+            for i, h in cells:
+                field[i, h, 0] = pltpu.roll(field[i, h, strips], 1, 0)
+                field[i, h, strips + 1] = pltpu.roll(field[i, h, 1], SUB - 1, 0)
+
+        def folded(value):
+            return jnp.sum(value, axis=0)
+
+        def total(acc):
+            return jnp.sum(jnp.sum(acc, axis=1, keepdims=True), axis=0, keepdims=True)
+
+        def uppers(row):
+            turned = [pltpu.roll(c, LANES - 1, 2) for c in row]
+            ends = turned[1:] + [jnp.zeros_like(row[0])]
+            return [jnp.where(last_lane, e, t) for t, e in zip(turned, ends)]
+
+        def lowers(row):
+            turned = [pltpu.roll(c, 1, 2) for c in row]
+            ends = [jnp.zeros_like(row[0])] + turned[:-1]
+            return [jnp.where(first_lane, e, t) for t, e in zip(turned, ends)]
+
+        def beside_planes(column):
+            if planes == 4:
+                even, odd = column[0] + column[2], column[1] + column[3]
+                return [odd, even, odd, even]
+            return [column[i - 1] + column[(i + 1) % planes] for i in range(planes)]
+
+        def stencil(field, o):
+            blocks = [[field[i][h, pl.ds(o, DEPTH + 2)] for h in range(halves)]
+                      for i in range(planes)]
+            inner = [[b[1:DEPTH + 1] for b in row] for row in blocks]
+            along_x = [beside_planes([inner[i][h] for i in range(planes)]) for h in range(halves)]
+            for i in range(planes):
+                upper, lower = uppers(inner[i]), lowers(inner[i])
+                for h in range(halves):
+                    b = blocks[i][h]
+                    six = (along_x[h][i] + (b[2:] + b[:DEPTH])) + (upper[h] + lower[h])
+                    yield i, h, inner[i][h], six, upper[h], lower[h]
+
+        def sweep(turn, init):
+            carry = init
+            for o in range(0, strips, DEPTH):
+                carry = turn(o, carry)
+            return carry
+
+        def planes_of(field):
+            return [field.at[i] for i in range(planes)]
+
+        for step in range(FINE):
+            last = step == FINE - 1
+            x = x_in if step == 0 else planes_of(x_next)
+
+            def first_pass(o, g00):
+                for i, h, v, six, upper, lower in stencil(x, o):
+                    slope = perm[i][h, pl.ds(o, DEPTH)] * (upper - lower) - 6.0 * DIFF
+                    value = DIFF * six + slope * v
+                    r[i, h, pl.ds(o + 1, DEPTH)] = value
+                    g00 = g00 + folded(value * value)
+                return g00
+
+            g00 = sweep(first_pass, zero)
+            wrap(r)
+
+            def second_pass(o, carry):
+                g01, g11 = carry
+                for i, h, v, six, _, _ in stencil(planes_of(r), o):
+                    value = six * (1.0 / 6.0)
+                    p1[i, h, pl.ds(o + 1, DEPTH)] = value
+                    g01 = g01 + folded(value * v)
+                    g11 = g11 + folded(value * value)
+                return g01, g11
+
+            g01, g11 = sweep(second_pass, (zero, zero))
+            wrap(p1)
+
+            def third_pass(o, carry):
+                g12, g22 = carry
+                for i, h, v, six, _, _ in stencil(planes_of(p1), o):
+                    value = six * (1.0 / 3.0) - r[i, h, pl.ds(o + 1, DEPTH)]
+                    p2[i, h, pl.ds(o + 1, DEPTH)] = value
+                    g12 = g12 + folded(value * v)
+                    g22 = g22 + folded(value * value)
+                return g12, g22
+
+            g12, g22 = sweep(third_pass, (zero, zero))
+            wrap(p2)
+
+            def fourth_pass(o, h22):
+                rows = []
+                for i in range(planes):
+                    blocks = [p2[i, h, pl.ds(o + 1, DEPTH + 1)] for h in range(halves)]
+                    inner = [b[:DEPTH] for b in blocks]
+                    rows.append(inner)
+                    upper = uppers(inner)
+                    for h in range(halves):
+                        h22 = h22 + folded(inner[h] * (blocks[h][1:] + upper[h]))
+                for h in range(halves):
+                    if planes == 4:
+                        h22 = h22 + folded((rows[0][h] + rows[2][h]) * (rows[1][h] + rows[3][h]))
+                    else:
+                        for i in range(planes):
+                            h22 = h22 + folded(rows[i][h] * rows[(i + 1) % planes][h])
+                return h22
+
+            h22 = sweep(fourth_pass, zero)
+            weights = gram_steps(
+                total(g00), total(g01), total(g11), total(g12), total(g22),
+                total(h22) * (1.0 / 3.0))
+            c0, c1, c2 = (jnp.broadcast_to(c, (DEPTH, SUB, LANES)) for c in weights)
+
+            def last_pass(o, carry):
+                for i, h in cells:
+                    at = pl.ds(o + 1, DEPTH)
+                    value = (x[i][h, at] + c0 * r[i, h, at]) + (c1 * p1[i, h, at] + c2 * p2[i, h, at])
+                    if last:
+                        outs[i][h, pl.ds(o, DEPTH)] = value
+                    else:
+                        x_next[i, h, at] = value
+                return carry
+
+            sweep(last_pass, 0)
+            if not last:
+                wrap(x_next)
+
+    return kernel
+
+
+def fine_steps(state_strips, perm_strips):
+    planes = len(state_strips)
+    halves, strips = perm_strips[0].shape[:2]
+    field = pltpu.VMEM((planes,) + state_strips[0].shape, jnp.float32)
+    return pl.pallas_call(
+        fine_kernel(planes, halves, strips),
+        out_shape=[jax.ShapeDtypeStruct(perm_strips[0].shape, jnp.float32)] * planes,
+        in_specs=in_vmem(2 * planes),
+        out_specs=in_vmem(planes),
+        scratch_shapes=[field] * 4,
+        compiler_params=small_vmem(),
+        name="fine_steps",
+    )(*state_strips, *perm_strips)
+
+
+def chosen(which, candidates, h, o):
+    value = candidates[0][h, o]
+    for k in range(1, len(candidates)):
+        value = jnp.where(which == k, candidates[k][h, o], value)
+    return value
+
+
+def coarse_change(which, candidates, own):
+    count = len(candidates)
+    halves, strips = candidates[0].shape[:2]
+
+    def kernel(choice, *refs):
+        ends, own_ref, out = refs[:count], refs[count], refs[count + 1]
+        read = lambda h, o: chosen(choice[0], ends, h, o)
+        for c, tile in enumerate(restrict_strips(read, halves, strips)):
+            out[c] = tile - own_ref[c]
+
+    return pl.pallas_call(
+        kernel,
+        out_shape=jax.ShapeDtypeStruct(own.shape, jnp.float32),
+        in_specs=in_smem(1) + in_vmem(count + 1),
+        out_specs=in_vmem(1)[0],
+        compiler_params=small_vmem(),
+        name="coarse_change",
+    )(which, *candidates, own)
+
+
+def corrected(choice, candidates, ratio, changes, start):
+    ny, nz = start.shape
+    count, turns = len(candidates), len(changes)
+    halves_count, strips = nz // LANES, ny // SUB
+
+    def kernel(which, *refs):
+        ends, share = refs[:count], refs[count]
+        others = refs[count + 1:count + 1 + turns]
+        begin, out, halves, sems = refs[count + 1 + turns:]
+
+        @pl.when(which[1] == 0)
+        def _():
+            copy = pltpu.make_async_copy(begin, out, sems.at[0])
+            copy.start()
+            copy.wait()
+
+        @pl.when(which[1] != 0)
+        def _():
+            copies = []
+            for c in range(halves_count // 2):
+                drift = jnp.zeros((ny // 2, LANES), jnp.float32)
+                for k in reversed(range(turns)):
+                    drift = share[c] * (drift + others[k][c])
+                for h in (2 * c, 2 * c + 1):
+                    wide = exact_dot(drift, pairs(c, h, True))
+                    for o in range(strips):
+                        first = (o // 2) * SUB
+                        value = chosen(which[0], ends, h, o) + wide[first:first + SUB]
+                        halves[h, pl.ds(o, SUB, stride=strips)] = value
+                    copy = pltpu.make_async_copy(
+                        halves.at[h], out.at[:, pl.ds(h * LANES, LANES)], sems.at[h])
+                    copy.start()
+                    copies.append(copy)
+            for copy in copies:
+                copy.wait()
+
+    return pl.pallas_call(
+        kernel,
+        out_shape=jax.ShapeDtypeStruct((ny, nz), jnp.float32),
+        in_specs=in_smem(1) + in_vmem(count + 1 + turns) + anywhere(1),
+        out_specs=anywhere(1)[0],
+        scratch_shapes=[pltpu.VMEM((halves_count, ny, LANES), jnp.float32),
+                        pltpu.SemaphoreType.DMA((halves_count,))],
+        compiler_params=small_vmem(),
+        name="corrected",
+    )(choice, *candidates, ratio, *changes, start)
+
+
+def gathered_body(state, classes, perm_table, rate_table):
+    start = state[0, 0]
+    kinds = classes[0]
+    width, slices = lax.axis_size("space"), lax.axis_size("tm")
+    axes = ("space", "tm")
+    place = lambda s, t: (s % width) * slices + t
+    site = lambda j: (width // 2 - 1 + j % 2) % width
+    used = range(slices - 1)
+    far_first = sorted(range(1, width), key=lambda k: -min(k, width - k))
+
+    def to_sites(array, k, late):
+        return lax.ppermute(array, axes, [
+            (place(site(j) + k, j + late), place(site(j), j + 1)) for j in used])
+
+    def from_sites(array, k):
+        return lax.ppermute(array, axes, [
+            (place(site(j), j + 1), place(site(j) + k, j + 1)) for j in used])
+
+    state_planes = {k: to_sites(start, k, 0) for k in far_first + [0]}
+    perm = strips_of_perm(kinds, perm_table)
+    perm_strips = {k: to_sites(perm, k, 1) for k in far_first}
+    perm_strips[0] = perm
+    own, ratio = coarse_parts(start, kinds, rate_table)
+    state_strips = strips_of_state([state_planes[k] for k in range(width)])
+    ends = fine_steps(state_strips, [perm_strips[k] for k in range(width)])
+    landed = {k: from_sites(ends[k], k) for k in far_first}
+    landed[0] = ends[0]
+    candidates = [landed[k] for k in range(width)]
+    turn = lax.axis_index("tm")
+    which = (lax.axis_index("space") - site(turn - 1)) % width
+    choice = jnp.stack([which, turn]).astype(jnp.int32)
+    change = coarse_change(choice, candidates, own)
+    changes = [
+        lax.ppermute(change, "tm", [(i, i + k) for i in range(1, slices - k)])
+        for k in range(1, slices - 1)
+    ]
+    return corrected(choice, candidates, ratio, changes, start)[None, None]
+
+
+def body(state, classes, perm_table, rate_table):
+    width = lax.axis_size("space")
+    one_plane = state.shape[:2] == (1, 1) and classes.shape[0] == 1
+    ny, nz = state.shape[2:]
+    tiles = ny % (2 * DEPTH * SUB) == 0 and nz % (2 * LANES) == 0
+    if one_plane and tiles and 2 < width <= MOST_PLANES and lax.axis_size("tm") > 2:
+        return gathered_body(state, classes, perm_table, rate_table)
+    return spread_body(state, classes, perm_table, rate_table)
+
+
 def solution(mesh):
     placed = (
         P(("groups", "tm"), "space", None, None),

time: 339 us -> 47.9 us (0.14); the launches traced: 334 us -> 47.5 us
  blocking collectives: 90.9 us -> 0 us
  local copies, waits for them, and re-layouts: 83.3 us -> 1.59 us
  waiting for transfers between devices: 79.1 us -> 19.8 us
  other arithmetic: 49.6 us -> 0.08 us
  between operations: 13.3 us -> 0.26 us
  Pallas kernels: 0 us -> 10.1 us
    psum x10 -> x0, blocking collectives: 90.9 us -> none  [the longest x6 58.3 us: squares(): return lax.psum(jnp.sum(residual * residual), 'space')]
    ppermute x20 -> x12, waiting for transfers between devices: 79.1 us -> 19.8 us  [the longest x7 9.27 us: to_sites(): lax.ppermute(array, axes, [(place(site(j) + k, j + late), place(site(j),...]
    reshape x3 -> x0, local copies, waits for them, and re-layouts: 54.3 us -> none  [restrict(): return field.reshape(cx, ny // 2, 2, nz // 2, 2).mean(axis=(2, 4))]
    reduce_sum x14 -> x0, other arithmetic: 39.9 us -> none  [the longest x4 32 us: restrict(): return field.reshape(cx, ny // 2, 2, nz // 2, 2).mean(axis=(2, 4))]
    another operation x1 -> x0, local copies, waits for them, and re-layouts: 18.9 us -> none  [restrict(): return field.reshape(cx, ny // 2, 2, nz // 2, 2).mean(axis=(2, 4))]
    pallas_call x0 -> x6, Pallas kernels: none -> 10.1 us  [the longest x1 5.05 us: fine_steps(): pl.pallas_call(fine_kernel(planes, halves, strips), out_shape=[jax.ShapeD...]
    sub x4 -> x0, other arithmetic: 6.74 us -> none  [the longest x2 5.81 us: fine_step(): residual = rhs - operate(solution)]
    slice x26 -> x0, local copies, waits for them, and re-layouts: 5.01 us -> none  [the longest x2 2.94 us: lookup(): values = jnp.where(classes == entry, table[entry], values)]
  transfers between devices with their start and end apart: 20 -> 12, of which waited for: 14 -> 8; matrix products, arithmetic and copies ran while one was open for 23% -> 0% of each run, Pallas kernels for 0% -> 6%
where the time goes in v2:
time: 47.9 us; the launch traced here: 47.5 us
  waiting for transfers between devices  19.8 us (41%)
  starting transfers between devices  15.7 us (33%)
  Pallas kernels  10.1 us (21%)
  local copies, waits for them, and re-layouts  1.59 us (3%)
    ppermute x7, waiting for transfers between devices, to_sites(): lax.ppermute(array, axes, [(place(site(j) + k, j + late), place(site(j),...  9.27 us
    ppermute x7, starting transfers between devices, to_sites(): lax.ppermute(array, axes, [(place(site(j) + k, j + late), place(site(j),...  9.15 us
    ppermute x2, waiting for transfers between devices, gathered_body(): lax.ppermute(change, 'tm', [(i, i + k) for i in range(1, slices - k)])  6.42 us
    pallas_call x1, Pallas kernels, fine_steps(): pl.pallas_call(fine_kernel(planes, halves, strips), out_shape=[jax.ShapeD...  5.05 us
    ppermute x3, waiting for transfers between devices, from_sites(): lax.ppermute(array, axes, [(place(site(j), j + 1), place(site(j) + k, j +...  4.15 us
    ppermute x3, starting transfers between devices, from_sites(): lax.ppermute(array, axes, [(place(site(j), j + 1), place(site(j) + k, j +...  3.92 us
    ppermute x2, starting transfers between devices, gathered_body(): lax.ppermute(change, 'tm', [(i, i + k) for i in range(1, slices - k)])  2.58 us
    unnamed x10, local copies, waits for them, and re-layouts  1.59 us
  transfers between devices with their start and end apart: 12, of which 8 were waited for; matrix products, arithmetic and copies ran while one was open for 0% of the time, Pallas kernels for 6%

profile of v2, /device:TPU:11, one launch (start us, length us, event | category | flops | bytes accessed | tf_op | source)
XLA Modules:
  0.0 47.5 jit_solution(6437499768331555345)
XLA Ops:
  0.0 0.0 copy-start.3
  0.0 1.4 %collective-permute-start = (f32[256,256]{1,0:T(8,128)}, f32[256,256]{1,0:T(8,128)S(1)}, u32[]{:S(2)}, u32[]{:S(2)}) collective-permute-start(f32[256,256]{1,0:T(8,128)} %bitcast.7), channel_id=1, source_target_pairs={{4,5},{9,10},{6,7},{20,21},{25,26},{22,23}} | collective-permute-start | bytes 786440 | tf_op jit(solution)/shard_map/ppermute | solution.py:558
  1.4 1.3 %collective-permute-start.1 = (f32[256,256]{1,0:T(8,128)}, f32[256,256]{1,0:T(8,128)S(1)}, u32[]{:S(2)}, u32[]{:S(2)}) collective-permute-start(f32[256,256]{1,0:T(8,128)} %bitcast.8), channel_id=1, source_target_pairs={{8,5},{13,10},{10,7},{24,21},{29,26},{26,23}} | collective-permute-start | bytes 786440 | tf_op jit(solution)/shard_map/ppermute | solution.py:558
  2.7 1.3 %collective-permute-start.2 = (f32[256,256]{1,0:T(8,128)}, f32[256,256]{1,0:T(8,128)S(1)}, u32[]{:S(2)}, u32[]{:S(2)}) collective-permute-start(f32[256,256]{1,0:T(8,128)} %bitcast.9), channel_id=1, source_target_pairs={{12,5},{1,10},{14,7},{28,21},{17,26},{30,23}} | collective-permute-start | bytes 786440 | tf_op jit(solution)/shard_map/ppermute | solution.py:558
  4.0 1.3 %collective-permute-start.3 = (f32[256,256]{1,0:T(8,128)}, f32[256,256]{1,0:T(8,128)S(1)}, u32[]{:S(2)}, u32[]{:S(2)}) collective-permute-start(f32[256,256]{1,0:T(8,128)} %bitcast.10), channel_id=1, source_target_pairs={{0,5},{5,10},{2,7},{16,21},{21,26},{18,23}} | collective-permute-start | bytes 786440 | tf_op jit(solution)/shard_map/ppermute | solution.py:558
  5.3 0.0 copy-done.3
  5.3 0.0 copy-start
  5.3 0.9 %copy-done = s32[1,256,256]{2,1,0:T(8,128)S(1)} copy-done((s32[1,256,256]{2,1,0:T(8,128)S(1)}, s32[1,256,256]{2,1,0:T(8,128)}, u32[]{:S(2)}) %copy-start) | copy-done | bytes 262168
  6.3 0.8 %strips_of_perm.1.refs_4_ = f32[2,32,8,128]{3,2,1,0:T(8,128)S(1)} custom-call(f32[4]{0:T(128)S(1)} %copy-done.3, s32[256,256]{1,0:T(8,128)S(1)} %bitcast.5), custom_call_target="tpu_custom_call" | custom-call | tf_op jit(solution)/shard_map/strips_of_perm/pallas_call | solution.py:203
  7.1 1.3 %collective-permute-start.4 = (f32[2,32,8,128]{3,2,1,0:T(8,128)S(1)}, f32[2,32,8,128]{3,2,1,0:T(8,128)S(1)}, u32[]{:S(2)}, u32[]{:S(2)}) collective-permute-start(f32[2,32,8,128]{3,2,1,0:T(8,128)S(1)} %strips_of_perm.1.refs_4_), channel_id=1, source_target_pairs={{9,5},{14,10},{11,7},{25,21},{30,26},{27,23}} | collective-permute-start | bytes 786440 | tf_op jit(solution)/shard_map/ppermute | solution.py:558
  8.4 0.0 collective-permute-done.refs_0_
  8.4 1.3 %collective-permute-start.5 = (f32[2,32,8,128]{3,2,1,0:T(8,128)S(1)}, f32[2,32,8,128]{3,2,1,0:T(8,128)S(1)}, u32[]{:S(2)}, u32[]{:S(2)}) collective-permute-start(f32[2,32,8,128]{3,2,1,0:T(8,128)S(1)} %strips_of_perm.1.refs_4_), channel_id=1, source_target_pairs={{13,5},{2,10},{15,7},{29,21},{18,26},{31,23}} | collective-permute-start | bytes 786440 | tf_op jit(solution)/shard_map/ppermute | solution.py:558
  9.7 3.1 %collective-permute-done.1.refs_1_ = f32[256,256]{1,0:T(8,128)S(1)} collective-permute-done((f32[256,256]{1,0:T(8,128)}, f32[256,256]{1,0:T(8,128)S(1)}, u32[]{:S(2)}, u32[]{:S(2)}) %collective-permute-start.1) | collective-permute-done | bytes 262176 | tf_op jit(solution)/shard_map/ppermute | solution.py:558
  12.8 1.3 %collective-permute-start.6 = (f32[2,32,8,128]{3,2,1,0:T(8,128)S(1)}, f32[2,32,8,128]{3,2,1,0:T(8,128)S(1)}, u32[]{:S(2)}, u32[]{:S(2)}) collective-permute-start(f32[2,32,8,128]{3,2,1,0:T(8,128)S(1)} %strips_of_perm.1.refs_4_), channel_id=1, source_target_pairs={{1,5},{6,10},{3,7},{17,21},{22,26},{19,23}} | collective-permute-start | bytes 786440 | tf_op jit(solution)/shard_map/ppermute | solution.py:558
  14.1 0.0 collective-permute-done.2.refs_2_
  14.1 0.0 collective-permute-done.3.refs_3_
  14.1 0.8 %strips_of_state.1 = (f32[2,34,8,128]{3,2,1,0:T(8,128)S(1)}, f32[2,34,8,128]{3,2,1,0:T(8,128)S(1)}, f32[2,34,8,128]{3,2,1,0:T(8,128)S(1)}, f32[2,34,8,128]{3,2,1,0:T(8,128)S(1)}) custom-call(f32[256,256]{1,0:T(8,128)S(1)} %collective-permute-done.refs_0_, f32[256,256]{1,0:T(8,128)S(1)} %collective-permute-done.1.refs_1_, ...), custom_call_target="tpu_custom_call" | custom-call | tf_op jit(solution)/shard_map/strips_of_state/pallas_call | solution.py:237
  15.0 2.1 %collective-permute-done.4.refs_5_ = f32[2,32,8,128]{3,2,1,0:T(8,128)S(1)} collective-permute-done((f32[2,32,8,128]{3,2,1,0:T(8,128)S(1)}, f32[2,32,8,128]{3,2,1,0:T(8,128)S(1)}, u32[]{:S(2)}, u32[]{:S(2)}) %collective-permute-start.4) | collective-permute-done | bytes 262176 | tf_op jit(solution)/shard_map/ppermute | solution.py:558
  17.0 1.6 %collective-permute-done.5.refs_6_ = f32[2,32,8,128]{3,2,1,0:T(8,128)S(1)} collective-permute-done((f32[2,32,8,128]{3,2,1,0:T(8,128)S(1)}, f32[2,32,8,128]{3,2,1,0:T(8,128)S(1)}, u32[]{:S(2)}, u32[]{:S(2)}) %collective-permute-start.5) | collective-permute-done | bytes 262176 | tf_op jit(solution)/shard_map/ppermute | solution.py:558
  18.7 2.4 %collective-permute-done.6.refs_7_ = f32[2,32,8,128]{3,2,1,0:T(8,128)S(1)} collective-permute-done((f32[2,32,8,128]{3,2,1,0:T(8,128)S(1)}, f32[2,32,8,128]{3,2,1,0:T(8,128)S(1)}, u32[]{:S(2)}, u32[]{:S(2)}) %collective-permute-start.6) | collective-permute-done | bytes 262176 | tf_op jit(solution)/shard_map/ppermute | solution.py:558
  21.1 0.0 copy-start.1
  21.1 0.0 copy-start.2
  21.1 5.0 %fine_steps.1 = (f32[2,32,8,128]{3,2,1,0:T(8,128)S(1)}, f32[2,32,8,128]{3,2,1,0:T(8,128)S(1)}, f32[2,32,8,128]{3,2,1,0:T(8,128)S(1)}, f32[2,32,8,128]{3,2,1,0:T(8,128)S(1)}) custom-call(f32[2,34,8,128]{3,2,1,0:T(8,128)S(1)} %get-tuple-element.15.refs_0_, f32[2,34,8,128]{3,2,1,0:T(8,128)S(1)} %get-tuple-element.16.refs_1_, ...), custom_call_target="tpu_custom_call" | custom-call | tf_op jit(solution)/shard_map/fine_steps/pallas_call | solution.py:461
  26.1 1.3 %collective-permute-start.7 = (f32[2,32,8,128]{3,2,1,0:T(8,128)S(1)}, f32[2,32,8,128]{3,2,1,0:T(8,128)S(1)}, u32[]{:S(2)}, u32[]{:S(2)}) collective-permute-start(f32[2,32,8,128]{3,2,1,0:T(8,128)S(1)} %get-tuple-element.20), channel_id=1, source_target_pairs={{5,9},{10,14},{7,11},{21,25},{26,30},{23,27}} | collective-permute-start | bytes 786440 | tf_op jit(solution)/shard_map/ppermute | solution.py:562
  27.5 1.3 %collective-permute-start.8 = (f32[2,32,8,128]{3,2,1,0:T(8,128)S(1)}, f32[2,32,8,128]{3,2,1,0:T(8,128)S(1)}, u32[]{:S(2)}, u32[]{:S(2)}) collective-permute-start(f32[2,32,8,128]{3,2,1,0:T(8,128)S(1)} %get-tuple-element.21), channel_id=1, source_target_pairs={{5,13},{10,2},{7,15},{21,29},{26,18},{23,31}} | collective-permute-start | bytes 786440 | tf_op jit(solution)/shard_map/ppermute | solution.py:562
  28.8 1.3 %collective-permute-start.9 = (f32[2,32,8,128]{3,2,1,0:T(8,128)S(1)}, f32[2,32,8,128]{3,2,1,0:T(8,128)S(1)}, u32[]{:S(2)}, u32[]{:S(2)}) collective-permute-start(f32[2,32,8,128]{3,2,1,0:T(8,128)S(1)} %get-tuple-element.22), channel_id=1, source_target_pairs={{5,1},{10,6},{7,3},{21,17},{26,22},{23,19}} | collective-permute-start | bytes 786440 | tf_op jit(solution)/shard_map/ppermute | solution.py:562
  30.1 0.0 copy-start.4
  30.1 0.0 copy-done.1
  30.2 0.0 copy-done.2
  30.2 0.6 %copy-done.4 = f32[4]{0:T(128)S(1)} copy-done((f32[4]{0:T(128)S(1)}, f32[4]{0:T(128)}, u32[]{:S(2)}) %copy-start.4) | copy-done | bytes 40
  30.8 1.1 %coarse_parts.1 = (f32[1,128,128]{2,1,0:T(8,128)S(1)}, f32[1,128,128]{2,1,0:T(8,128)S(1)}) custom-call(f32[4]{0:T(128)S(1)} %copy-done.4, f32[256,256]{1,0:T(8,128)S(1)} %bitcast.11, s32[256,256]{1,0:T(8,128)S(1)} %bitcast.6), custom_call_target="tpu_custom_call" | custom-call | tf_op jit(solution)/shard_map/coarse_parts/pallas_call | solution.py:274
  32.0 0.1 pad_add_fusion.choice.which
  32.0 0.0 collective-permute-done.7.refs_1_
  32.0 1.6 %collective-permute-done.8.refs_2_ = f32[2,32,8,128]{3,2,1,0:T(8,128)S(1)} collective-permute-done((f32[2,32,8,128]{3,2,1,0:T(8,128)S(1)}, f32[2,32,8,128]{3,2,1,0:T(8,128)S(1)}, u32[]{:S(2)}, u32[]{:S(2)}) %collective-permute-start.8) | collective-permute-done | bytes 262176 | tf_op jit(solution)/shard_map/ppermute | solution.py:562
  33.6 2.6 %collective-permute-done.9.refs_3_ = f32[2,32,8,128]{3,2,1,0:T(8,128)S(1)} collective-permute-done((f32[2,32,8,128]{3,2,1,0:T(8,128)S(1)}, f32[2,32,8,128]{3,2,1,0:T(8,128)S(1)}, u32[]{:S(2)}, u32[]{:S(2)}) %collective-permute-start.9) | collective-permute-done | bytes 262176 | tf_op jit(solution)/shard_map/ppermute | solution.py:562
  36.2 0.8 %coarse_change.1 = f32[1,128,128]{2,1,0:T(8,128)S(1)} custom-call(s32[2]{0:T(128)S(1)} %pad_add_fusion.choice.which, f32[2,32,8,128]{3,2,1,0:T(8,128)S(1)} %get-tuple-element.19.refs_0_, f32[2,32,8,128]{3,2,1,0:T(8,128)S(1)} %collective-permute-done.7.refs_1_, f32[2,32,8,128]{3,2,1,0:T(8,128)S(1)} %collective-permute-done.8.refs_2_, ...), custom_call_target="tpu_custom_call" | custom-call | tf_op jit(solution)/shard_map/coarse_change/pallas_call | solution.py:489
  37.0 1.3 %collective-permute-start.10 = (f32[1,128,128]{2,1,0:T(8,128)S(1)}, f32[1,128,128]{2,1,0:T(8,128)S(1)}, u32[]{:S(2)}, u32[]{:S(2)}) collective-permute-start(f32[1,128,128]{2,1,0:T(8,128)S(1)} %coarse_change.1), channel_id=1, source_target_pairs={{1,2},{2,3},{5,6},{6,7},{9,10},{10,11},{13,14},{14,15},{17,18},{18... | collective-permute-start | bytes 196616 | tf_op jit(solution)/shard_map/ppermute | solution.py:580
  38.3 1.3 %collective-permute-start.11 = (f32[1,128,128]{2,1,0:T(8,128)S(1)}, f32[1,128,128]{2,1,0:T(8,128)S(1)}, u32[]{:S(2)}, u32[]{:S(2)}) collective-permute-start(f32[1,128,128]{2,1,0:T(8,128)S(1)} %coarse_change.1), channel_id=1, source_target_pairs={{1,3},{5,7},{9,11},{13,15},{17,19},{21,23},{25,27},{29,31}} | collective-permute-start | bytes 196616 | tf_op jit(solution)/shard_map/ppermute | solution.py:580
  39.6 2.9 %collective-permute-done.10.refs_5_ = f32[1,128,128]{2,1,0:T(8,128)S(1)} collective-permute-done((f32[1,128,128]{2,1,0:T(8,128)S(1)}, f32[1,128,128]{2,1,0:T(8,128)S(1)}, u32[]{:S(2)}, u32[]{:S(2)}) %collective-permute-start.10) | collective-permute-done | bytes 65568 | tf_op jit(solution)/shard_map/ppermute | solution.py:580
  42.4 3.5 %collective-permute-done.11.refs_6_ = f32[1,128,128]{2,1,0:T(8,128)S(1)} collective-permute-done((f32[1,128,128]{2,1,0:T(8,128)S(1)}, f32[1,128,128]{2,1,0:T(8,128)S(1)}, u32[]{:S(2)}, u32[]{:S(2)}) %collective-permute-start.11) | collective-permute-done | bytes 65568 | tf_op jit(solution)/shard_map/ppermute | solution.py:580
  46.0 1.6 %corrected.1 = f32[256,256]{1,0:T(8,128)} custom-call(s32[2]{0:T(128)S(1)} %pad_add_fusion.choice.which, f32[2,32,8,128]{3,2,1,0:T(8,128)S(1)} %get-tuple-element.19.refs_0_, f32[2,32,8,128]{3,2,1,0:T(8,128)S(1)} %collective-permute-done.7.refs_1_, f32[2,32,8,128]{3,2,1,0:T(8,128)S(1)} %collective-permute-done.8.refs_2_, ...), custom_call_target="tpu_custom_call" | custom-call | tf_op jit(solution)/shard_map/corrected/pallas_call | solution.py:535
Async XLA Ops:
  0.0 5.3 %copy-start.3 = (f32[4]{0:T(128)S(1)}, f32[4]{0:T(128)}, u32[]{:S(2)}) copy-start(f32[4]{0:T(128)} %values.1) | copy-start | bytes 52
  0.0 8.4 %collective-permute-start = (f32[256,256]{1,0:T(8,128)}, f32[256,256]{1,0:T(8,128)S(1)}, u32[]{:S(2)}, u32[]{:S(2)}) collective-permute-start(f32[256,256]{1,0:T(8,128)} %bitcast.7), channel_id=1, source_target_pairs={{4,5},{9,10},{6,7},{20,21},{25,26},{22,23}} | collective-permute-start | bytes 786440 | tf_op jit(solution)/shard_map/ppermute | solution.py:558
  1.4 11.4 %collective-permute-start.1 = (f32[256,256]{1,0:T(8,128)}, f32[256,256]{1,0:T(8,128)S(1)}, u32[]{:S(2)}, u32[]{:S(2)}) collective-permute-start(f32[256,256]{1,0:T(8,128)} %bitcast.8), channel_id=1, source_target_pairs={{8,5},{13,10},{10,7},{24,21},{29,26},{26,23}} | collective-permute-start | bytes 786440 | tf_op jit(solution)/shard_map/ppermute | solution.py:558
  2.7 11.4 %collective-permute-start.2 = (f32[256,256]{1,0:T(8,128)}, f32[256,256]{1,0:T(8,128)S(1)}, u32[]{:S(2)}, u32[]{:S(2)}) collective-permute-start(f32[256,256]{1,0:T(8,128)} %bitcast.9), channel_id=1, source_target_pairs={{12,5},{1,10},{14,7},{28,21},{17,26},{30,23}} | collective-permute-start | bytes 786440 | tf_op jit(solution)/shard_map/ppermute | solution.py:558
  4.0 10.1 %collective-permute-start.3 = (f32[256,256]{1,0:T(8,128)}, f32[256,256]{1,0:T(8,128)S(1)}, u32[]{:S(2)}, u32[]{:S(2)}) collective-permute-start(f32[256,256]{1,0:T(8,128)} %bitcast.10), channel_id=1, source_target_pairs={{0,5},{5,10},{2,7},{16,21},{21,26},{18,23}} | collective-permute-start | bytes 786440 | tf_op jit(solution)/shard_map/ppermute | solution.py:558
  5.3 1.0 %copy-start = (s32[1,256,256]{2,1,0:T(8,128)S(1)}, s32[1,256,256]{2,1,0:T(8,128)}, u32[]{:S(2)}) copy-start(s32[1,256,256]{2,1,0:T(8,128)} %param.5) | copy-start | bytes 786436
  7.1 10.0 %collective-permute-start.4 = (f32[2,32,8,128]{3,2,1,0:T(8,128)S(1)}, f32[2,32,8,128]{3,2,1,0:T(8,128)S(1)}, u32[]{:S(2)}, u32[]{:S(2)}) collective-permute-start(f32[2,32,8,128]{3,2,1,0:T(8,128)S(1)} %strips_of_perm.1.refs_4_), channel_id=1, source_target_pairs={{9,5},{14,10},{11,7},{25,21},{30,26},{27,23}} | collective-permute-start | bytes 786440 | tf_op jit(solution)/shard_map/ppermute | solution.py:558
  8.4 10.3 %collective-permute-start.5 = (f32[2,32,8,128]{3,2,1,0:T(8,128)S(1)}, f32[2,32,8,128]{3,2,1,0:T(8,128)S(1)}, u32[]{:S(2)}, u32[]{:S(2)}) collective-permute-start(f32[2,32,8,128]{3,2,1,0:T(8,128)S(1)} %strips_of_perm.1.refs_4_), channel_id=1, source_target_pairs={{13,5},{2,10},{15,7},{29,21},{18,26},{31,23}} | collective-permute-start | bytes 786440 | tf_op jit(solution)/shard_map/ppermute | solution.py:558
  12.8 8.3 %collective-permute-start.6 = (f32[2,32,8,128]{3,2,1,0:T(8,128)S(1)}, f32[2,32,8,128]{3,2,1,0:T(8,128)S(1)}, u32[]{:S(2)}, u32[]{:S(2)}) collective-permute-start(f32[2,32,8,128]{3,2,1,0:T(8,128)S(1)} %strips_of_perm.1.refs_4_), channel_id=1, source_target_pairs={{1,5},{6,10},{3,7},{17,21},{22,26},{19,23}} | collective-permute-start | bytes 786440 | tf_op jit(solution)/shard_map/ppermute | solution.py:558
  21.1 9.1 %copy-start.1 = (s32[1,256,256]{2,1,0:T(8,128)S(1)}, s32[1,256,256]{2,1,0:T(8,128)}, u32[]{:S(2)}) copy-start(s32[1,256,256]{2,1,0:T(8,128)} %param.5) | copy-start | bytes 786436
  21.1 9.1 %copy-start.2 = (f32[1,1,256,256]{3,2,1,0:T(8,128)S(1)}, f32[1,1,256,256]{3,2,1,0:T(8,128)}, u32[]{:S(2)}) copy-start(f32[1,1,256,256]{3,2,1,0:T(8,128)} %param.4) | copy-start | bytes 786436
  26.1 5.9 %collective-permute-start.7 = (f32[2,32,8,128]{3,2,1,0:T(8,128)S(1)}, f32[2,32,8,128]{3,2,1,0:T(8,128)S(1)}, u32[]{:S(2)}, u32[]{:S(2)}) collective-permute-start(f32[2,32,8,128]{3,2,1,0:T(8,128)S(1)} %get-tuple-element.20), channel_id=1, source_target_pairs={{5,9},{10,14},{7,11},{21,25},{26,30},{23,27}} | collective-permute-start | bytes 786440 | tf_op jit(solution)/shard_map/ppermute | solution.py:562
  27.5 6.1 %collective-permute-start.8 = (f32[2,32,8,128]{3,2,1,0:T(8,128)S(1)}, f32[2,32,8,128]{3,2,1,0:T(8,128)S(1)}, u32[]{:S(2)}, u32[]{:S(2)}) collective-permute-start(f32[2,32,8,128]{3,2,1,0:T(8,128)S(1)} %get-tuple-element.21), channel_id=1, source_target_pairs={{5,13},{10,2},{7,15},{21,29},{26,18},{23,31}} | collective-permute-start | bytes 786440 | tf_op jit(solution)/shard_map/ppermute | solution.py:562
  28.8 7.4 %collective-permute-start.9 = (f32[2,32,8,128]{3,2,1,0:T(8,128)S(1)}, f32[2,32,8,128]{3,2,1,0:T(8,128)S(1)}, u32[]{:S(2)}, u32[]{:S(2)}) collective-permute-start(f32[2,32,8,128]{3,2,1,0:T(8,128)S(1)} %get-tuple-element.22), channel_id=1, source_target_pairs={{5,1},{10,6},{7,3},{21,17},{26,22},{23,19}} | collective-permute-start | bytes 786440 | tf_op jit(solution)/shard_map/ppermute | solution.py:562
  30.1 0.7 %copy-start.4 = (f32[4]{0:T(128)S(1)}, f32[4]{0:T(128)}, u32[]{:S(2)}) copy-start(f32[4]{0:T(128)} %rates.1) | copy-start | bytes 52
  37.0 5.5 %collective-permute-start.10 = (f32[1,128,128]{2,1,0:T(8,128)S(1)}, f32[1,128,128]{2,1,0:T(8,128)S(1)}, u32[]{:S(2)}, u32[]{:S(2)}) collective-permute-start(f32[1,128,128]{2,1,0:T(8,128)S(1)} %coarse_change.1), channel_id=1, source_target_pairs={{1,2},{2,3},{5,6},{6,7},{9,10},{10,11},{13,14},{14,15},{17,18},{18... | collective-permute-start | bytes 196616 | tf_op jit(solution)/shard_map/ppermute | solution.py:580
  38.3 7.7 %collective-permute-start.11 = (f32[1,128,128]{2,1,0:T(8,128)S(1)}, f32[1,128,128]{2,1,0:T(8,128)S(1)}, u32[]{:S(2)}, u32[]{:S(2)}) collective-permute-start(f32[1,128,128]{2,1,0:T(8,128)S(1)} %coarse_change.1), channel_id=1, source_target_pairs={{1,3},{5,7},{9,11},{13,15},{17,19},{21,23},{25,27},{29,31}} | collective-permute-start | bytes 196616 | tf_op jit(solution)/shard_map/ppermute | solution.py:580

commit v3 on v2

--- a/solution.py
+++ b/solution.py
@@ -128,6 +128,10 @@
     return [pl.BlockSpec(memory_space=pl.ANY)] * count
 
 
+def in_hbm(count):
+    return [pl.BlockSpec(memory_space=pltpu.HBM)] * count
+
+
 def in_smem(count):
     return [pl.BlockSpec(memory_space=pltpu.SMEM)] * count
 
@@ -203,7 +207,7 @@
     return pl.pallas_call(
         kernel,
         out_shape=jax.ShapeDtypeStruct(shape, jnp.float32),
-        in_specs=in_smem(1) + anywhere(1),
+        in_specs=in_smem(1) + in_hbm(1),
         out_specs=in_vmem(1)[0],
         scratch_shapes=[pltpu.VMEM((shape[0], ny, LANES), jnp.int32),
                         pltpu.SemaphoreType.DMA((shape[0],))],
@@ -274,14 +278,14 @@
     return pl.pallas_call(
         kernel,
         out_shape=[jax.ShapeDtypeStruct(coarse, jnp.float32)] * 2,
-        in_specs=in_smem(1) + anywhere(2),
+        in_specs=in_smem(1) + in_hbm(2),
         out_specs=in_vmem(2),
         scratch_shapes=[pltpu.VMEM((halves_count, ny, LANES), jnp.float32),
                         pltpu.VMEM((halves_count, ny, LANES), jnp.int32),
                         pltpu.SemaphoreType.DMA((2, halves_count))],
         compiler_params=small_vmem(),
         name="coarse_parts",
-    )(rate_table, state, classes)
+    )(rate_table, pltpu.with_memory_space_constraint(state, pltpu.HBM), pltpu.with_memory_space_constraint(classes, pltpu.HBM))
 
 
 def gram_steps(g00, g01, g11, g12, g22, h22):
@@ -316,10 +320,17 @@
     return (alpha0 + alpha1 * e + alpha2 * u, alpha1 * f + alpha2 * v, alpha2 * w)
 
 
-def fine_kernel(planes, halves, strips):
-    def kernel(*refs):
-        x_in = refs[:planes]
-        perm = refs[planes:2 * planes]
+def fine_kernel(order, halves, strips):
+    planes = len(order)
+
+    def kernel(active, *refs):
+        @pl.when(active[0] == 1)
+        def _():
+            steps(*refs)
+
+    def steps(*refs):
+        x_in = [refs[order.index(k)] for k in range(planes)]
+        perm = [refs[planes + order.index(k)] for k in range(planes)]
         outs = refs[2 * planes:3 * planes]
         x_next, r, p1, p2 = refs[3 * planes:]
         lane = lax.broadcasted_iota(jnp.int32, (DEPTH, SUB, LANES), 2)
@@ -454,19 +465,19 @@
     return kernel
 
 
-def fine_steps(state_strips, perm_strips):
-    planes = len(state_strips)
-    halves, strips = perm_strips[0].shape[:2]
+def fine_steps(active, state_strips, perm_strips, order):
+    planes = len(order)
+    shape = perm_strips[0].shape
     field = pltpu.VMEM((planes,) + state_strips[0].shape, jnp.float32)
     return pl.pallas_call(
-        fine_kernel(planes, halves, strips),
-        out_shape=[jax.ShapeDtypeStruct(perm_strips[0].shape, jnp.float32)] * planes,
-        in_specs=in_vmem(2 * planes),
+        fine_kernel(order, *shape[:2]),
+        out_shape=[jax.ShapeDtypeStruct(shape, jnp.float32)] * planes,
+        in_specs=in_smem(1) + in_vmem(2 * planes),
         out_specs=in_vmem(planes),
         scratch_shapes=[field] * 4,
         compiler_params=small_vmem(),
         name="fine_steps",
-    )(*state_strips, *perm_strips)
+    )(active, *[state_strips[k] for k in order], *[perm_strips[k] for k in order])
 
 
 def chosen(which, candidates, h, o):
@@ -535,13 +546,13 @@
     return pl.pallas_call(
         kernel,
         out_shape=jax.ShapeDtypeStruct((ny, nz), jnp.float32),
-        in_specs=in_smem(1) + in_vmem(count + 1 + turns) + anywhere(1),
-        out_specs=anywhere(1)[0],
+        in_specs=in_smem(1) + in_vmem(count + 1 + turns) + in_hbm(1),
+        out_specs=in_hbm(1)[0],
         scratch_shapes=[pltpu.VMEM((halves_count, ny, LANES), jnp.float32),
                         pltpu.SemaphoreType.DMA((halves_count,))],
         compiler_params=small_vmem(),
         name="corrected",
-    )(choice, *candidates, ratio, *changes, start)
+    )(choice, *candidates, ratio, *changes, pltpu.with_memory_space_constraint(start, pltpu.HBM))
 
 
 def gathered_body(state, classes, perm_table, rate_table):
@@ -552,28 +563,28 @@
     place = lambda s, t: (s % width) * slices + t
     site = lambda j: (width // 2 - 1 + j % 2) % width
     used = range(slices - 1)
-    far_first = sorted(range(1, width), key=lambda k: -min(k, width - k))
-
-    def to_sites(array, k, late):
+
+    def to_sites(array, k):
         return lax.ppermute(array, axes, [
-            (place(site(j) + k, j + late), place(site(j), j + 1)) for j in used])
+            (place(site(j) + k, j), place(site(j), j)) for j in used])
 
     def from_sites(array, k):
         return lax.ppermute(array, axes, [
-            (place(site(j), j + 1), place(site(j) + k, j + 1)) for j in used])
-
-    state_planes = {k: to_sites(start, k, 0) for k in far_first + [0]}
+            (place(site(j), j), place(site(j) + k, j + 1)) for j in used])
+
+    order = sorted(range(1, width), key=lambda k: (min(k, width - k), -k)) + [0]
+    state_planes = {k: to_sites(start, k) for k in order[:-1]}
+    state_planes[0] = start
     perm = strips_of_perm(kinds, perm_table)
-    perm_strips = {k: to_sites(perm, k, 1) for k in far_first}
+    perm_strips = {k: to_sites(perm, k) for k in order[:-1]}
     perm_strips[0] = perm
     own, ratio = coarse_parts(start, kinds, rate_table)
-    state_strips = strips_of_state([state_planes[k] for k in range(width)])
-    ends = fine_steps(state_strips, [perm_strips[k] for k in range(width)])
-    landed = {k: from_sites(ends[k], k) for k in far_first}
-    landed[0] = ends[0]
-    candidates = [landed[k] for k in range(width)]
-    turn = lax.axis_index("tm")
-    which = (lax.axis_index("space") - site(turn - 1)) % width
+    state_strips = dict(zip(order, strips_of_state([state_planes[k] for k in order])))
+    turn, plane = lax.axis_index("tm"), lax.axis_index("space")
+    here = (turn < slices - 1) & (plane == site(turn))
+    ends = fine_steps(here.astype(jnp.int32)[None], state_strips, perm_strips, order)
+    candidates = [from_sites(ends[k], k) for k in range(width)]
+    which = (plane - site(turn - 1)) % width
     choice = jnp.stack([which, turn]).astype(jnp.int32)
     change = coarse_change(choice, candidates, own)
     changes = [

time: 47.9 us -> 45.6 us (0.952)
  waiting for transfers between devices: 19.8 us -> 27 us
  starting transfers between devices: 15.7 us -> 10.1 us
  Pallas kernels: 10.1 us -> 6.14 us
    ppermute x2, waiting for transfers between devices: 6.42 us -> 13.8 us  [gathered_body(): lax.ppermute(change, 'tm', [(i, i + k) for i in range(1, slices - k)])]
    ppermute x10, starting transfers between devices: 13.1 us -> 7.51 us  [the longest x6 4.18 us: to_sites(): lax.ppermute(array, axes, [(place(site(j) + k, j), place(site(j), j)) for...]
    pallas_call x1, Pallas kernels: 5.05 us -> 0.01 us  [fine_steps(): pl.pallas_call(fine_kernel(order, *shape[:2]), out_shape=[jax.ShapeDtypeS...]
    pallas_call x1, Pallas kernels: 1.15 us -> 2.19 us  [coarse_parts(): pl.pallas_call(kernel, out_shape=[jax.ShapeDtypeStruct(coarse, jnp.float3...]
    unnamed x10 -> x8, local copies, waits for them, and re-layouts: 1.59 us -> 1.6 us
  transfers between devices with their start and end apart: 12 -> 12, of which waited for: 8 -> 3; matrix products, arithmetic and copies ran while one was open for 0% -> 0% of each run, Pallas kernels for 6% -> 8%
where the time goes in v3:
time: 45.6 us; the launch traced here: 45.2 us
  waiting for transfers between devices  27 us (59%)
  starting transfers between devices  10.1 us (22%)
  Pallas kernels  6.14 us (13%)
  local copies, waits for them, and re-layouts  1.6 us (4%)
    ppermute x2, waiting for transfers between devices, gathered_body(): lax.ppermute(change, 'tm', [(i, i + k) for i in range(1, slices - k)])  13.8 us
    ppermute x4, waiting for transfers between devices, from_sites(): lax.ppermute(array, axes, [(place(site(j), j), place(site(j) + k, j + 1))...  13.2 us
    ppermute x6, starting transfers between devices, to_sites(): lax.ppermute(array, axes, [(place(site(j) + k, j), place(site(j), j)) for...  4.18 us
    ppermute x4, starting transfers between devices, from_sites(): lax.ppermute(array, axes, [(place(site(j), j), place(site(j) + k, j + 1))...  3.32 us
    ppermute x2, starting transfers between devices, gathered_body(): lax.ppermute(change, 'tm', [(i, i + k) for i in range(1, slices - k)])  2.58 us
    pallas_call x1, Pallas kernels, coarse_parts(): pl.pallas_call(kernel, out_shape=[jax.ShapeDtypeStruct(coarse, jnp.float3...  2.19 us
    unnamed x8, local copies, waits for them, and re-layouts  1.6 us
    pallas_call x1, Pallas kernels, corrected(): pl.pallas_call(kernel, out_shape=jax.ShapeDtypeStruct((ny, nz), jnp.float...  1.57 us
  transfers between devices with their start and end apart: 12, of which 3 were waited for; matrix products, arithmetic and copies ran while one was open for 0% of the time, Pallas kernels for 8%

profile of v3, /device:TPU:11, one launch (start us, length us, event | category | flops | bytes accessed | tf_op | source)
XLA Modules:
  0.0 45.2 jit_solution(13096108650058296274)
XLA Ops:
  0.0 0.0 copy-start.2
  0.0 0.8 %collective-permute-start = (f32[256,256]{1,0:T(8,128)}, f32[256,256]{1,0:T(8,128)S(1)}, u32[]{:S(2)}, u32[]{:S(2)}) collective-permute-start(f32[256,256]{1,0:T(8,128)} %bitcast.6), channel_id=1, source_target_pairs={{0,4},{5,9},{2,6},{16,20},{21,25},{18,22}} | collective-permute-start | bytes 786440 | tf_op jit(solution)/shard_map/ppermute | solution.py:568
  0.8 0.7 %collective-permute-start.1 = (f32[256,256]{1,0:T(8,128)}, f32[256,256]{1,0:T(8,128)S(1)}, u32[]{:S(2)}, u32[]{:S(2)}) collective-permute-start(f32[256,256]{1,0:T(8,128)} %bitcast.7), channel_id=1, source_target_pairs={{8,4},{13,9},{10,6},{24,20},{29,25},{26,22}} | collective-permute-start | bytes 786440 | tf_op jit(solution)/shard_map/ppermute | solution.py:568
  1.5 0.7 %collective-permute-start.2 = (f32[256,256]{1,0:T(8,128)}, f32[256,256]{1,0:T(8,128)S(1)}, u32[]{:S(2)}, u32[]{:S(2)}) collective-permute-start(f32[256,256]{1,0:T(8,128)} %bitcast.8), channel_id=1, source_target_pairs={{12,4},{1,9},{14,6},{28,20},{17,25},{30,22}} | collective-permute-start | bytes 786440 | tf_op jit(solution)/shard_map/ppermute | solution.py:568
  2.2 0.0 copy-done.2
  2.2 0.0 copy-start.1
  2.2 0.9 %copy-done.1 = s32[1,256,256]{2,1,0:T(8,128)S(1)} copy-done((s32[1,256,256]{2,1,0:T(8,128)S(1)}, s32[1,256,256]{2,1,0:T(8,128)}, u32[]{:S(2)}) %copy-start.1) | copy-done | bytes 262168
  3.1 0.0 copy-start
  3.1 0.8 %strips_of_perm.1.refs_7_ = f32[2,32,8,128]{3,2,1,0:T(8,128)S(1)} custom-call(f32[4]{0:T(128)S(1)} %copy-done.2, s32[256,256]{1,0:T(8,128)S(1)} %bitcast.13), custom_call_target="tpu_custom_call" | custom-call | tf_op jit(solution)/shard_map/strips_of_perm/pallas_call | solution.py:207
  3.9 0.7 %collective-permute-start.3 = (f32[2,32,8,128]{3,2,1,0:T(8,128)S(1)}, f32[2,32,8,128]{3,2,1,0:T(8,128)S(1)}, u32[]{:S(2)}, u32[]{:S(2)}) collective-permute-start(f32[2,32,8,128]{3,2,1,0:T(8,128)S(1)} %strips_of_perm.1.refs_7_), channel_id=1, source_target_pairs={{0,4},{5,9},{2,6},{16,20},{21,25},{18,22}} | collective-permute-start | bytes 786440 | tf_op jit(solution)/shard_map/ppermute | solution.py:568
  4.6 0.7 %collective-permute-start.4 = (f32[2,32,8,128]{3,2,1,0:T(8,128)S(1)}, f32[2,32,8,128]{3,2,1,0:T(8,128)S(1)}, u32[]{:S(2)}, u32[]{:S(2)}) collective-permute-start(f32[2,32,8,128]{3,2,1,0:T(8,128)S(1)} %strips_of_perm.1.refs_7_), channel_id=1, source_target_pairs={{8,4},{13,9},{10,6},{24,20},{29,25},{26,22}} | collective-permute-start | bytes 786440 | tf_op jit(solution)/shard_map/ppermute | solution.py:568
  5.3 0.0 collective-permute-done.refs_0_
  5.3 0.7 %collective-permute-start.5 = (f32[2,32,8,128]{3,2,1,0:T(8,128)S(1)}, f32[2,32,8,128]{3,2,1,0:T(8,128)S(1)}, u32[]{:S(2)}, u32[]{:S(2)}) collective-permute-start(f32[2,32,8,128]{3,2,1,0:T(8,128)S(1)} %strips_of_perm.1.refs_7_), channel_id=1, source_target_pairs={{12,4},{1,9},{14,6},{28,20},{17,25},{30,22}} | collective-permute-start | bytes 786440 | tf_op jit(solution)/shard_map/ppermute | solution.py:568
  6.0 0.0 collective-permute-done.1.refs_1_
  6.0 0.0 collective-permute-done.2.refs_2_
  6.0 0.0 copy-done
  6.1 0.8 %strips_of_state.1 = (f32[2,34,8,128]{3,2,1,0:T(8,128)S(1)}, f32[2,34,8,128]{3,2,1,0:T(8,128)S(1)}, f32[2,34,8,128]{3,2,1,0:T(8,128)S(1)}, f32[2,34,8,128]{3,2,1,0:T(8,128)S(1)}) custom-call(f32[256,256]{1,0:T(8,128)S(1)} %collective-permute-done.refs_0_, f32[256,256]{1,0:T(8,128)S(1)} %collective-permute-done.1.refs_1_, ...), custom_call_target="tpu_custom_call" | custom-call | tf_op jit(solution)/shard_map/strips_of_state/pallas_call | solution.py:241
  6.9 0.0 collective-permute-done.3.refs_4_
  6.9 0.0 collective-permute-done.4.refs_5_
  6.9 0.0 collective-permute-done.5.refs_6_
  6.9 1.3 %collective-permute-start.6 = (f32[2,32,8,128]{3,2,1,0:T(8,128)S(1)}, f32[2,32,8,128]{3,2,1,0:T(8,128)S(1)}, u32[]{:S(2)}, u32[]{:S(2)}) collective-permute-start(f32[2,32,8,128]{3,2,1,0:T(8,128)S(1)} %get-tuple-element.19), channel_id=1, source_target_pairs={{4,5},{9,10},{6,7},{20,21},{25,26},{22,23}} | collective-permute-start | bytes 786440 | tf_op jit(solution)/shard_map/ppermute | solution.py:572
  8.2 0.7 %collective-permute-start.7 = (f32[2,32,8,128]{3,2,1,0:T(8,128)S(1)}, f32[2,32,8,128]{3,2,1,0:T(8,128)S(1)}, u32[]{:S(2)}, u32[]{:S(2)}) collective-permute-start(f32[2,32,8,128]{3,2,1,0:T(8,128)S(1)} %get-tuple-element.20), channel_id=1, source_target_pairs={{4,9},{9,14},{6,11},{20,25},{25,30},{22,27}} | collective-permute-start | bytes 786440 | tf_op jit(solution)/shard_map/ppermute | solution.py:572
  8.9 0.7 %collective-permute-start.8 = (f32[2,32,8,128]{3,2,1,0:T(8,128)S(1)}, f32[2,32,8,128]{3,2,1,0:T(8,128)S(1)}, u32[]{:S(2)}, u32[]{:S(2)}) collective-permute-start(f32[2,32,8,128]{3,2,1,0:T(8,128)S(1)} %get-tuple-element.21), channel_id=1, source_target_pairs={{4,13},{9,2},{6,15},{20,29},{25,18},{22,31}} | collective-permute-start | bytes 786440 | tf_op jit(solution)/shard_map/ppermute | solution.py:572
  9.6 0.7 %collective-permute-start.9 = (f32[2,32,8,128]{3,2,1,0:T(8,128)S(1)}, f32[2,32,8,128]{3,2,1,0:T(8,128)S(1)}, u32[]{:S(2)}, u32[]{:S(2)}) collective-permute-start(f32[2,32,8,128]{3,2,1,0:T(8,128)S(1)} %get-tuple-element.22), channel_id=1, source_target_pairs={{4,1},{9,6},{6,3},{20,17},{25,22},{22,19}} | collective-permute-start | bytes 786440 | tf_op jit(solution)/shard_map/ppermute | solution.py:572
  10.3 0.0 copy-start.3
  10.3 0.6 %copy-done.3 = f32[4]{0:T(128)S(1)} copy-done((f32[4]{0:T(128)S(1)}, f32[4]{0:T(128)}, u32[]{:S(2)}) %copy-start.3) | copy-done | bytes 40
  11.0 2.2 %coarse_parts.1 = (f32[1,128,128]{2,1,0:T(8,128)S(1)}, f32[1,128,128]{2,1,0:T(8,128)S(1)}) custom-call(f32[4]{0:T(128)S(1)} %copy-done.3, f32[256,256]{1,0:T(8,128)} %bitcast.9, s32[256,256]{1,0:T(8,128)} %bitcast.12), custom_call_target="tpu_custom_call" | custom-call | tf_op jit(solution)/shard_map/coarse_parts/pallas_call | solution.py:278
  13.2 0.1 pad_add_fusion.choice.which
  13.3 13.2 %collective-permute-done.6.refs_0_ = f32[2,32,8,128]{3,2,1,0:T(8,128)S(1)} collective-permute-done((f32[2,32,8,128]{3,2,1,0:T(8,128)S(1)}, f32[2,32,8,128]{3,2,1,0:T(8,128)S(1)}, u32[]{:S(2)}, u32[]{:S(2)}) %collective-permute-start.6) | collective-permute-done | bytes 262176 | tf_op jit(solution)/shard_map/ppermute | solution.py:572
  26.5 0.0 collective-permute-done.7.refs_1_
  26.5 0.0 collective-permute-done.8.refs_2_
  26.5 0.0 collective-permute-done.9.refs_3_
  26.5 0.8 %coarse_change.1 = f32[1,128,128]{2,1,0:T(8,128)S(1)} custom-call(s32[2]{0:T(128)S(1)} %pad_add_fusion.choice.which, f32[2,32,8,128]{3,2,1,0:T(8,128)S(1)} %collective-permute-done.6.refs_0_, f32[2,32,8,128]{3,2,1,0:T(8,128)S(1)} %collective-permute-done.7.refs_1_, f32[2,32,8,128]{3,2,1,0:T(8,128)S(1)} %collective-permute-done.8.refs_2_, ...), custom_call_target="tpu_custom_call" | custom-call | tf_op jit(solution)/shard_map/coarse_change/pallas_call | solution.py:500
  27.3 1.3 %collective-permute-start.10 = (f32[1,128,128]{2,1,0:T(8,128)S(1)}, f32[1,128,128]{2,1,0:T(8,128)S(1)}, u32[]{:S(2)}, u32[]{:S(2)}) collective-permute-start(f32[1,128,128]{2,1,0:T(8,128)S(1)} %coarse_change.1), channel_id=1, source_target_pairs={{1,2},{2,3},{5,6},{6,7},{9,10},{10,11},{13,14},{14,15},{17,18},{18... | collective-permute-start | bytes 196616 | tf_op jit(solution)/shard_map/ppermute | solution.py:591
  28.6 1.3 %collective-permute-start.11 = (f32[1,128,128]{2,1,0:T(8,128)S(1)}, f32[1,128,128]{2,1,0:T(8,128)S(1)}, u32[]{:S(2)}, u32[]{:S(2)}) collective-permute-start(f32[1,128,128]{2,1,0:T(8,128)S(1)} %coarse_change.1), channel_id=1, source_target_pairs={{1,3},{5,7},{9,11},{13,15},{17,19},{21,23},{25,27},{29,31}} | collective-permute-start | bytes 196616 | tf_op jit(solution)/shard_map/ppermute | solution.py:591
  29.9 10.3 %collective-permute-done.10.refs_5_ = f32[1,128,128]{2,1,0:T(8,128)S(1)} collective-permute-done((f32[1,128,128]{2,1,0:T(8,128)S(1)}, f32[1,128,128]{2,1,0:T(8,128)S(1)}, u32[]{:S(2)}, u32[]{:S(2)}) %collective-permute-start.10) | collective-permute-done | bytes 65568 | tf_op jit(solution)/shard_map/ppermute | solution.py:591
  40.1 3.5 %collective-permute-done.11.refs_6_ = f32[1,128,128]{2,1,0:T(8,128)S(1)} collective-permute-done((f32[1,128,128]{2,1,0:T(8,128)S(1)}, f32[1,128,128]{2,1,0:T(8,128)S(1)}, u32[]{:S(2)}, u32[]{:S(2)}) %collective-permute-start.11) | collective-permute-done | bytes 65568 | tf_op jit(solution)/shard_map/ppermute | solution.py:591
  43.7 1.6 %corrected.1 = f32[256,256]{1,0:T(8,128)} custom-call(s32[2]{0:T(128)S(1)} %pad_add_fusion.choice.which, f32[2,32,8,128]{3,2,1,0:T(8,128)S(1)} %collective-permute-done.6.refs_0_, f32[2,32,8,128]{3,2,1,0:T(8,128)S(1)} %collective-permute-done.7.refs_1_, f32[2,32,8,128]{3,2,1,0:T(8,128)S(1)} %collective-permute-done.8.refs_2_, ...), custom_call_target="tpu_custom_call" | custom-call | tf_op jit(solution)/shard_map/corrected/pallas_call | solution.py:546
  (1 shorter events, 0.0 us)
Async XLA Ops:
  0.0 2.2 %copy-start.2 = (f32[4]{0:T(128)S(1)}, f32[4]{0:T(128)}, u32[]{:S(2)}) copy-start(f32[4]{0:T(128)} %values.1) | copy-start | bytes 52
  0.0 5.3 %collective-permute-start = (f32[256,256]{1,0:T(8,128)}, f32[256,256]{1,0:T(8,128)S(1)}, u32[]{:S(2)}, u32[]{:S(2)}) collective-permute-start(f32[256,256]{1,0:T(8,128)} %bitcast.6), channel_id=1, source_target_pairs={{0,4},{5,9},{2,6},{16,20},{21,25},{18,22}} | collective-permute-start | bytes 786440 | tf_op jit(solution)/shard_map/ppermute | solution.py:568
  0.8 5.2 %collective-permute-start.1 = (f32[256,256]{1,0:T(8,128)}, f32[256,256]{1,0:T(8,128)S(1)}, u32[]{:S(2)}, u32[]{:S(2)}) collective-permute-start(f32[256,256]{1,0:T(8,128)} %bitcast.7), channel_id=1, source_target_pairs={{8,4},{13,9},{10,6},{24,20},{29,25},{26,22}} | collective-permute-start | bytes 786440 | tf_op jit(solution)/shard_map/ppermute | solution.py:568
  1.5 4.5 %collective-permute-start.2 = (f32[256,256]{1,0:T(8,128)}, f32[256,256]{1,0:T(8,128)S(1)}, u32[]{:S(2)}, u32[]{:S(2)}) collective-permute-start(f32[256,256]{1,0:T(8,128)} %bitcast.8), channel_id=1, source_target_pairs={{12,4},{1,9},{14,6},{28,20},{17,25},{30,22}} | collective-permute-start | bytes 786440 | tf_op jit(solution)/shard_map/ppermute | solution.py:568
  2.2 1.0 %copy-start.1 = (s32[1,256,256]{2,1,0:T(8,128)S(1)}, s32[1,256,256]{2,1,0:T(8,128)}, u32[]{:S(2)}) copy-start(s32[1,256,256]{2,1,0:T(8,128)} %param.5) | copy-start | bytes 786436
  3.1 2.9 %copy-start = (f32[1,1,256,256]{3,2,1,0:T(8,128)S(1)}, f32[1,1,256,256]{3,2,1,0:T(8,128)}, u32[]{:S(2)}) copy-start(f32[1,1,256,256]{3,2,1,0:T(8,128)} %param.4) | copy-start | bytes 786436
  3.9 3.0 %collective-permute-start.3 = (f32[2,32,8,128]{3,2,1,0:T(8,128)S(1)}, f32[2,32,8,128]{3,2,1,0:T(8,128)S(1)}, u32[]{:S(2)}, u32[]{:S(2)}) collective-permute-start(f32[2,32,8,128]{3,2,1,0:T(8,128)S(1)} %strips_of_perm.1.refs_7_), channel_id=1, source_target_pairs={{0,4},{5,9},{2,6},{16,20},{21,25},{18,22}} | collective-permute-start | bytes 786440 | tf_op jit(solution)/shard_map/ppermute | solution.py:568
  4.6 2.3 %collective-permute-start.4 = (f32[2,32,8,128]{3,2,1,0:T(8,128)S(1)}, f32[2,32,8,128]{3,2,1,0:T(8,128)S(1)}, u32[]{:S(2)}, u32[]{:S(2)}) collective-permute-start(f32[2,32,8,128]{3,2,1,0:T(8,128)S(1)} %strips_of_perm.1.refs_7_), channel_id=1, source_target_pairs={{8,4},{13,9},{10,6},{24,20},{29,25},{26,22}} | collective-permute-start | bytes 786440 | tf_op jit(solution)/shard_map/ppermute | solution.py:568
  5.3 1.6 %collective-permute-start.5 = (f32[2,32,8,128]{3,2,1,0:T(8,128)S(1)}, f32[2,32,8,128]{3,2,1,0:T(8,128)S(1)}, u32[]{:S(2)}, u32[]{:S(2)}) collective-permute-start(f32[2,32,8,128]{3,2,1,0:T(8,128)S(1)} %strips_of_perm.1.refs_7_), channel_id=1, source_target_pairs={{12,4},{1,9},{14,6},{28,20},{17,25},{30,22}} | collective-permute-start | bytes 786440 | tf_op jit(solution)/shard_map/ppermute | solution.py:568
  6.9 19.5 %collective-permute-start.6 = (f32[2,32,8,128]{3,2,1,0:T(8,128)S(1)}, f32[2,32,8,128]{3,2,1,0:T(8,128)S(1)}, u32[]{:S(2)}, u32[]{:S(2)}) collective-permute-start(f32[2,32,8,128]{3,2,1,0:T(8,128)S(1)} %get-tuple-element.19), channel_id=1, source_target_pairs={{4,5},{9,10},{6,7},{20,21},{25,26},{22,23}} | collective-permute-start | bytes 786440 | tf_op jit(solution)/shard_map/ppermute | solution.py:572
  8.2 18.2 %collective-permute-start.7 = (f32[2,32,8,128]{3,2,1,0:T(8,128)S(1)}, f32[2,32,8,128]{3,2,1,0:T(8,128)S(1)}, u32[]{:S(2)}, u32[]{:S(2)}) collective-permute-start(f32[2,32,8,128]{3,2,1,0:T(8,128)S(1)} %get-tuple-element.20), channel_id=1, source_target_pairs={{4,9},{9,14},{6,11},{20,25},{25,30},{22,27}} | collective-permute-start | bytes 786440 | tf_op jit(solution)/shard_map/ppermute | solution.py:572
  8.9 17.6 %collective-permute-start.8 = (f32[2,32,8,128]{3,2,1,0:T(8,128)S(1)}, f32[2,32,8,128]{3,2,1,0:T(8,128)S(1)}, u32[]{:S(2)}, u32[]{:S(2)}) collective-permute-start(f32[2,32,8,128]{3,2,1,0:T(8,128)S(1)} %get-tuple-element.21), channel_id=1, source_target_pairs={{4,13},{9,2},{6,15},{20,29},{25,18},{22,31}} | collective-permute-start | bytes 786440 | tf_op jit(solution)/shard_map/ppermute | solution.py:572
  9.6 16.9 %collective-permute-start.9 = (f32[2,32,8,128]{3,2,1,0:T(8,128)S(1)}, f32[2,32,8,128]{3,2,1,0:T(8,128)S(1)}, u32[]{:S(2)}, u32[]{:S(2)}) collective-permute-start(f32[2,32,8,128]{3,2,1,0:T(8,128)S(1)} %get-tuple-element.22), channel_id=1, source_target_pairs={{4,1},{9,6},{6,3},{20,17},{25,22},{22,19}} | collective-permute-start | bytes 786440 | tf_op jit(solution)/shard_map/ppermute | solution.py:572
  10.3 0.7 %copy-start.3 = (f32[4]{0:T(128)S(1)}, f32[4]{0:T(128)}, u32[]{:S(2)}) copy-start(f32[4]{0:T(128)} %rates.1) | copy-start | bytes 52
  27.3 12.9 %collective-permute-start.10 = (f32[1,128,128]{2,1,0:T(8,128)S(1)}, f32[1,128,128]{2,1,0:T(8,128)S(1)}, u32[]{:S(2)}, u32[]{:S(2)}) collective-permute-start(f32[1,128,128]{2,1,0:T(8,128)S(1)} %coarse_change.1), channel_id=1, source_target_pairs={{1,2},{2,3},{5,6},{6,7},{9,10},{10,11},{13,14},{14,15},{17,18},{18... | collective-permute-start | bytes 196616 | tf_op jit(solution)/shard_map/ppermute | solution.py:591
  28.6 15.1 %collective-permute-start.11 = (f32[1,128,128]{2,1,0:T(8,128)S(1)}, f32[1,128,128]{2,1,0:T(8,128)S(1)}, u32[]{:S(2)}, u32[]{:S(2)}) collective-permute-start(f32[1,128,128]{2,1,0:T(8,128)S(1)} %coarse_change.1), channel_id=1, source_target_pairs={{1,3},{5,7},{9,11},{13,15},{17,19},{21,23},{25,27},{29,31}} | collective-permute-start | bytes 196616 | tf_op jit(solution)/shard_map/ppermute | solution.py:591

commit v4 on v3

--- a/solution.py
+++ b/solution.py
@@ -519,9 +519,17 @@
 
         @pl.when(which[1] == 0)
         def _():
-            copy = pltpu.make_async_copy(begin, out, sems.at[0])
-            copy.start()
-            copy.wait()
+            copies = halves_of(begin, halves, sems)
+            for copy in copies:
+                copy.start()
+            leaving = []
+            for h, copy in enumerate(copies):
+                copy.wait()
+                leaving.append(pltpu.make_async_copy(
+                    halves.at[h], out.at[:, pl.ds(h * LANES, LANES)], sems.at[h]))
+                leaving[h].start()
+            for copy in leaving:
+                copy.wait()
 
         @pl.when(which[1] != 0)
         def _():

time: 45.6 us -> 45.6 us (level)
  no operation moved by 1% of the time
where the time goes in v4:
time: 45.6 us; the launch traced here: 45.2 us
  waiting for transfers between devices  27 us (59%)
  starting transfers between devices  10.1 us (22%)
  Pallas kernels  6.14 us (13%)
  local copies, waits for them, and re-layouts  1.6 us (4%)
    ppermute x2, waiting for transfers between devices, gathered_body(): lax.ppermute(change, 'tm', [(i, i + k) for i in range(1, slices - k)])  13.8 us
    ppermute x4, waiting for transfers between devices, from_sites(): lax.ppermute(array, axes, [(place(site(j), j), place(site(j) + k, j + 1))...  13.2 us
    ppermute x6, starting transfers between devices, to_sites(): lax.ppermute(array, axes, [(place(site(j) + k, j), place(site(j), j)) for...  4.18 us
    ppermute x4, starting transfers between devices, from_sites(): lax.ppermute(array, axes, [(place(site(j), j), place(site(j) + k, j + 1))...  3.32 us
    ppermute x2, starting transfers between devices, gathered_body(): lax.ppermute(change, 'tm', [(i, i + k) for i in range(1, slices - k)])  2.58 us
    pallas_call x1, Pallas kernels, coarse_parts(): pl.pallas_call(kernel, out_shape=[jax.ShapeDtypeStruct(coarse, jnp.float3...  2.19 us
    unnamed x8, local copies, waits for them, and re-layouts  1.6 us
    pallas_call x1, Pallas kernels, corrected(): pl.pallas_call(kernel, out_shape=jax.ShapeDtypeStruct((ny, nz), jnp.float...  1.58 us
  transfers between devices with their start and end apart: 12, of which 3 were waited for; matrix products, arithmetic and copies ran while one was open for 0% of the time, Pallas kernels for 8%

profile of v4, /device:TPU:11, one launch (start us, length us, event | category | flops | bytes accessed | tf_op | source)
XLA Modules:
  0.0 45.2 jit_solution(13144033598448411780)
XLA Ops:
  0.0 0.0 copy-start.2
  0.0 0.8 %collective-permute-start = (f32[256,256]{1,0:T(8,128)}, f32[256,256]{1,0:T(8,128)S(1)}, u32[]{:S(2)}, u32[]{:S(2)}) collective-permute-start(f32[256,256]{1,0:T(8,128)} %bitcast.6), channel_id=1, source_target_pairs={{0,4},{5,9},{2,6},{16,20},{21,25},{18,22}} | collective-permute-start | bytes 786440 | tf_op jit(solution)/shard_map/ppermute | solution.py:576
  0.8 0.7 %collective-permute-start.1 = (f32[256,256]{1,0:T(8,128)}, f32[256,256]{1,0:T(8,128)S(1)}, u32[]{:S(2)}, u32[]{:S(2)}) collective-permute-start(f32[256,256]{1,0:T(8,128)} %bitcast.7), channel_id=1, source_target_pairs={{8,4},{13,9},{10,6},{24,20},{29,25},{26,22}} | collective-permute-start | bytes 786440 | tf_op jit(solution)/shard_map/ppermute | solution.py:576
  1.5 0.7 %collective-permute-start.2 = (f32[256,256]{1,0:T(8,128)}, f32[256,256]{1,0:T(8,128)S(1)}, u32[]{:S(2)}, u32[]{:S(2)}) collective-permute-start(f32[256,256]{1,0:T(8,128)} %bitcast.8), channel_id=1, source_target_pairs={{12,4},{1,9},{14,6},{28,20},{17,25},{30,22}} | collective-permute-start | bytes 786440 | tf_op jit(solution)/shard_map/ppermute | solution.py:576
  2.2 0.0 copy-done.2
  2.2 0.0 copy-start.1
  2.2 0.9 %copy-done.1 = s32[1,256,256]{2,1,0:T(8,128)S(1)} copy-done((s32[1,256,256]{2,1,0:T(8,128)S(1)}, s32[1,256,256]{2,1,0:T(8,128)}, u32[]{:S(2)}) %copy-start.1) | copy-done | bytes 262168
  3.1 0.0 copy-start
  3.1 0.8 %strips_of_perm.1.refs_7_ = f32[2,32,8,128]{3,2,1,0:T(8,128)S(1)} custom-call(f32[4]{0:T(128)S(1)} %copy-done.2, s32[256,256]{1,0:T(8,128)S(1)} %bitcast.13), custom_call_target="tpu_custom_call" | custom-call | tf_op jit(solution)/shard_map/strips_of_perm/pallas_call | solution.py:207
  3.9 0.7 %collective-permute-start.3 = (f32[2,32,8,128]{3,2,1,0:T(8,128)S(1)}, f32[2,32,8,128]{3,2,1,0:T(8,128)S(1)}, u32[]{:S(2)}, u32[]{:S(2)}) collective-permute-start(f32[2,32,8,128]{3,2,1,0:T(8,128)S(1)} %strips_of_perm.1.refs_7_), channel_id=1, source_target_pairs={{0,4},{5,9},{2,6},{16,20},{21,25},{18,22}} | collective-permute-start | bytes 786440 | tf_op jit(solution)/shard_map/ppermute | solution.py:576
  4.6 0.7 %collective-permute-start.4 = (f32[2,32,8,128]{3,2,1,0:T(8,128)S(1)}, f32[2,32,8,128]{3,2,1,0:T(8,128)S(1)}, u32[]{:S(2)}, u32[]{:S(2)}) collective-permute-start(f32[2,32,8,128]{3,2,1,0:T(8,128)S(1)} %strips_of_perm.1.refs_7_), channel_id=1, source_target_pairs={{8,4},{13,9},{10,6},{24,20},{29,25},{26,22}} | collective-permute-start | bytes 786440 | tf_op jit(solution)/shard_map/ppermute | solution.py:576
  5.3 0.0 collective-permute-done.refs_0_
  5.3 0.7 %collective-permute-start.5 = (f32[2,32,8,128]{3,2,1,0:T(8,128)S(1)}, f32[2,32,8,128]{3,2,1,0:T(8,128)S(1)}, u32[]{:S(2)}, u32[]{:S(2)}) collective-permute-start(f32[2,32,8,128]{3,2,1,0:T(8,128)S(1)} %strips_of_perm.1.refs_7_), channel_id=1, source_target_pairs={{12,4},{1,9},{14,6},{28,20},{17,25},{30,22}} | collective-permute-start | bytes 786440 | tf_op jit(solution)/shard_map/ppermute | solution.py:576
  6.0 0.0 collective-permute-done.1.refs_1_
  6.0 0.0 collective-permute-done.2.refs_2_
  6.0 0.0 copy-done
  6.1 0.8 %strips_of_state.1 = (f32[2,34,8,128]{3,2,1,0:T(8,128)S(1)}, f32[2,34,8,128]{3,2,1,0:T(8,128)S(1)}, f32[2,34,8,128]{3,2,1,0:T(8,128)S(1)}, f32[2,34,8,128]{3,2,1,0:T(8,128)S(1)}) custom-call(f32[256,256]{1,0:T(8,128)S(1)} %collective-permute-done.refs_0_, f32[256,256]{1,0:T(8,128)S(1)} %collective-permute-done.1.refs_1_, ...), custom_call_target="tpu_custom_call" | custom-call | tf_op jit(solution)/shard_map/strips_of_state/pallas_call | solution.py:241
  6.9 0.0 collective-permute-done.3.refs_4_
  6.9 0.0 collective-permute-done.4.refs_5_
  6.9 0.0 collective-permute-done.5.refs_6_
  6.9 1.3 %collective-permute-start.6 = (f32[2,32,8,128]{3,2,1,0:T(8,128)S(1)}, f32[2,32,8,128]{3,2,1,0:T(8,128)S(1)}, u32[]{:S(2)}, u32[]{:S(2)}) collective-permute-start(f32[2,32,8,128]{3,2,1,0:T(8,128)S(1)} %get-tuple-element.19), channel_id=1, source_target_pairs={{4,5},{9,10},{6,7},{20,21},{25,26},{22,23}} | collective-permute-start | bytes 786440 | tf_op jit(solution)/shard_map/ppermute | solution.py:580
  8.2 0.7 %collective-permute-start.7 = (f32[2,32,8,128]{3,2,1,0:T(8,128)S(1)}, f32[2,32,8,128]{3,2,1,0:T(8,128)S(1)}, u32[]{:S(2)}, u32[]{:S(2)}) collective-permute-start(f32[2,32,8,128]{3,2,1,0:T(8,128)S(1)} %get-tuple-element.20), channel_id=1, source_target_pairs={{4,9},{9,14},{6,11},{20,25},{25,30},{22,27}} | collective-permute-start | bytes 786440 | tf_op jit(solution)/shard_map/ppermute | solution.py:580
  8.9 0.7 %collective-permute-start.8 = (f32[2,32,8,128]{3,2,1,0:T(8,128)S(1)}, f32[2,32,8,128]{3,2,1,0:T(8,128)S(1)}, u32[]{:S(2)}, u32[]{:S(2)}) collective-permute-start(f32[2,32,8,128]{3,2,1,0:T(8,128)S(1)} %get-tuple-element.21), channel_id=1, source_target_pairs={{4,13},{9,2},{6,15},{20,29},{25,18},{22,31}} | collective-permute-start | bytes 786440 | tf_op jit(solution)/shard_map/ppermute | solution.py:580
  9.6 0.7 %collective-permute-start.9 = (f32[2,32,8,128]{3,2,1,0:T(8,128)S(1)}, f32[2,32,8,128]{3,2,1,0:T(8,128)S(1)}, u32[]{:S(2)}, u32[]{:S(2)}) collective-permute-start(f32[2,32,8,128]{3,2,1,0:T(8,128)S(1)} %get-tuple-element.22), channel_id=1, source_target_pairs={{4,1},{9,6},{6,3},{20,17},{25,22},{22,19}} | collective-permute-start | bytes 786440 | tf_op jit(solution)/shard_map/ppermute | solution.py:580
  10.3 0.0 copy-start.3
  10.3 0.6 %copy-done.3 = f32[4]{0:T(128)S(1)} copy-done((f32[4]{0:T(128)S(1)}, f32[4]{0:T(128)}, u32[]{:S(2)}) %copy-start.3) | copy-done | bytes 40
  11.0 2.2 %coarse_parts.1 = (f32[1,128,128]{2,1,0:T(8,128)S(1)}, f32[1,128,128]{2,1,0:T(8,128)S(1)}) custom-call(f32[4]{0:T(128)S(1)} %copy-done.3, f32[256,256]{1,0:T(8,128)} %bitcast.9, s32[256,256]{1,0:T(8,128)} %bitcast.12), custom_call_target="tpu_custom_call" | custom-call | tf_op jit(solution)/shard_map/coarse_parts/pallas_call | solution.py:278
  13.2 0.1 pad_add_fusion.choice.which
  13.3 13.2 %collective-permute-done.6.refs_0_ = f32[2,32,8,128]{3,2,1,0:T(8,128)S(1)} collective-permute-done((f32[2,32,8,128]{3,2,1,0:T(8,128)S(1)}, f32[2,32,8,128]{3,2,1,0:T(8,128)S(1)}, u32[]{:S(2)}, u32[]{:S(2)}) %collective-permute-start.6) | collective-permute-done | bytes 262176 | tf_op jit(solution)/shard_map/ppermute | solution.py:580
  26.5 0.0 collective-permute-done.7.refs_1_
  26.5 0.0 collective-permute-done.8.refs_2_
  26.5 0.0 collective-permute-done.9.refs_3_
  26.5 0.8 %coarse_change.1 = f32[1,128,128]{2,1,0:T(8,128)S(1)} custom-call(s32[2]{0:T(128)S(1)} %pad_add_fusion.choice.which, f32[2,32,8,128]{3,2,1,0:T(8,128)S(1)} %collective-permute-done.6.refs_0_, f32[2,32,8,128]{3,2,1,0:T(8,128)S(1)} %collective-permute-done.7.refs_1_, f32[2,32,8,128]{3,2,1,0:T(8,128)S(1)} %collective-permute-done.8.refs_2_, ...), custom_call_target="tpu_custom_call" | custom-call | tf_op jit(solution)/shard_map/coarse_change/pallas_call | solution.py:500
  27.3 1.3 %collective-permute-start.10 = (f32[1,128,128]{2,1,0:T(8,128)S(1)}, f32[1,128,128]{2,1,0:T(8,128)S(1)}, u32[]{:S(2)}, u32[]{:S(2)}) collective-permute-start(f32[1,128,128]{2,1,0:T(8,128)S(1)} %coarse_change.1), channel_id=1, source_target_pairs={{1,2},{2,3},{5,6},{6,7},{9,10},{10,11},{13,14},{14,15},{17,18},{18... | collective-permute-start | bytes 196616 | tf_op jit(solution)/shard_map/ppermute | solution.py:599
  28.6 1.3 %collective-permute-start.11 = (f32[1,128,128]{2,1,0:T(8,128)S(1)}, f32[1,128,128]{2,1,0:T(8,128)S(1)}, u32[]{:S(2)}, u32[]{:S(2)}) collective-permute-start(f32[1,128,128]{2,1,0:T(8,128)S(1)} %coarse_change.1), channel_id=1, source_target_pairs={{1,3},{5,7},{9,11},{13,15},{17,19},{21,23},{25,27},{29,31}} | collective-permute-start | bytes 196616 | tf_op jit(solution)/shard_map/ppermute | solution.py:599
  29.9 10.3 %collective-permute-done.10.refs_5_ = f32[1,128,128]{2,1,0:T(8,128)S(1)} collective-permute-done((f32[1,128,128]{2,1,0:T(8,128)S(1)}, f32[1,128,128]{2,1,0:T(8,128)S(1)}, u32[]{:S(2)}, u32[]{:S(2)}) %collective-permute-start.10) | collective-permute-done | bytes 65568 | tf_op jit(solution)/shard_map/ppermute | solution.py:599
  40.1 3.5 %collective-permute-done.11.refs_6_ = f32[1,128,128]{2,1,0:T(8,128)S(1)} collective-permute-done((f32[1,128,128]{2,1,0:T(8,128)S(1)}, f32[1,128,128]{2,1,0:T(8,128)S(1)}, u32[]{:S(2)}, u32[]{:S(2)}) %collective-permute-start.11) | collective-permute-done | bytes 65568 | tf_op jit(solution)/shard_map/ppermute | solution.py:599
  43.7 1.6 %corrected.1 = f32[256,256]{1,0:T(8,128)} custom-call(s32[2]{0:T(128)S(1)} %pad_add_fusion.choice.which, f32[2,32,8,128]{3,2,1,0:T(8,128)S(1)} %collective-permute-done.6.refs_0_, f32[2,32,8,128]{3,2,1,0:T(8,128)S(1)} %collective-permute-done.7.refs_1_, f32[2,32,8,128]{3,2,1,0:T(8,128)S(1)} %collective-permute-done.8.refs_2_, ...), custom_call_target="tpu_custom_call" | custom-call | tf_op jit(solution)/shard_map/corrected/pallas_call | solution.py:554
  (1 shorter events, 0.0 us)
Async XLA Ops:
  0.0 2.2 %copy-start.2 = (f32[4]{0:T(128)S(1)}, f32[4]{0:T(128)}, u32[]{:S(2)}) copy-start(f32[4]{0:T(128)} %values.1) | copy-start | bytes 52
  0.0 5.3 %collective-permute-start = (f32[256,256]{1,0:T(8,128)}, f32[256,256]{1,0:T(8,128)S(1)}, u32[]{:S(2)}, u32[]{:S(2)}) collective-permute-start(f32[256,256]{1,0:T(8,128)} %bitcast.6), channel_id=1, source_target_pairs={{0,4},{5,9},{2,6},{16,20},{21,25},{18,22}} | collective-permute-start | bytes 786440 | tf_op jit(solution)/shard_map/ppermute | solution.py:576
  0.8 5.2 %collective-permute-start.1 = (f32[256,256]{1,0:T(8,128)}, f32[256,256]{1,0:T(8,128)S(1)}, u32[]{:S(2)}, u32[]{:S(2)}) collective-permute-start(f32[256,256]{1,0:T(8,128)} %bitcast.7), channel_id=1, source_target_pairs={{8,4},{13,9},{10,6},{24,20},{29,25},{26,22}} | collective-permute-start | bytes 786440 | tf_op jit(solution)/shard_map/ppermute | solution.py:576
  1.5 4.5 %collective-permute-start.2 = (f32[256,256]{1,0:T(8,128)}, f32[256,256]{1,0:T(8,128)S(1)}, u32[]{:S(2)}, u32[]{:S(2)}) collective-permute-start(f32[256,256]{1,0:T(8,128)} %bitcast.8), channel_id=1, source_target_pairs={{12,4},{1,9},{14,6},{28,20},{17,25},{30,22}} | collective-permute-start | bytes 786440 | tf_op jit(solution)/shard_map/ppermute | solution.py:576
  2.2 1.0 %copy-start.1 = (s32[1,256,256]{2,1,0:T(8,128)S(1)}, s32[1,256,256]{2,1,0:T(8,128)}, u32[]{:S(2)}) copy-start(s32[1,256,256]{2,1,0:T(8,128)} %param.5) | copy-start | bytes 786436
  3.1 2.9 %copy-start = (f32[1,1,256,256]{3,2,1,0:T(8,128)S(1)}, f32[1,1,256,256]{3,2,1,0:T(8,128)}, u32[]{:S(2)}) copy-start(f32[1,1,256,256]{3,2,1,0:T(8,128)} %param.4) | copy-start | bytes 786436
  3.9 3.0 %collective-permute-start.3 = (f32[2,32,8,128]{3,2,1,0:T(8,128)S(1)}, f32[2,32,8,128]{3,2,1,0:T(8,128)S(1)}, u32[]{:S(2)}, u32[]{:S(2)}) collective-permute-start(f32[2,32,8,128]{3,2,1,0:T(8,128)S(1)} %strips_of_perm.1.refs_7_), channel_id=1, source_target_pairs={{0,4},{5,9},{2,6},{16,20},{21,25},{18,22}} | collective-permute-start | bytes 786440 | tf_op jit(solution)/shard_map/ppermute | solution.py:576
  4.6 2.3 %collective-permute-start.4 = (f32[2,32,8,128]{3,2,1,0:T(8,128)S(1)}, f32[2,32,8,128]{3,2,1,0:T(8,128)S(1)}, u32[]{:S(2)}, u32[]{:S(2)}) collective-permute-start(f32[2,32,8,128]{3,2,1,0:T(8,128)S(1)} %strips_of_perm.1.refs_7_), channel_id=1, source_target_pairs={{8,4},{13,9},{10,6},{24,20},{29,25},{26,22}} | collective-permute-start | bytes 786440 | tf_op jit(solution)/shard_map/ppermute | solution.py:576
  5.3 1.6 %collective-permute-start.5 = (f32[2,32,8,128]{3,2,1,0:T(8,128)S(1)}, f32[2,32,8,128]{3,2,1,0:T(8,128)S(1)}, u32[]{:S(2)}, u32[]{:S(2)}) collective-permute-start(f32[2,32,8,128]{3,2,1,0:T(8,128)S(1)} %strips_of_perm.1.refs_7_), channel_id=1, source_target_pairs={{12,4},{1,9},{14,6},{28,20},{17,25},{30,22}} | collective-permute-start | bytes 786440 | tf_op jit(solution)/shard_map/ppermute | solution.py:576
  6.9 19.5 %collective-permute-start.6 = (f32[2,32,8,128]{3,2,1,0:T(8,128)S(1)}, f32[2,32,8,128]{3,2,1,0:T(8,128)S(1)}, u32[]{:S(2)}, u32[]{:S(2)}) collective-permute-start(f32[2,32,8,128]{3,2,1,0:T(8,128)S(1)} %get-tuple-element.19), channel_id=1, source_target_pairs={{4,5},{9,10},{6,7},{20,21},{25,26},{22,23}} | collective-permute-start | bytes 786440 | tf_op jit(solution)/shard_map/ppermute | solution.py:580
  8.2 18.2 %collective-permute-start.7 = (f32[2,32,8,128]{3,2,1,0:T(8,128)S(1)}, f32[2,32,8,128]{3,2,1,0:T(8,128)S(1)}, u32[]{:S(2)}, u32[]{:S(2)}) collective-permute-start(f32[2,32,8,128]{3,2,1,0:T(8,128)S(1)} %get-tuple-element.20), channel_id=1, source_target_pairs={{4,9},{9,14},{6,11},{20,25},{25,30},{22,27}} | collective-permute-start | bytes 786440 | tf_op jit(solution)/shard_map/ppermute | solution.py:580
  8.9 17.6 %collective-permute-start.8 = (f32[2,32,8,128]{3,2,1,0:T(8,128)S(1)}, f32[2,32,8,128]{3,2,1,0:T(8,128)S(1)}, u32[]{:S(2)}, u32[]{:S(2)}) collective-permute-start(f32[2,32,8,128]{3,2,1,0:T(8,128)S(1)} %get-tuple-element.21), channel_id=1, source_target_pairs={{4,13},{9,2},{6,15},{20,29},{25,18},{22,31}} | collective-permute-start | bytes 786440 | tf_op jit(solution)/shard_map/ppermute | solution.py:580
  9.6 16.9 %collective-permute-start.9 = (f32[2,32,8,128]{3,2,1,0:T(8,128)S(1)}, f32[2,32,8,128]{3,2,1,0:T(8,128)S(1)}, u32[]{:S(2)}, u32[]{:S(2)}) collective-permute-start(f32[2,32,8,128]{3,2,1,0:T(8,128)S(1)} %get-tuple-element.22), channel_id=1, source_target_pairs={{4,1},{9,6},{6,3},{20,17},{25,22},{22,19}} | collective-permute-start | bytes 786440 | tf_op jit(solution)/shard_map/ppermute | solution.py:580
  10.3 0.7 %copy-start.3 = (f32[4]{0:T(128)S(1)}, f32[4]{0:T(128)}, u32[]{:S(2)}) copy-start(f32[4]{0:T(128)} %rates.1) | copy-start | bytes 52
  27.3 12.9 %collective-permute-start.10 = (f32[1,128,128]{2,1,0:T(8,128)S(1)}, f32[1,128,128]{2,1,0:T(8,128)S(1)}, u32[]{:S(2)}, u32[]{:S(2)}) collective-permute-start(f32[1,128,128]{2,1,0:T(8,128)S(1)} %coarse_change.1), channel_id=1, source_target_pairs={{1,2},{2,3},{5,6},{6,7},{9,10},{10,11},{13,14},{14,15},{17,18},{18... | collective-permute-start | bytes 196616 | tf_op jit(solution)/shard_map/ppermute | solution.py:599
  28.6 15.1 %collective-permute-start.11 = (f32[1,128,128]{2,1,0:T(8,128)S(1)}, f32[1,128,128]{2,1,0:T(8,128)S(1)}, u32[]{:S(2)}, u32[]{:S(2)}) collective-permute-start(f32[1,128,128]{2,1,0:T(8,128)S(1)} %coarse_change.1), channel_id=1, source_target_pairs={{1,3},{5,7},{9,11},{13,15},{17,19},{21,23},{25,27},{29,31}} | collective-permute-start | bytes 196616 | tf_op jit(solution)/shard_map/ppermute | solution.py:599

commit v5 on v4

--- a/solution.py
+++ b/solution.py
@@ -493,9 +493,12 @@
 
     def kernel(choice, *refs):
         ends, own_ref, out = refs[:count], refs[count], refs[count + 1]
-        read = lambda h, o: chosen(choice[0], ends, h, o)
-        for c, tile in enumerate(restrict_strips(read, halves, strips)):
-            out[c] = tile - own_ref[c]
+        for k in range(count):
+            @pl.when(choice[0] == k)
+            def _():
+                read = lambda h, o: ends[k][h, o]
+                for c, tile in enumerate(restrict_strips(read, halves, strips)):
+                    out[c] = tile - own_ref[c]
 
     return pl.pallas_call(
         kernel,

time: 45.6 us -> 45.6 us (level)
  no operation moved by 1% of the time
where the time goes in v5:
time: 45.6 us; the launch traced here: 45.3 us
  waiting for transfers between devices  27 us (59%)
  starting transfers between devices  10.1 us (22%)
  Pallas kernels  6.16 us (14%)
  local copies, waits for them, and re-layouts  1.6 us (4%)
    ppermute x2, waiting for transfers between devices, gathered_body(): lax.ppermute(change, 'tm', [(i, i + k) for i in range(1, slices - k)])  13.8 us
    ppermute x4, waiting for transfers between devices, from_sites(): lax.ppermute(array, axes, [(place(site(j), j), place(site(j) + k, j + 1))...  13.2 us
    ppermute x6, starting transfers between devices, to_sites(): lax.ppermute(array, axes, [(place(site(j) + k, j), place(site(j), j)) for...  4.18 us
    ppermute x4, starting transfers between devices, from_sites(): lax.ppermute(array, axes, [(place(site(j), j), place(site(j) + k, j + 1))...  3.32 us
    ppermute x2, starting transfers between devices, gathered_body(): lax.ppermute(change, 'tm', [(i, i + k) for i in range(1, slices - k)])  2.58 us
    pallas_call x1, Pallas kernels, coarse_parts(): pl.pallas_call(kernel, out_shape=[jax.ShapeDtypeStruct(coarse, jnp.float3...  2.19 us
    unnamed x8, local copies, waits for them, and re-layouts  1.6 us
    pallas_call x1, Pallas kernels, corrected(): pl.pallas_call(kernel, out_shape=jax.ShapeDtypeStruct((ny, nz), jnp.float...  1.58 us
  transfers between devices with their start and end apart: 12, of which 3 were waited for; matrix products, arithmetic and copies ran while one was open for 0% of the time, Pallas kernels for 8%

profile of v5, /device:TPU:11, one launch (start us, length us, event | category | flops | bytes accessed | tf_op | source)
XLA Modules:
  0.0 45.3 jit_solution(2344466916858980686)
XLA Ops:
  0.0 0.0 copy-start.2
  0.0 0.8 %collective-permute-start = (f32[256,256]{1,0:T(8,128)}, f32[256,256]{1,0:T(8,128)S(1)}, u32[]{:S(2)}, u32[]{:S(2)}) collective-permute-start(f32[256,256]{1,0:T(8,128)} %bitcast.6), channel_id=1, source_target_pairs={{0,4},{5,9},{2,6},{16,20},{21,25},{18,22}} | collective-permute-start | bytes 786440 | tf_op jit(solution)/shard_map/ppermute | solution.py:579
  0.8 0.7 %collective-permute-start.1 = (f32[256,256]{1,0:T(8,128)}, f32[256,256]{1,0:T(8,128)S(1)}, u32[]{:S(2)}, u32[]{:S(2)}) collective-permute-start(f32[256,256]{1,0:T(8,128)} %bitcast.7), channel_id=1, source_target_pairs={{8,4},{13,9},{10,6},{24,20},{29,25},{26,22}} | collective-permute-start | bytes 786440 | tf_op jit(solution)/shard_map/ppermute | solution.py:579
  1.5 0.7 %collective-permute-start.2 = (f32[256,256]{1,0:T(8,128)}, f32[256,256]{1,0:T(8,128)S(1)}, u32[]{:S(2)}, u32[]{:S(2)}) collective-permute-start(f32[256,256]{1,0:T(8,128)} %bitcast.8), channel_id=1, source_target_pairs={{12,4},{1,9},{14,6},{28,20},{17,25},{30,22}} | collective-permute-start | bytes 786440 | tf_op jit(solution)/shard_map/ppermute | solution.py:579
  2.2 0.0 copy-done.2
  2.2 0.0 copy-start.1
  2.2 0.9 %copy-done.1 = s32[1,256,256]{2,1,0:T(8,128)S(1)} copy-done((s32[1,256,256]{2,1,0:T(8,128)S(1)}, s32[1,256,256]{2,1,0:T(8,128)}, u32[]{:S(2)}) %copy-start.1) | copy-done | bytes 262168
  3.1 0.0 copy-start
  3.1 0.8 %strips_of_perm.1.refs_7_ = f32[2,32,8,128]{3,2,1,0:T(8,128)S(1)} custom-call(f32[4]{0:T(128)S(1)} %copy-done.2, s32[256,256]{1,0:T(8,128)S(1)} %bitcast.13), custom_call_target="tpu_custom_call" | custom-call | tf_op jit(solution)/shard_map/strips_of_perm/pallas_call | solution.py:207
  3.9 0.7 %collective-permute-start.3 = (f32[2,32,8,128]{3,2,1,0:T(8,128)S(1)}, f32[2,32,8,128]{3,2,1,0:T(8,128)S(1)}, u32[]{:S(2)}, u32[]{:S(2)}) collective-permute-start(f32[2,32,8,128]{3,2,1,0:T(8,128)S(1)} %strips_of_perm.1.refs_7_), channel_id=1, source_target_pairs={{0,4},{5,9},{2,6},{16,20},{21,25},{18,22}} | collective-permute-start | bytes 786440 | tf_op jit(solution)/shard_map/ppermute | solution.py:579
  4.6 0.7 %collective-permute-start.4 = (f32[2,32,8,128]{3,2,1,0:T(8,128)S(1)}, f32[2,32,8,128]{3,2,1,0:T(8,128)S(1)}, u32[]{:S(2)}, u32[]{:S(2)}) collective-permute-start(f32[2,32,8,128]{3,2,1,0:T(8,128)S(1)} %strips_of_perm.1.refs_7_), channel_id=1, source_target_pairs={{8,4},{13,9},{10,6},{24,20},{29,25},{26,22}} | collective-permute-start | bytes 786440 | tf_op jit(solution)/shard_map/ppermute | solution.py:579
  5.3 0.0 collective-permute-done.refs_0_
  5.3 0.7 %collective-permute-start.5 = (f32[2,32,8,128]{3,2,1,0:T(8,128)S(1)}, f32[2,32,8,128]{3,2,1,0:T(8,128)S(1)}, u32[]{:S(2)}, u32[]{:S(2)}) collective-permute-start(f32[2,32,8,128]{3,2,1,0:T(8,128)S(1)} %strips_of_perm.1.refs_7_), channel_id=1, source_target_pairs={{12,4},{1,9},{14,6},{28,20},{17,25},{30,22}} | collective-permute-start | bytes 786440 | tf_op jit(solution)/shard_map/ppermute | solution.py:579
  6.0 0.0 collective-permute-done.1.refs_1_
  6.0 0.0 collective-permute-done.2.refs_2_
  6.0 0.0 copy-done
  6.1 0.8 %strips_of_state.1 = (f32[2,34,8,128]{3,2,1,0:T(8,128)S(1)}, f32[2,34,8,128]{3,2,1,0:T(8,128)S(1)}, f32[2,34,8,128]{3,2,1,0:T(8,128)S(1)}, f32[2,34,8,128]{3,2,1,0:T(8,128)S(1)}) custom-call(f32[256,256]{1,0:T(8,128)S(1)} %collective-permute-done.refs_0_, f32[256,256]{1,0:T(8,128)S(1)} %collective-permute-done.1.refs_1_, ...), custom_call_target="tpu_custom_call" | custom-call | tf_op jit(solution)/shard_map/strips_of_state/pallas_call | solution.py:241
  6.9 0.0 collective-permute-done.3.refs_4_
  6.9 0.0 collective-permute-done.4.refs_5_
  6.9 0.0 collective-permute-done.5.refs_6_
  6.9 1.3 %collective-permute-start.6 = (f32[2,32,8,128]{3,2,1,0:T(8,128)S(1)}, f32[2,32,8,128]{3,2,1,0:T(8,128)S(1)}, u32[]{:S(2)}, u32[]{:S(2)}) collective-permute-start(f32[2,32,8,128]{3,2,1,0:T(8,128)S(1)} %get-tuple-element.19), channel_id=1, source_target_pairs={{4,5},{9,10},{6,7},{20,21},{25,26},{22,23}} | collective-permute-start | bytes 786440 | tf_op jit(solution)/shard_map/ppermute | solution.py:583
  8.2 0.7 %collective-permute-start.7 = (f32[2,32,8,128]{3,2,1,0:T(8,128)S(1)}, f32[2,32,8,128]{3,2,1,0:T(8,128)S(1)}, u32[]{:S(2)}, u32[]{:S(2)}) collective-permute-start(f32[2,32,8,128]{3,2,1,0:T(8,128)S(1)} %get-tuple-element.20), channel_id=1, source_target_pairs={{4,9},{9,14},{6,11},{20,25},{25,30},{22,27}} | collective-permute-start | bytes 786440 | tf_op jit(solution)/shard_map/ppermute | solution.py:583
  8.9 0.7 %collective-permute-start.8 = (f32[2,32,8,128]{3,2,1,0:T(8,128)S(1)}, f32[2,32,8,128]{3,2,1,0:T(8,128)S(1)}, u32[]{:S(2)}, u32[]{:S(2)}) collective-permute-start(f32[2,32,8,128]{3,2,1,0:T(8,128)S(1)} %get-tuple-element.21), channel_id=1, source_target_pairs={{4,13},{9,2},{6,15},{20,29},{25,18},{22,31}} | collective-permute-start | bytes 786440 | tf_op jit(solution)/shard_map/ppermute | solution.py:583
  9.6 0.7 %collective-permute-start.9 = (f32[2,32,8,128]{3,2,1,0:T(8,128)S(1)}, f32[2,32,8,128]{3,2,1,0:T(8,128)S(1)}, u32[]{:S(2)}, u32[]{:S(2)}) collective-permute-start(f32[2,32,8,128]{3,2,1,0:T(8,128)S(1)} %get-tuple-element.22), channel_id=1, source_target_pairs={{4,1},{9,6},{6,3},{20,17},{25,22},{22,19}} | collective-permute-start | bytes 786440 | tf_op jit(solution)/shard_map/ppermute | solution.py:583
  10.3 0.0 copy-start.3
  10.3 0.6 %copy-done.3 = f32[4]{0:T(128)S(1)} copy-done((f32[4]{0:T(128)S(1)}, f32[4]{0:T(128)}, u32[]{:S(2)}) %copy-start.3) | copy-done | bytes 40
  11.0 2.2 %coarse_parts.1 = (f32[1,128,128]{2,1,0:T(8,128)S(1)}, f32[1,128,128]{2,1,0:T(8,128)S(1)}) custom-call(f32[4]{0:T(128)S(1)} %copy-done.3, f32[256,256]{1,0:T(8,128)} %bitcast.9, s32[256,256]{1,0:T(8,128)} %bitcast.12), custom_call_target="tpu_custom_call" | custom-call | tf_op jit(solution)/shard_map/coarse_parts/pallas_call | solution.py:278
  13.2 0.1 pad_add_fusion.choice.which
  13.3 13.2 %collective-permute-done.6.refs_0_ = f32[2,32,8,128]{3,2,1,0:T(8,128)S(1)} collective-permute-done((f32[2,32,8,128]{3,2,1,0:T(8,128)S(1)}, f32[2,32,8,128]{3,2,1,0:T(8,128)S(1)}, u32[]{:S(2)}, u32[]{:S(2)}) %collective-permute-start.6) | collective-permute-done | bytes 262176 | tf_op jit(solution)/shard_map/ppermute | solution.py:583
  26.5 0.0 collective-permute-done.7.refs_1_
  26.5 0.0 collective-permute-done.8.refs_2_
  26.5 0.0 collective-permute-done.9.refs_3_
  26.5 0.8 %coarse_change.1 = f32[1,128,128]{2,1,0:T(8,128)S(1)} custom-call(s32[2]{0:T(128)S(1)} %pad_add_fusion.choice.which, f32[2,32,8,128]{3,2,1,0:T(8,128)S(1)} %collective-permute-done.6.refs_0_, f32[2,32,8,128]{3,2,1,0:T(8,128)S(1)} %collective-permute-done.7.refs_1_, f32[2,32,8,128]{3,2,1,0:T(8,128)S(1)} %collective-permute-done.8.refs_2_, ...), custom_call_target="tpu_custom_call" | custom-call | tf_op jit(solution)/shard_map/coarse_change/pallas_call | solution.py:503
  27.3 1.3 %collective-permute-start.10 = (f32[1,128,128]{2,1,0:T(8,128)S(1)}, f32[1,128,128]{2,1,0:T(8,128)S(1)}, u32[]{:S(2)}, u32[]{:S(2)}) collective-permute-start(f32[1,128,128]{2,1,0:T(8,128)S(1)} %coarse_change.1), channel_id=1, source_target_pairs={{1,2},{2,3},{5,6},{6,7},{9,10},{10,11},{13,14},{14,15},{17,18},{18... | collective-permute-start | bytes 196616 | tf_op jit(solution)/shard_map/ppermute | solution.py:602
  28.6 1.3 %collective-permute-start.11 = (f32[1,128,128]{2,1,0:T(8,128)S(1)}, f32[1,128,128]{2,1,0:T(8,128)S(1)}, u32[]{:S(2)}, u32[]{:S(2)}) collective-permute-start(f32[1,128,128]{2,1,0:T(8,128)S(1)} %coarse_change.1), channel_id=1, source_target_pairs={{1,3},{5,7},{9,11},{13,15},{17,19},{21,23},{25,27},{29,31}} | collective-permute-start | bytes 196616 | tf_op jit(solution)/shard_map/ppermute | solution.py:602
  29.9 10.3 %collective-permute-done.10.refs_5_ = f32[1,128,128]{2,1,0:T(8,128)S(1)} collective-permute-done((f32[1,128,128]{2,1,0:T(8,128)S(1)}, f32[1,128,128]{2,1,0:T(8,128)S(1)}, u32[]{:S(2)}, u32[]{:S(2)}) %collective-permute-start.10) | collective-permute-done | bytes 65568 | tf_op jit(solution)/shard_map/ppermute | solution.py:602
  40.1 3.5 %collective-permute-done.11.refs_6_ = f32[1,128,128]{2,1,0:T(8,128)S(1)} collective-permute-done((f32[1,128,128]{2,1,0:T(8,128)S(1)}, f32[1,128,128]{2,1,0:T(8,128)S(1)}, u32[]{:S(2)}, u32[]{:S(2)}) %collective-permute-start.11) | collective-permute-done | bytes 65568 | tf_op jit(solution)/shard_map/ppermute | solution.py:602
  43.7 1.6 %corrected.1 = f32[256,256]{1,0:T(8,128)} custom-call(s32[2]{0:T(128)S(1)} %pad_add_fusion.choice.which, f32[2,32,8,128]{3,2,1,0:T(8,128)S(1)} %collective-permute-done.6.refs_0_, f32[2,32,8,128]{3,2,1,0:T(8,128)S(1)} %collective-permute-done.7.refs_1_, f32[2,32,8,128]{3,2,1,0:T(8,128)S(1)} %collective-permute-done.8.refs_2_, ...), custom_call_target="tpu_custom_call" | custom-call | tf_op jit(solution)/shard_map/corrected/pallas_call | solution.py:557
  (1 shorter events, 0.0 us)
Async XLA Ops:
  0.0 2.2 %copy-start.2 = (f32[4]{0:T(128)S(1)}, f32[4]{0:T(128)}, u32[]{:S(2)}) copy-start(f32[4]{0:T(128)} %values.1) | copy-start | bytes 52
  0.0 5.3 %collective-permute-start = (f32[256,256]{1,0:T(8,128)}, f32[256,256]{1,0:T(8,128)S(1)}, u32[]{:S(2)}, u32[]{:S(2)}) collective-permute-start(f32[256,256]{1,0:T(8,128)} %bitcast.6), channel_id=1, source_target_pairs={{0,4},{5,9},{2,6},{16,20},{21,25},{18,22}} | collective-permute-start | bytes 786440 | tf_op jit(solution)/shard_map/ppermute | solution.py:579
  0.8 5.2 %collective-permute-start.1 = (f32[256,256]{1,0:T(8,128)}, f32[256,256]{1,0:T(8,128)S(1)}, u32[]{:S(2)}, u32[]{:S(2)}) collective-permute-start(f32[256,256]{1,0:T(8,128)} %bitcast.7), channel_id=1, source_target_pairs={{8,4},{13,9},{10,6},{24,20},{29,25},{26,22}} | collective-permute-start | bytes 786440 | tf_op jit(solution)/shard_map/ppermute | solution.py:579
  1.5 4.5 %collective-permute-start.2 = (f32[256,256]{1,0:T(8,128)}, f32[256,256]{1,0:T(8,128)S(1)}, u32[]{:S(2)}, u32[]{:S(2)}) collective-permute-start(f32[256,256]{1,0:T(8,128)} %bitcast.8), channel_id=1, source_target_pairs={{12,4},{1,9},{14,6},{28,20},{17,25},{30,22}} | collective-permute-start | bytes 786440 | tf_op jit(solution)/shard_map/ppermute | solution.py:579
  2.2 1.0 %copy-start.1 = (s32[1,256,256]{2,1,0:T(8,128)S(1)}, s32[1,256,256]{2,1,0:T(8,128)}, u32[]{:S(2)}) copy-start(s32[1,256,256]{2,1,0:T(8,128)} %param.5) | copy-start | bytes 786436
  3.1 2.9 %copy-start = (f32[1,1,256,256]{3,2,1,0:T(8,128)S(1)}, f32[1,1,256,256]{3,2,1,0:T(8,128)}, u32[]{:S(2)}) copy-start(f32[1,1,256,256]{3,2,1,0:T(8,128)} %param.4) | copy-start | bytes 786436
  3.9 3.0 %collective-permute-start.3 = (f32[2,32,8,128]{3,2,1,0:T(8,128)S(1)}, f32[2,32,8,128]{3,2,1,0:T(8,128)S(1)}, u32[]{:S(2)}, u32[]{:S(2)}) collective-permute-start(f32[2,32,8,128]{3,2,1,0:T(8,128)S(1)} %strips_of_perm.1.refs_7_), channel_id=1, source_target_pairs={{0,4},{5,9},{2,6},{16,20},{21,25},{18,22}} | collective-permute-start | bytes 786440 | tf_op jit(solution)/shard_map/ppermute | solution.py:579
  4.6 2.3 %collective-permute-start.4 = (f32[2,32,8,128]{3,2,1,0:T(8,128)S(1)}, f32[2,32,8,128]{3,2,1,0:T(8,128)S(1)}, u32[]{:S(2)}, u32[]{:S(2)}) collective-permute-start(f32[2,32,8,128]{3,2,1,0:T(8,128)S(1)} %strips_of_perm.1.refs_7_), channel_id=1, source_target_pairs={{8,4},{13,9},{10,6},{24,20},{29,25},{26,22}} | collective-permute-start | bytes 786440 | tf_op jit(solution)/shard_map/ppermute | solution.py:579
  5.3 1.6 %collective-permute-start.5 = (f32[2,32,8,128]{3,2,1,0:T(8,128)S(1)}, f32[2,32,8,128]{3,2,1,0:T(8,128)S(1)}, u32[]{:S(2)}, u32[]{:S(2)}) collective-permute-start(f32[2,32,8,128]{3,2,1,0:T(8,128)S(1)} %strips_of_perm.1.refs_7_), channel_id=1, source_target_pairs={{12,4},{1,9},{14,6},{28,20},{17,25},{30,22}} | collective-permute-start | bytes 786440 | tf_op jit(solution)/shard_map/ppermute | solution.py:579
  6.9 19.5 %collective-permute-start.6 = (f32[2,32,8,128]{3,2,1,0:T(8,128)S(1)}, f32[2,32,8,128]{3,2,1,0:T(8,128)S(1)}, u32[]{:S(2)}, u32[]{:S(2)}) collective-permute-start(f32[2,32,8,128]{3,2,1,0:T(8,128)S(1)} %get-tuple-element.19), channel_id=1, source_target_pairs={{4,5},{9,10},{6,7},{20,21},{25,26},{22,23}} | collective-permute-start | bytes 786440 | tf_op jit(solution)/shard_map/ppermute | solution.py:583
  8.2 18.2 %collective-permute-start.7 = (f32[2,32,8,128]{3,2,1,0:T(8,128)S(1)}, f32[2,32,8,128]{3,2,1,0:T(8,128)S(1)}, u32[]{:S(2)}, u32[]{:S(2)}) collective-permute-start(f32[2,32,8,128]{3,2,1,0:T(8,128)S(1)} %get-tuple-element.20), channel_id=1, source_target_pairs={{4,9},{9,14},{6,11},{20,25},{25,30},{22,27}} | collective-permute-start | bytes 786440 | tf_op jit(solution)/shard_map/ppermute | solution.py:583
  8.9 17.6 %collective-permute-start.8 = (f32[2,32,8,128]{3,2,1,0:T(8,128)S(1)}, f32[2,32,8,128]{3,2,1,0:T(8,128)S(1)}, u32[]{:S(2)}, u32[]{:S(2)}) collective-permute-start(f32[2,32,8,128]{3,2,1,0:T(8,128)S(1)} %get-tuple-element.21), channel_id=1, source_target_pairs={{4,13},{9,2},{6,15},{20,29},{25,18},{22,31}} | collective-permute-start | bytes 786440 | tf_op jit(solution)/shard_map/ppermute | solution.py:583
  9.6 16.9 %collective-permute-start.9 = (f32[2,32,8,128]{3,2,1,0:T(8,128)S(1)}, f32[2,32,8,128]{3,2,1,0:T(8,128)S(1)}, u32[]{:S(2)}, u32[]{:S(2)}) collective-permute-start(f32[2,32,8,128]{3,2,1,0:T(8,128)S(1)} %get-tuple-element.22), channel_id=1, source_target_pairs={{4,1},{9,6},{6,3},{20,17},{25,22},{22,19}} | collective-permute-start | bytes 786440 | tf_op jit(solution)/shard_map/ppermute | solution.py:583
  10.3 0.7 %copy-start.3 = (f32[4]{0:T(128)S(1)}, f32[4]{0:T(128)}, u32[]{:S(2)}) copy-start(f32[4]{0:T(128)} %rates.1) | copy-start | bytes 52
  27.3 12.9 %collective-permute-start.10 = (f32[1,128,128]{2,1,0:T(8,128)S(1)}, f32[1,128,128]{2,1,0:T(8,128)S(1)}, u32[]{:S(2)}, u32[]{:S(2)}) collective-permute-start(f32[1,128,128]{2,1,0:T(8,128)S(1)} %coarse_change.1), channel_id=1, source_target_pairs={{1,2},{2,3},{5,6},{6,7},{9,10},{10,11},{13,14},{14,15},{17,18},{18... | collective-permute-start | bytes 196616 | tf_op jit(solution)/shard_map/ppermute | solution.py:602
  28.6 15.1 %collective-permute-start.11 = (f32[1,128,128]{2,1,0:T(8,128)S(1)}, f32[1,128,128]{2,1,0:T(8,128)S(1)}, u32[]{:S(2)}, u32[]{:S(2)}) collective-permute-start(f32[1,128,128]{2,1,0:T(8,128)S(1)} %coarse_change.1), channel_id=1, source_target_pairs={{1,3},{5,7},{9,11},{13,15},{17,19},{21,23},{25,27},{29,31}} | collective-permute-start | bytes 196616 | tf_op jit(solution)/shard_map/ppermute | solution.py:602
